TPU v7x, 128 devices: a whole 4x4x4 slice. The times are simulated.
128 devices in a mesh: tx: 8 (over x, core), ty: 16 (over z, y).
Axes of the slice: x: 4, y: 4, z: 4, core: 2. Of those that a mesh axis runs over, the one named last changes fastest.
Arguments:
- granule_blocks: bfloat16 [8192, 13, 16, 128], P(('tx', 'ty')), may hold values from -6 to 6
- row_weights: bfloat16 [8192, 8, 16], P(('tx', 'ty')), may hold values from -1.5 to 1.5
- column_bank: bfloat16 [8, 128, 128], replicated, may hold values from -0.5 to 0.5
- destination: int32 [8192], P(('tx', 'ty')), may hold values from 0 to 127, as said below
- window_index: int32 [8192], P(('tx', 'ty')), may hold values from 0 to 31
- bank_index: int32 [8192], P(('tx', 'ty')), may hold values from 0 to 7
- kernel_one: bfloat16 [3, 3, 13, 64], replicated, may hold values from -1 to 1
- reduce_two: bfloat16 [2, 2, 64, 128], replicated, may hold values from -0.5 to 0.5
- kernel_two: bfloat16 [3, 3, 128, 128], replicated, may hold values from -0.25 to 0.25
- reduce_three: bfloat16 [2, 2, 128, 256], replicated, may hold values from -0.375 to 0.375
- kernel_three: bfloat16 [3, 3, 256, 256], replicated, may hold values from -0.1875 to 0.1875
- reduce_four: bfloat16 [2, 2, 256, 512], replicated, may hold values from -0.25 to 0.25
- kernel_four: bfloat16 [3, 3, 512, 512], replicated, may hold values from -0.125 to 0.125
Outputs:
- gridded: bfloat16 [13, 4096, 1024], P(None, 'ty', 'tx')
- bottleneck: bfloat16 [512, 512, 128], P(None, 'ty', 'tx')
Inputs may be any that keep to these rules, and one draw needn't show every extreme that they name: At most 2 of the blocks that one device holds name the same destination; in every draw one destination is named by 2 blocks of every device.
All inputs are finite; a program needn't handle non-finite values.
Results may differ from a plain program's by a relative error of at most 0.015.
Values may be sent and summed in bfloat16 or wider, within the bound.
A program may use at most 128 MiB of HBM per device.

v0:
```python
import jax
import jax.numpy as jnp
from jax import lax
from jax.sharding import PartitionSpec as P

WIN_ROWS = 8
CAP = 2
TILE_ROWS = 256


def padded_2(block, sides, width):
    for axis, dim in sides:
        count = lax.axis_size(axis)
        forward = [(i, i + 1) for i in range(count - 1)]
        backward = [(target, source) for source, target in forward]
        low = lax.ppermute(
            lax.slice_in_dim(block, block.shape[dim] - width, None, axis=dim), axis, forward
        )
        high = lax.ppermute(lax.slice_in_dim(block, 0, width, axis=dim), axis, backward)
        block = jnp.concatenate([low, block, high], axis=dim)
    return block


def resample(raw_data, row_weight, bank_choice, column_bank):
    rowed = jnp.einsum(
        "nrk,nbkc->nbrc", row_weight, raw_data, preferred_element_type=jnp.float32
    ).astype(jnp.bfloat16)
    select = (
        bank_choice[:, None] == jnp.arange(column_bank.shape[0], dtype=jnp.int32)[None, :]
    ).astype(jnp.bfloat16)
    matrices = jnp.einsum(
        "nk,kct->nct", select, column_bank, preferred_element_type=jnp.float32
    ).astype(jnp.bfloat16)
    return jnp.einsum("nbrc,nct->nbrt", rowed, matrices, preferred_element_type=jnp.float32).astype(
        jnp.bfloat16
    )


def place(tensor, slot_index, slot_total, fill_value):
    buffer = jnp.full((slot_total,) + tensor.shape[1:], fill_value, tensor.dtype)
    return buffer.at[slot_index].set(tensor)


def leading(tensor, leading_dims):
    return tensor.reshape(leading_dims + tensor.shape[1:])


def flatten(tensor, skip_count):
    return tensor.reshape((-1,) + tensor.shape[skip_count:])


def conv_same(field, kernel):
    padded = padded_2(field, (("tx", 2), ("ty", 1)), 1)
    output = lax.conv_general_dilated(
        padded[None],
        kernel,
        (1, 1),
        "VALID",
        dimension_numbers=("NCHW", "HWIO", "NCHW"),
        preferred_element_type=jnp.float32,
    )[0]
    return jnp.maximum(output, 0.0).astype(jnp.bfloat16)


def reduce_half(field, kernel):
    output = lax.conv_general_dilated(
        field[None],
        kernel,
        (2, 2),
        "VALID",
        dimension_numbers=("NCHW", "HWIO", "NCHW"),
        preferred_element_type=jnp.float32,
    )[0]
    return jnp.maximum(output, 0.0).astype(jnp.bfloat16)


def body(
    granule_blocks,
    row_weights,
    column_bank,
    destination,
    window_index,
    bank_index,
    kernel_one,
    reduce_two,
    kernel_two,
    reduce_three,
    kernel_three,
    reduce_four,
    kernel_four,
):
    across = lax.axis_size("tx")
    down_count = lax.axis_size("ty")
    tile_count = across * down_count
    slot_total = tile_count * CAP
    held_blocks = destination.shape[0]
    windows = TILE_ROWS // WIN_ROWS
    matches = destination[:, None] == destination[None, :]
    before = jnp.arange(held_blocks)[None, :] < jnp.arange(held_blocks)[:, None]
    rank_within = jnp.sum((matches & before).astype(jnp.int32), axis=1)
    slot_index = destination * CAP + rank_within
    window_slots = place(window_index, slot_index, slot_total, -1)
    tile_dims = (tile_count, CAP)
    raw_slots = place(granule_blocks, slot_index, slot_total, 0)
    weight_slots = place(row_weights, slot_index, slot_total, 0)
    bank_slots = place(bank_index, slot_index, slot_total, 0)
    got_raw, got_weight, got_bank, got_window = (
        lax.all_to_all(
            leading(raw_slots, tile_dims), ("tx", "ty"), split_axis=0, concat_axis=0, tiled=True
        ),
        lax.all_to_all(
            leading(weight_slots, tile_dims), ("tx", "ty"), split_axis=0, concat_axis=0, tiled=True
        ),
        lax.all_to_all(
            leading(bank_slots, tile_dims), ("tx", "ty"), split_axis=0, concat_axis=0, tiled=True
        ),
        lax.all_to_all(
            leading(window_slots, tile_dims), ("tx", "ty"), split_axis=0, concat_axis=0, tiled=True
        ),
    )
    skip_count = 2
    received = resample(
        flatten(got_raw, skip_count),
        flatten(got_weight, skip_count),
        flatten(got_bank, skip_count),
        column_bank,
    )
    arrived = flatten(got_window, skip_count)
    onehot = arrived[None, :] == jnp.arange(windows, dtype=jnp.int32)[:, None]
    counts = jnp.sum(onehot.astype(jnp.int32), axis=1)
    sums = jnp.einsum(
        "ws,sbrt->bwrt", onehot.astype(jnp.bfloat16), received, preferred_element_type=jnp.float32
    )
    divisor = jnp.maximum(counts, 1).astype(jnp.float32)
    averaged = sums / divisor[None, :, None, None]
    gridded = averaged.reshape(averaged.shape[0], windows * WIN_ROWS, averaged.shape[3]).astype(
        jnp.bfloat16
    )
    level_one = conv_same(gridded, kernel_one)
    level_two = conv_same(reduce_half(level_one, reduce_two), kernel_two)
    level_three = conv_same(reduce_half(level_two, reduce_three), kernel_three)
    bottleneck = conv_same(reduce_half(level_three, reduce_four), kernel_four)
    return (gridded, bottleneck)


def solution(mesh):
    in_specs = (
        P(("tx", "ty"), None, None, None),
        P(("tx", "ty"), None, None),
        P(),
        P(("tx", "ty")),
        P(("tx", "ty")),
        P(("tx", "ty")),
        P(),
        P(),
        P(),
        P(),
        P(),
        P(),
        P(),
    )
    out_specs = (P(None, "ty", "tx"), P(None, "ty", "tx"))
    return jax.shard_map(body, mesh=mesh, in_specs=in_specs, out_specs=out_specs, check_vma=False)
```

profile of v0, /device:TPU:29, one launch (start us, length us, event | category | flops | bytes accessed | tf_op | source)
XLA Modules:
  0.0 444.4 jit_solution(13095702540672242100)
XLA Ops:
  3.9 10.6 %all-to-all-start.2 = ((s32[128,1,2]{2,1,0:T(1,128)}), s32[128,1,2]{2,1,0:T(1,128)S(1)}, u32[]{:S(2)}, u32[]{:S(2)}) async-start(s32[128,1,2]{2,1,0:T(1,128)} %bitcast.7), calls=%async_computation.2 | async-start | bytes 131072 | tf_op jit(solution)/shard_map/all_to_all | solution.py:114
  16.2 4.2 all-to-all-done.2
  20.4 8.1 %all-to-all-start.3 = ((s32[128,1,2]{2,1,0:T(1,128)}), s32[128,1,2]{2,1,0:T(1,128)S(1)}, u32[]{:S(2)}, u32[]{:S(2)}) async-start(s32[128,1,2]{2,1,0:T(1,128)} %bitcast.10), calls=%async_computation.3 | async-start | bytes 131072 | tf_op jit(solution)/shard_map/all_to_all | solution.py:117
  34.4 8.2 %all-to-all-start.1 = ((bf16[128,2,128]{2,1,0:T(2,128)(2,1)}), bf16[128,2,128]{2,1,0:T(2,128)(2,1)S(1)}, u32[]{:S(2)}, u32[]{:S(2)}) async-start(bf16[128,2,128]{2,1,0:T(2,128)(2,1)} %reshape.190), calls=%async_computation.1 | async-start | bytes 131072 | tf_op jit(solution)/shard_map/all_to_all | solution.py:111
  42.7 6.7 %broadcast_in_dim.18 = bf16[256,13,16,128]{3,2,1,0:T(8,128)(2,1)} broadcast(bf16[]{:T(256)} %constant.7.clone.1), dimensions={} | broadcast | bytes 13631490 | tf_op jit(solution)/shard_map/broadcast_in_dim | solution.py:40
  49.4 11.4 %scatter_fusion = bf16[256,13,16,128]{3,2,1,0:T(8,128)(2,1)} fusion(bf16[256,13,16,128]{3,2,1,0:T(8,128)(2,1)} %broadcast_in_dim.18, s32[64]{0:T(128)S(1)} %compare_select_fusion, bf16[64,13,16,128]{3,2,1,0:T(8,128)(2,1)} %param.13), kind=kCustom, calls=%fused_computation | custom fusion | bytes 10223872 | tf_op jit(solution)/shard_map/scatter | solution.py:41
  60.8 10.4 %all-to-all-start = ((bf16[128,2,13,16,128]{4,3,2,1,0:T(8,128)(2,1)}), bf16[128,2,13,16,128]{4,3,2,1,0:T(8,128)(2,1)}, u32[]{:S(2)}, u32[]{:S(2)}) async-start(bf16[128,2,13,16,128]{4,3,2,1,0:T(8,128)(2,1)} %bitcast.114), calls=%async_computation | async-start | bytes 27262976 | tf_op jit(solution)/shard_map/all_to_all | solution.py:108
  73.8 5.6 %convert_bitcast_fusion = bf16[256,128,128,1]{2,0,1,3:T(8,128)(2,1)} fusion(bf16[8,128,128]{2,1,0:T(8,128)(2,1)S(1)} %copy-done.3, s32[256]{0:T(256)S(1)} %eq.46), kind=kOutput, calls=%fused_computation.24 | convolution fusion | flops 71305216 | bytes 8651776 | tf_op jit(solution)/shard_map/nk,kct->nct/dot_general | solution.py:31
  79.8 162.0 %all-to-all-done = bf16[128,2,13,16,128]{4,3,2,1,0:T(8,128)(2,1)} async-done(((bf16[128,2,13,16,128]{4,3,2,1,0:T(8,128)(2,1)}), bf16[128,2,13,16,128]{4,3,2,1,0:T(8,128)(2,1)}, u32[]{:S(2)}, u32[]{:S(2)}) %all-to-all-start) | async-done | bytes 13631520 | tf_op jit(solution)/shard_map/all_to_all | solution.py:108
  241.8 18.3 %fusion.19 = bf16[256,13,8,128]{3,2,1,0:T(8,128)(2,1)} fusion(bf16[256,128,128,1]{2,0,1,3:T(8,128)(2,1)} %convert_bitcast_fusion, bf16[256,13,16,128]{3,2,1,0:T(8,128)(2,1)} %bitcast.1, bf16[256,8,16,1]{2,1,3,0:T(8,128)(2,1)S(1)} %bitcast.140), kind=kOutput, calls=%fused_computation.25 | convolution fusion | flops 988282880 | bytes 28901376 | tf_op jit(solution)/shard_map/nbrc,nct->nbrt/dot_general | solution.py:34
  260.2 4.2 fusion.85
  277.9 6.4 %collective-permute-start.2 = (bf16[13,1,130]{2,1,0:T(2,128)(2,1)S(1)}, bf16[13,1,130]{2,1,0:T(2,128)(2,1)S(1)}, u32[]{:S(2)}, u32[]{:S(2)}) collective-permute-start(bf16[13,1,130]{2,1,0:T(2,128)(2,1)S(1)} %get-tuple-element.8), channel_id=1, source_target_pairs={{0,1},{1,2},{2,3},{3,4},{4,5},{5,6},{6,7},{7,8},{8,9},{9,10},{10,1... | collective-permute-start | bytes 10148 | tf_op jit(solution)/shard_map/ppermute | solution.py:16
  286.2 4.6 %collective-permute-done.3 = bf16[13,1,130]{2,1,0:T(2,128)(2,1)S(1)} collective-permute-done((bf16[13,1,130]{2,1,0:T(2,128)(2,1)S(1)}, bf16[13,1,130]{2,1,0:T(2,128)(2,1)S(1)}, u32[]{:S(2)}, u32[]{:S(2)}) %collective-permute-start.3) | collective-permute-done | bytes 3412 | tf_op jit(solution)/shard_map/ppermute | solution.py:19
  293.5 4.0 copy.120
  299.3 11.4 %copy.92 = bf16[13,258,1,8,17]{0,3,4,1,2:T(8,128)(2,1)} copy(bf16[13,258,1,8,17]{1,0,4,3,2:T(8,128)(2,1)S(1)} %bitcast.130) | data formatting | bytes 1824576 | tf_op jit(solution)/shard_map/conv_general_dilated | solution.py:54
  312.2 16.3 %fusion.13 = bf16[256,8,17,64]{3,1,2,0:T(8,128)(2,1)} fusion(pred[8,17]{0,1:T(8,128)(4,1)S(1)} %copy-done.9, bf16[3,3,13,64]{3,2,1,0:T(8,128)(2,1)S(1)} %copy-done.8, bf16[13,258,1,7,2]{0,3,4,1,2:T(8,128)(2,1)S(1)} %slice.80, bf16[13,258,1,8,17]{0,3,4,1,2:T(8,128)(2,1)} %copy.92), kind=kOutput, calls=%fused_computation.18 | convolution fusion | flops 533376160 | bytes 5477760 | tf_op jit(solution)/shard_map/conv_general_dilated | solution.py:54
  328.5 11.6 %copy.93 = bf16[256,8,17,64]{0,3,2,1:T(8,128)(2,1)} copy(bf16[256,8,17,64]{3,1,2,0:T(8,128)(2,1)} %fusion.13) | data formatting | bytes 8912896 | tf_op jit(solution)/shard_map/convert_element_type | solution.py:62
  340.1 4.8 %slice.81 = bf16[256,1,128,64]{0,3,2,1:T(8,128)(2,1)} slice(bf16[256,1,136,64]{0,3,2,1:T(8,128)(2,1)} %bitcast.122), slice={[0:256], [0:1], [0:128], [0:64]} | slice | bytes 8388608 | tf_op jit(solution)/shard_map/convert_element_type | solution.py:62
  344.9 13.0 %copy.95 = bf16[256,1,8,16,64]{4,2,3,0,1:T(8,128)(2,1)} copy(bf16[256,1,8,16,64]{0,4,3,2,1:T(8,128)(2,1)} %bitcast.123) | data formatting | bytes 8388608 | tf_op jit(solution)/shard_map/convert_element_type | solution.py:62
  359.1 5.4 %maximum_convert_fusion.2 = bf16[128,8,8,128]{3,1,2,0:T(8,128)(2,1)S(1)} fusion(bf16[2,2,64,128]{3,2,1,0:T(8,128)(2,1)S(1)} %copy-done.7, bf16[256,1,7,1,64]{4,2,3,0,1:T(8,128)(2,1)S(1)} %slice.82, bf16[256,1,8,16,64]{4,2,3,0,1:T(8,128)(2,1)} %copy.95), kind=kOutput, calls=%fused_computation.37 | convolution fusion | flops 552337408 | bytes 6586368 | tf_op jit(solution)/shard_map/conv_general_dilated | solution.py:66
  365.2 3.4 collective-permute-start.4
  370.5 3.6 collective-permute-done.5
  376.1 3.4 collective-permute-start.7
  386.3 5.9 %fusion.45 = bf16[128,8,9,128]{3,1,2,0:T(8,128)(2,1)S(1)} fusion(pred[8,9]{0,1:T(8,128)(4,1)S(1)} %copy-done.10, bf16[3,3,128,128]{3,2,1,0:T(8,128)(2,1)S(1)} %copy-done.5, bf16[128,130,1,7,2]{0,3,4,1,2:T(8,128)(2,1)S(1)} %slice.85, bf16[128,130,1,8,9]{0,3,4,1,2:T(8,128)(2,1)S(1)} %copy.99), kind=kOutput, calls=%fused_computation.55 | convolution fusion | flops 2731413504 | bytes 5516360 | tf_op jit(solution)/shard_map/conv_general_dilated | solution.py:54
  401.7 3.3 collective-permute-done.9
  407.0 3.5 collective-permute-start.11
  410.5 3.2 collective-permute-done.11
  415.2 3.2 fusion.63
  426.0 3.3 collective-permute-done.13
  431.3 3.4 collective-permute-start.15
  434.7 3.4 collective-permute-done.15
  439.1 3.8 maximum_convert_fusion.5
  (119 shorter events, 72.1 us)
Async XLA Ops:
  0.6 414.4 %copy-start = (bf16[3,3,256,256]{3,2,1,0:T(8,128)(2,1)S(1)}, bf16[3,3,256,256]{3,2,1,0:T(8,128)(2,1)}, u32[]{:S(2)}) copy-start(bf16[3,3,256,256]{3,2,1,0:T(8,128)(2,1)} %param.23) | copy-start | bytes 3538948
  3.9 16.5 %all-to-all-start.2 = ((s32[128,1,2]{2,1,0:T(1,128)}), s32[128,1,2]{2,1,0:T(1,128)S(1)}, u32[]{:S(2)}, u32[]{:S(2)}) async-start(s32[128,1,2]{2,1,0:T(1,128)} %bitcast.7), calls=%async_computation.2 | async-start | bytes 131072 | tf_op jit(solution)/shard_map/all_to_all | solution.py:114
  20.4 14.0 %all-to-all-start.3 = ((s32[128,1,2]{2,1,0:T(1,128)}), s32[128,1,2]{2,1,0:T(1,128)S(1)}, u32[]{:S(2)}, u32[]{:S(2)}) async-start(s32[128,1,2]{2,1,0:T(1,128)} %bitcast.10), calls=%async_computation.3 | async-start | bytes 131072 | tf_op jit(solution)/shard_map/all_to_all | solution.py:117
  34.4 26.4 %all-to-all-start.1 = ((bf16[128,2,128]{2,1,0:T(2,128)(2,1)}), bf16[128,2,128]{2,1,0:T(2,128)(2,1)S(1)}, u32[]{:S(2)}, u32[]{:S(2)}) async-start(bf16[128,2,128]{2,1,0:T(2,128)(2,1)} %reshape.190), calls=%async_computation.1 | async-start | bytes 131072 | tf_op jit(solution)/shard_map/all_to_all | solution.py:111
  60.8 13.0 %copy-start.3 = (bf16[8,128,128]{2,1,0:T(8,128)(2,1)S(1)}, bf16[8,128,128]{2,1,0:T(8,128)(2,1)}, u32[]{:S(2)}) copy-start(bf16[8,128,128]{2,1,0:T(8,128)(2,1)} %param.15) | copy-start | bytes 786436
  60.8 181.0 %all-to-all-start = ((bf16[128,2,13,16,128]{4,3,2,1,0:T(8,128)(2,1)}), bf16[128,2,13,16,128]{4,3,2,1,0:T(8,128)(2,1)}, u32[]{:S(2)}, u32[]{:S(2)}) async-start(bf16[128,2,13,16,128]{4,3,2,1,0:T(8,128)(2,1)} %bitcast.114), calls=%async_computation | async-start | bytes 27262976 | tf_op jit(solution)/shard_map/all_to_all | solution.py:108
  264.7 26.2 %copy-start.1 = (bf16[13,32,8,128]{3,2,1,0:T(8,128)(2,1)}, bf16[13,32,8,128]{3,2,1,0:T(8,128)(2,1)S(1)}, u32[]{:S(2)}) copy-start(bf16[13,32,8,128]{3,2,1,0:T(8,128)(2,1)S(1)} %copy.137) | copy-start | bytes 2555908
  267.5 5.1 %collective-permute-start = (bf16[13,256,1]{1,0,2:T(8,128)(2,1)S(1)}, bf16[13,256,1]{1,0,2:T(8,128)(2,1)S(1)}, u32[]{:S(2)}, u32[]{:S(2)}) collective-permute-start(bf16[13,256,1]{1,0,2:T(8,128)(2,1)S(1)} %copy.86), channel_id=1, source_target_pairs={{0,16},{16,32},{32,48},{48,64},{64,80},{80,96},{96,112},{1,17},{17... | collective-permute-start | bytes 19976 | tf_op jit(solution)/shard_map/ppermute | solution.py:16
  270.7 5.0 %collective-permute-start.1 = (bf16[13,256,1]{1,0,2:T(8,128)(2,1)S(1)}, bf16[13,256,1]{1,0,2:T(8,128)(2,1)S(1)}, u32[]{:S(2)}, u32[]{:S(2)}) collective-permute-start(bf16[13,256,1]{1,0,2:T(8,128)(2,1)S(1)} %copy.87), channel_id=1, source_target_pairs={{16,0},{32,16},{48,32},{64,48},{80,64},{96,80},{112,96},{17,1},{33... | collective-permute-start | bytes 19976 | tf_op jit(solution)/shard_map/ppermute | solution.py:19
  276.9 13.9 %copy-start.2 = (bf16[13,256,1]{2,1,0:T(8,128)(2,1)S(1)}, bf16[13,256,1]{2,1,0:T(8,128)(2,1)}, u32[]{:S(2)}) copy-start(bf16[13,256,1]{2,1,0:T(8,128)(2,1)} %copy.89) | copy-start | bytes 19972
  277.9 8.3 %collective-permute-start.2 = (bf16[13,1,130]{2,1,0:T(2,128)(2,1)S(1)}, bf16[13,1,130]{2,1,0:T(2,128)(2,1)S(1)}, u32[]{:S(2)}, u32[]{:S(2)}) collective-permute-start(bf16[13,1,130]{2,1,0:T(2,128)(2,1)S(1)} %get-tuple-element.8), channel_id=1, source_target_pairs={{0,1},{1,2},{2,3},{3,4},{4,5},{5,6},{6,7},{7,8},{8,9},{9,10},{10,1... | collective-permute-start | bytes 10148 | tf_op jit(solution)/shard_map/ppermute | solution.py:16
  284.3 6.6 %collective-permute-start.3 = (bf16[13,1,130]{2,1,0:T(2,128)(2,1)S(1)}, bf16[13,1,130]{2,1,0:T(2,128)(2,1)S(1)}, u32[]{:S(2)}, u32[]{:S(2)}) collective-permute-start(bf16[13,1,130]{2,1,0:T(2,128)(2,1)S(1)} %get-tuple-element.9), channel_id=1, source_target_pairs={{1,0},{2,1},{3,2},{4,3},{5,4},{6,5},{7,6},{8,7},{9,8},{10,9},{11,1... | collective-permute-start | bytes 10148 | tf_op jit(solution)/shard_map/ppermute | solution.py:19
  299.2 12.9 %copy-start.8 = (bf16[3,3,13,64]{3,2,1,0:T(8,128)(2,1)S(1)}, bf16[3,3,13,64]{3,2,1,0:T(8,128)(2,1)}, u32[]{:S(2)}) copy-start(bf16[3,3,13,64]{3,2,1,0:T(8,128)(2,1)} %param.19) | copy-start | bytes 44932
  299.2 12.9 %copy-start.9 = (pred[8,17]{0,1:T(8,128)(4,1)S(1)}, pred[8,17]{0,1:T(8,128)(4,1)}, u32[]{:S(2)}) copy-start(pred[8,17]{0,1:T(8,128)(4,1)} %constant.55) | copy-start | bytes 412
  344.9 14.2 %copy-start.7 = (bf16[2,2,64,128]{3,2,1,0:T(8,128)(2,1)S(1)}, bf16[2,2,64,128]{3,2,1,0:T(8,128)(2,1)}, u32[]{:S(2)}) copy-start(bf16[2,2,64,128]{3,2,1,0:T(8,128)(2,1)} %param.20) | copy-start | bytes 196612
  365.2 5.3 %collective-permute-start.4 = (bf16[128,128,1]{0,2,1:T(2,128)(2,1)S(1)}, bf16[128,128,1]{0,2,1:T(2,128)(2,1)S(1)}, u32[]{:S(2)}, u32[]{:S(2)}) collective-permute-start(bf16[128,128,1]{0,2,1:T(2,128)(2,1)S(1)} %get-tuple-element.12), channel_id=1, source_target_pairs={{0,16},{16,32},{32,48},{48,64},{64,80},{80,96},{96,112},{1,17},{17... | collective-permute-start | bytes 98312 | tf_op jit(solution)/shard_map/ppermute | solution.py:16
  368.6 5.6 %collective-permute-start.5 = (bf16[128,128,1]{0,2,1:T(2,128)(2,1)S(1)}, bf16[128,128,1]{0,2,1:T(2,128)(2,1)S(1)}, u32[]{:S(2)}, u32[]{:S(2)}) collective-permute-start(bf16[128,128,1]{0,2,1:T(2,128)(2,1)S(1)} %get-tuple-element.13), channel_id=1, source_target_pairs={{16,0},{32,16},{48,32},{64,48},{80,64},{96,80},{112,96},{17,1},{33... | collective-permute-start | bytes 98312 | tf_op jit(solution)/shard_map/ppermute | solution.py:19
  374.2 5.3 %collective-permute-start.6 = (bf16[128,1,66]{0,2,1:T(8,128)(2,1)S(1)}, bf16[128,1,66]{0,2,1:T(8,128)(2,1)S(1)}, u32[]{:S(2)}, u32[]{:S(2)}) collective-permute-start(bf16[128,1,66]{0,2,1:T(8,128)(2,1)S(1)} %get-tuple-element.10), channel_id=1, source_target_pairs={{0,1},{1,2},{2,3},{3,4},{4,5},{5,6},{6,7},{7,8},{8,9},{9,10},{10,1... | collective-permute-start | bytes 50696 | tf_op jit(solution)/shard_map/ppermute | solution.py:16
  376.1 6.6 %collective-permute-start.7 = (bf16[128,1,66]{0,2,1:T(8,128)(2,1)S(1)}, bf16[128,1,66]{0,2,1:T(8,128)(2,1)S(1)}, u32[]{:S(2)}, u32[]{:S(2)}) collective-permute-start(bf16[128,1,66]{0,2,1:T(8,128)(2,1)S(1)} %get-tuple-element.11), channel_id=1, source_target_pairs={{1,0},{2,1},{3,2},{4,3},{5,4},{6,5},{7,6},{8,7},{9,8},{10,9},{11,1... | collective-permute-start | bytes 50696 | tf_op jit(solution)/shard_map/ppermute | solution.py:19
  385.4 1.0 copy-start.5
  396.7 5.0 %collective-permute-start.8 = (bf16[256,64,1]{0,1,2:T(8,128)(2,1)S(1)}, bf16[256,64,1]{0,1,2:T(8,128)(2,1)S(1)}, u32[]{:S(2)}, u32[]{:S(2)}) collective-permute-start(bf16[256,64,1]{0,1,2:T(8,128)(2,1)S(1)} %get-tuple-element.16), channel_id=1, source_target_pairs={{0,16},{16,32},{32,48},{48,64},{64,80},{80,96},{96,112},{1,17},{17... | collective-permute-start | bytes 98312 | tf_op jit(solution)/shard_map/ppermute | solution.py:16
  399.7 5.2 %collective-permute-start.9 = (bf16[256,64,1]{0,1,2:T(8,128)(2,1)S(1)}, bf16[256,64,1]{0,1,2:T(8,128)(2,1)S(1)}, u32[]{:S(2)}, u32[]{:S(2)}) collective-permute-start(bf16[256,64,1]{0,1,2:T(8,128)(2,1)S(1)} %get-tuple-element.17), channel_id=1, source_target_pairs={{16,0},{32,16},{48,32},{64,48},{80,64},{96,80},{112,96},{17,1},{33... | collective-permute-start | bytes 98312 | tf_op jit(solution)/shard_map/ppermute | solution.py:19
  405.0 5.5 %collective-permute-start.10 = (bf16[256,1,34]{0,1,2:T(2,128)(2,1)S(1)}, bf16[256,1,34]{0,1,2:T(2,128)(2,1)S(1)}, u32[]{:S(2)}, u32[]{:S(2)}) collective-permute-start(bf16[256,1,34]{0,1,2:T(2,128)(2,1)S(1)} %get-tuple-element.14), channel_id=1, source_target_pairs={{0,1},{1,2},{2,3},{3,4},{4,5},{5,6},{6,7},{7,8},{8,9},{9,10},{10,1... | collective-permute-start | bytes 52232 | tf_op jit(solution)/shard_map/ppermute | solution.py:16
  407.0 6.8 %collective-permute-start.11 = (bf16[256,1,34]{0,1,2:T(2,128)(2,1)S(1)}, bf16[256,1,34]{0,1,2:T(2,128)(2,1)S(1)}, u32[]{:S(2)}, u32[]{:S(2)}) collective-permute-start(bf16[256,1,34]{0,1,2:T(2,128)(2,1)S(1)} %get-tuple-element.15), channel_id=1, source_target_pairs={{1,0},{2,1},{3,2},{4,3},{5,4},{6,5},{7,6},{8,7},{9,8},{10,9},{11,1... | collective-permute-start | bytes 52232 | tf_op jit(solution)/shard_map/ppermute | solution.py:19
  418.8 1.2 copy-start.4
  418.8 20.2 %slice-start = ((s8[4718592]{0:T(1024)(128)(4,1)}), s8[4194304]{0:T(1024)(128)(4,1)S(1)}, s32[]{:S(2)}) async-start(s8[4718592]{0:T(1024)(128)(4,1)} %bitcast.141), calls=%async_computation.4 | async-start | bytes 8388608
  420.0 19.0 %slice-start.1 = ((s8[4718592]{0:T(1024)(128)(4,1)}), s8[524288]{0:T(1024)(128)(4,1)S(1)}, s32[]{:S(2)}) async-start(s8[4718592]{0:T(1024)(128)(4,1)} %bitcast.141), calls=%async_computation.5 | async-start | bytes 1048576
  421.0 5.0 %collective-permute-start.12 = (bf16[512,32,1]{0,1,2:T(8,128)(2,1)S(1)}, bf16[512,32,1]{0,1,2:T(8,128)(2,1)S(1)}, u32[]{:S(2)}, u32[]{:S(2)}) collective-permute-start(bf16[512,32,1]{0,1,2:T(8,128)(2,1)S(1)} %get-tuple-element.22), channel_id=1, source_target_pairs={{0,16},{16,32},{32,48},{48,64},{64,80},{80,96},{96,112},{1,17},{17... | collective-permute-start | bytes 98312 | tf_op jit(solution)/shard_map/ppermute | solution.py:16
  424.1 5.2 %collective-permute-start.13 = (bf16[512,32,1]{0,1,2:T(8,128)(2,1)S(1)}, bf16[512,32,1]{0,1,2:T(8,128)(2,1)S(1)}, u32[]{:S(2)}, u32[]{:S(2)}) collective-permute-start(bf16[512,32,1]{0,1,2:T(8,128)(2,1)S(1)} %get-tuple-element.23), channel_id=1, source_target_pairs={{16,0},{32,16},{48,32},{64,48},{80,64},{96,80},{112,96},{17,1},{33... | collective-permute-start | bytes 98312 | tf_op jit(solution)/shard_map/ppermute | solution.py:19
  429.4 5.3 %collective-permute-start.14 = (bf16[512,1,18]{0,1,2:T(2,128)(2,1)S(1)}, bf16[512,1,18]{0,1,2:T(2,128)(2,1)S(1)}, u32[]{:S(2)}, u32[]{:S(2)}) collective-permute-start(bf16[512,1,18]{0,1,2:T(2,128)(2,1)S(1)} %get-tuple-element.20), channel_id=1, source_target_pairs={{0,1},{1,2},{2,3},{3,4},{4,5},{5,6},{6,7},{7,8},{8,9},{9,10},{10,1... | collective-permute-start | bytes 55304 | tf_op jit(solution)/shard_map/ppermute | solution.py:16
  431.3 7.7 %copy-start.12 = (pred[8,3]{0,1:T(4,128)(4,1)S(1)}, pred[8,3]{0,1:T(4,128)(4,1)}, u32[]{:S(2)}) copy-start(pred[8,3]{0,1:T(4,128)(4,1)} %constant.50) | copy-start | bytes 76
  431.3 6.8 %collective-permute-start.15 = (bf16[512,1,18]{0,1,2:T(2,128)(2,1)S(1)}, bf16[512,1,18]{0,1,2:T(2,128)(2,1)S(1)}, u32[]{:S(2)}, u32[]{:S(2)}) collective-permute-start(bf16[512,1,18]{0,1,2:T(2,128)(2,1)S(1)} %get-tuple-element.21), channel_id=1, source_target_pairs={{1,0},{2,1},{3,2},{4,3},{5,4},{6,5},{7,6},{8,7},{9,8},{10,9},{11,1... | collective-permute-start | bytes 55304 | tf_op jit(solution)/shard_map/ppermute | solution.py:19
  (3 other events, 2.6 us)
where the time goes:
time: 451 us; the launch traced here: 444 us
  waiting for transfers between devices  195 us (43%)
  local copies, waits for them, and re-layouts  91.5 us (20%)
  starting transfers between devices  81.6 us (18%)
  matrix products  64.2 us (14%)
  other arithmetic  10.4 us (2%)
    all_to_all x1, waiting for transfers between devices, body(): lax.all_to_all(leading(raw_slots, tile_dims), ('tx', 'ty'), split_axis=0,...  162 us
    convert_element_type x15, local copies, waits for them, and re-layouts, conv_same(): return jnp.maximum(output, 0.0).astype(jnp.bfloat16)  34.7 us
    conv_general_dilated x4, matrix products, conv_same(): lax.conv_general_dilated(padded[None], kernel, (1, 1), 'VALID', dimension...  29.3 us
    ppermute x8, waiting for transfers between devices, padded_2(): lax.ppermute(lax.slice_in_dim(block, 0, width, axis=dim), axis, backward)  27.3 us
    ppermute x8, starting transfers between devices, padded_2(): lax.ppermute(lax.slice_in_dim(block, block.shape[dim] - width, None, axis...  24.4 us
    ppermute x8, starting transfers between devices, padded_2(): lax.ppermute(lax.slice_in_dim(block, 0, width, axis=dim), axis, backward)  19.9 us
    dot_general x1, matrix products, resample(): jnp.einsum('nbrc,nct->nbrt', rowed, matrices, preferred_element_type=jnp....  18.3 us
    scatter x4, local copies, waits for them, and re-layouts, place(): return buffer.at[slot_index].set(tensor)  15.6 us
  transfers between devices with their start and end apart: 20, of which 11 were waited for; matrix products, arithmetic and copies ran while one was open for 7% of the time, Pallas kernels for 0%

commit v1 on v0

v1 whole, which is shorter than its diff:
```python
import functools

import jax
import jax.numpy as jnp
import numpy as np
from jax import lax
from jax.experimental import pallas as pl
from jax.experimental.pallas import tpu as pltpu
from jax.sharding import PartitionSpec as P

MESH = pl.DeviceIdType.MESH
BANDS = 13
CAP = 2
WIN = 8
NWIN = 32
BR = BANDS * WIN
HALO = 16


def resample_kernel(dest, bank_index, raw, weights, bank, out, tiled, res, count, sem):
    step = pl.program_id(0)
    per = raw.shape[0]
    held = res.shape[0]
    lanes = BANDS * 16

    @pl.when(step == 0)
    def _():
        spread = (
            lax.broadcasted_iota(jnp.int32, (16, lanes), 1) % 16
            == lax.broadcasted_iota(jnp.int32, (16, lanes), 0)
        ).astype(jnp.bfloat16)
        tiled[...] = jnp.dot(weights[...], spread, preferred_element_type=jnp.float32)

        @pl.loop(0, count.shape[0])
        def _(t):
            count[t] = 0

    own_band = (
        lax.broadcasted_iota(jnp.int32, (BANDS, WIN, lanes), 2) // 16
        == lax.broadcasted_iota(jnp.int32, (BANDS, WIN, lanes), 0)
    )
    for k in range(per):
        n = step * per + k
        row = tiled[pl.ds(pl.multiple_of(n * WIN, WIN), WIN), :]
        block = jnp.where(own_band, row[None], 0.0).reshape(BR, lanes).astype(jnp.bfloat16)
        rowed = jnp.dot(
            block, raw[k].reshape(lanes, 128), preferred_element_type=jnp.float32
        ).astype(jnp.bfloat16)
        res[n] = jnp.dot(
            rowed, bank[bank_index[n]], preferred_element_type=jnp.float32
        ).astype(jnp.bfloat16)
        tile = dest[n]
        rank = count[tile]
        count[tile] = rank + 1
        pltpu.make_async_copy(res.at[n], out.at[tile * CAP + rank], sem).start()

    @pl.when(step == pl.num_programs(0) - 1)
    def _():
        pltpu.make_async_copy(res, out.at[pl.ds(0, held)], sem).wait()


def resample(raw, weights, bank, dest, bank_index, tiles):
    held = raw.shape[0]
    per = 8
    return pl.pallas_call(
        resample_kernel,
        grid=(held // per,),
        in_specs=[
            pl.BlockSpec(memory_space=pltpu.SMEM),
            pl.BlockSpec(memory_space=pltpu.SMEM),
            pl.BlockSpec((per, BANDS, 16, 128), lambda i: (i, 0, 0, 0)),
            pl.BlockSpec((held * WIN, 16), lambda i: (0, 0)),
            pl.BlockSpec(bank.shape, lambda i: (0, 0, 0)),
        ],
        out_specs=pl.BlockSpec(memory_space=pl.ANY),
        out_shape=jax.ShapeDtypeStruct((tiles * CAP, BR, 128), jnp.bfloat16),
        scratch_shapes=[
            pltpu.VMEM((held * WIN, BANDS * 16), jnp.float32),
            pltpu.VMEM((held, BR, 128), jnp.bfloat16),
            pltpu.SMEM((tiles,), jnp.int32),
            pltpu.SemaphoreType.DMA,
        ],
        compiler_params=pltpu.CompilerParams(vmem_limit_bytes=24 << 20),
        name="resample",
    )(dest, bank_index, raw, weights.reshape(held * WIN, 16), bank)


def gather_kernel(window, got, gridded, turned, acc, count):
    step = pl.program_id(0)
    per = got.shape[0]

    @pl.when(step == 0)
    def _():
        acc[...] = jnp.zeros_like(acc)

        @pl.loop(0, NWIN)
        def _(t):
            count[t] = 0

    @pl.loop(0, per)
    def _(k):
        w = window[step * per + k]

        @pl.when(w >= 0)
        def _():
            acc[w] += got[k].astype(jnp.float32)
            count[w] = count[w] + 1

    @pl.when(step == pl.num_programs(0) - 1)
    def _():
        pad = jnp.zeros((128 - BR, 128), jnp.float32)

        @pl.loop(0, NWIN // 2)
        def _(p):
            pair = []
            for e in range(2):
                w = p * 2 + e
                divisor = jnp.maximum(count[w], 1).astype(jnp.float32)
                mean = acc[w] / jnp.full((BR, 128), divisor, jnp.float32)
                pair.append(mean)
                turned[w] = jnp.concatenate([mean, pad], axis=0).T.astype(jnp.bfloat16)
            for b in range(BANDS):
                rows = slice(b * WIN, (b + 1) * WIN)
                gridded[b, pl.ds(pl.multiple_of(p * 16, 16), 16), :] = jnp.concatenate(
                    [pair[0][rows], pair[1][rows]], axis=0
                ).astype(jnp.bfloat16)


def gather_windows(got, window):
    slots = got.shape[0]
    per = 16
    return pl.pallas_call(
        gather_kernel,
        grid=(slots // per,),
        in_specs=[
            pl.BlockSpec(memory_space=pltpu.SMEM),
            pl.BlockSpec((per, BR, 128), lambda i: (i, 0, 0)),
        ],
        out_specs=[
            pl.BlockSpec((BANDS, NWIN * WIN, 128), lambda i: (0, 0, 0)),
            pl.BlockSpec((NWIN, 128, 128), lambda i: (0, 0, 0)),
        ],
        out_shape=[
            jax.ShapeDtypeStruct((BANDS, NWIN * WIN, 128), jnp.bfloat16),
            jax.ShapeDtypeStruct((NWIN, 128, 128), jnp.bfloat16),
        ],
        scratch_shapes=[
            pltpu.VMEM((NWIN, BR, 128), jnp.float32),
            pltpu.SMEM((NWIN,), jnp.int32),
        ],
        compiler_params=pltpu.CompilerParams(vmem_limit_bytes=24 << 20),
        name="gather_windows",
    )(window, got)


HALO_WIN = HALO // WIN
LAST_WIN = NWIN + HALO_WIN
LAST_COL = 128 + HALO
SIDE = {
    -1: ((0, HALO_WIN), (LAST_WIN, HALO_WIN)),
    0: ((0, NWIN), (HALO_WIN, NWIN)),
    1: ((NWIN - HALO_WIN, HALO_WIN), (0, HALO_WIN)),
}
EDGE = {
    -1: ((0, HALO), (LAST_COL, HALO)),
    0: ((0, 128), (HALO, 128)),
    1: ((128 - HALO, HALO), (0, HALO)),
}
MOVES = [(1, 0), (-1, 0), (0, 1), (0, -1), (1, 1), (1, -1), (-1, 1), (-1, -1)]


def widen_kernel(zeros, tile, wide, own_sem, zero_sem, send_sem, recv_sem):
    tx, ty = lax.axis_index("tx"), lax.axis_index("ty")
    nx, ny = lax.axis_size("tx"), lax.axis_size("ty")

    def inside(dx, dy):
        ok = None
        for d, at, n in ((dx, tx, nx), (dy, ty, ny)):
            if d:
                here = at + d >= 0 if d < 0 else at + d < n
                ok = here if ok is None else jnp.logical_and(ok, here)
        return ok

    def source(dx, dy):
        (w, wn), (c, cn) = SIDE[dy][0], EDGE[dx][0]
        return tile.at[pl.ds(w, wn), pl.ds(c, cn)]

    def target(dx, dy):
        (w, wn), (c, cn) = SIDE[dy][1], EDGE[dx][1]
        return wide.at[pl.ds(w, wn), pl.ds(c, cn)]

    barrier = pltpu.get_barrier_semaphore()
    for dx, dy in MOVES:

        @pl.when(inside(dx, dy))
        def _():
            pl.semaphore_signal(
                barrier, inc=1, device_id=(tx + dx, ty + dy), device_id_type=MESH
            )

    own = pltpu.make_async_copy(tile, target(0, 0), own_sem)
    own.start()
    peers = sum(inside(dx, dy).astype(jnp.int32) for dx, dy in MOVES)
    pl.semaphore_wait(barrier, peers)

    copies = []
    for i, (dx, dy) in enumerate(MOVES):
        send = pltpu.make_async_remote_copy(
            src_ref=source(dx, dy),
            dst_ref=target(dx, dy),
            send_sem=send_sem.at[i],
            recv_sem=recv_sem.at[i],
            device_id=(tx + dx, ty + dy),
            device_id_type=MESH,
        )
        (w, wn), (c, cn) = SIDE[dy][1], EDGE[dx][1]
        blank = pltpu.make_async_copy(
            zeros.at[pl.ds(0, wn), pl.ds(0, cn)], target(dx, dy), zero_sem.at[i]
        )
        copies.append((send, blank, inside(dx, dy), inside(-dx, -dy)))
    for send, blank, goes, comes in copies:

        @pl.when(goes)
        def _():
            send.start()

        @pl.when(jnp.logical_not(comes))
        def _():
            blank.start()

    own.wait()
    for send, blank, goes, comes in copies:

        @pl.when(goes)
        def _():
            send.wait_send()

        @pl.when(comes)
        def _():
            send.wait_recv()

        @pl.when(jnp.logical_not(comes))
        def _():
            blank.wait()


def widen(turned):
    moves = len(MOVES)
    return pl.pallas_call(
        widen_kernel,
        in_specs=[pl.BlockSpec(memory_space=pltpu.VMEM), pl.BlockSpec(memory_space=pl.ANY)],
        out_specs=pl.BlockSpec(memory_space=pl.ANY),
        out_shape=jax.ShapeDtypeStruct(
            (NWIN + 2 * HALO_WIN, 128 + 2 * HALO, 128), jnp.bfloat16
        ),
        scratch_shapes=[
            pltpu.SemaphoreType.DMA,
            pltpu.SemaphoreType.DMA((moves,)),
            pltpu.SemaphoreType.DMA((moves,)),
            pltpu.SemaphoreType.DMA((moves,)),
        ],
        compiler_params=pltpu.CompilerParams(
            collective_id=0, has_side_effects=True, vmem_limit_bytes=16 << 20
        ),
        name="widen",
    )(jnp.zeros((NWIN, 128, 128), jnp.bfloat16), turned)


HALVES = 8
PIX = 80


def level_one_kernel(limits, wide, weight_one, weight_two, out, slab, patch):
    step = pl.program_id(0)
    last = wide.shape[0] - 1
    cols = wide.shape[1]
    low = lax.broadcasted_iota(jnp.int32, (cols, 128), 1) % 8 < 4
    for k in range(HALVES):
        w = step * (HALVES // 2) + k // 2
        here = wide[jnp.minimum(w, last)].astype(jnp.float32)
        if k % 2:
            after = wide[jnp.minimum(w + 1, last)].astype(jnp.float32)
            here = jnp.where(low, pltpu.roll(here, 124, 1), pltpu.roll(after, 4, 1))
        slab[k, pl.ds(0, cols), :] = here
        for q in range(4):
            patch[k, :, q * 128 : (q + 1) * 128] = slab[
                k, pl.ds(1 + q, PIX, stride=2), :
            ].astype(jnp.bfloat16)
    hidden = jnp.dot(
        patch[...].reshape(HALVES * PIX, 512), weight_one[...], preferred_element_type=jnp.float32
    )
    hidden = jnp.maximum(hidden, 0.0).astype(jnp.bfloat16)
    col = lax.broadcasted_iota(jnp.int32, (PIX, 128), 0) - 7
    col_ok = jnp.logical_and(col >= limits[2], col < limits[3])
    for e in range(2):
        down = jnp.dot(
            hidden[:, e * 256 : (e + 1) * 256],
            weight_two[...],
            preferred_element_type=jnp.float32,
        )
        down = jnp.maximum(down, 0.0).reshape(HALVES, PIX, 128)
        for k in range(HALVES):
            row = (step * HALVES + k) * 2 + e - 7
            row_ok = jnp.logical_and(row >= limits[0], row < limits[1])
            keep = jnp.logical_and(col_ok, row_ok)
            out[k * 2 + e] = jnp.where(keep, down[k], 0.0).astype(jnp.bfloat16)


def level_one(wide, weight_one, weight_two, limits):
    steps = 9
    return pl.pallas_call(
        level_one_kernel,
        grid=(steps,),
        in_specs=[
            pl.BlockSpec(memory_space=pltpu.SMEM),
            pl.BlockSpec(wide.shape, lambda i: (0, 0, 0)),
            pl.BlockSpec(weight_one.shape, lambda i: (0, 0)),
            pl.BlockSpec(weight_two.shape, lambda i: (0, 0)),
        ],
        out_specs=pl.BlockSpec((2 * HALVES, PIX, 128), lambda i: (i, 0, 0)),
        out_shape=jax.ShapeDtypeStruct((steps * 2 * HALVES, PIX, 128), jnp.bfloat16),
        scratch_shapes=[
            pltpu.VMEM((HALVES, 168, 128), jnp.float32),
            pltpu.VMEM((HALVES, PIX, 512), jnp.bfloat16),
        ],
        compiler_params=pltpu.CompilerParams(vmem_limit_bytes=32 << 20),
        name="level_one",
    )(limits, wide, weight_one, weight_two)


def patch_weights(kernel):
    rows = np.zeros((8, 4, 3), np.float32)
    for r in range(8):
        for y in range(4):
            u = r - (2 + y) + 1
            if 0 <= u < 3:
                rows[r, y, u] = 1
    cols = np.zeros((4, 2, 3), np.float32)
    for q in range(4):
        for g in range(2):
            v = q - g
            if 0 <= v < 3:
                cols[q, g, v] = 1
    spread = jnp.einsum("ryu,uvbo->rybvo", jnp.asarray(rows, jnp.bfloat16), kernel)
    spread = jnp.einsum("qgv,rybvo->qbrygo", jnp.asarray(cols, jnp.bfloat16), spread)
    spread = spread.reshape(4, BR, 512).astype(jnp.bfloat16)
    return jnp.pad(spread, ((0, 0), (0, 128 - BR), (0, 0))).reshape(512, 512)


def conv(field, kernel, stride):
    out = lax.conv_general_dilated(
        field[None],
        kernel,
        (stride, stride),
        "VALID",
        dimension_numbers=("NHWC", "HWIO", "NHWC"),
        preferred_element_type=jnp.float32,
    )[0]
    return jnp.maximum(out, 0.0)


def on_map(field, halo, tx, ty, nx, ny):
    rows = jnp.arange(field.shape[0]) - halo
    cols = jnp.arange(field.shape[1]) - halo
    r = (rows + ty * (field.shape[0] - 2 * halo) >= 0) & (
        rows + ty * (field.shape[0] - 2 * halo) < ny * (field.shape[0] - 2 * halo)
    )
    c = (cols + tx * (field.shape[1] - 2 * halo) >= 0) & (
        cols + tx * (field.shape[1] - 2 * halo) < nx * (field.shape[1] - 2 * halo)
    )
    return jnp.where((r[:, None] & c[None, :])[:, :, None], field, 0.0)


def body(
    granule_blocks,
    row_weights,
    column_bank,
    destination,
    window_index,
    bank_index,
    kernel_one,
    reduce_two,
    kernel_two,
    reduce_three,
    kernel_three,
    reduce_four,
    kernel_four,
):
    nx, ny = lax.axis_size("tx"), lax.axis_size("ty")
    tx, ty = lax.axis_index("tx"), lax.axis_index("ty")
    tiles = nx * ny
    held = destination.shape[0]
    tags = lax.all_gather(destination * NWIN + window_index, ("tx", "ty"), tiled=False)
    sent = resample(granule_blocks, row_weights, column_bank, destination, bank_index, tiles)
    got = lax.all_to_all(
        sent.reshape(tiles, CAP * BR, 128), ("tx", "ty"), split_axis=0, concat_axis=0, tiled=True
    ).reshape(tiles * CAP, BR, 128)
    tags = tags.reshape(tiles, held)
    mine = tags // NWIN == tx * ny + ty
    code = jnp.arange(held, dtype=jnp.int32)[None, :] * NWIN + tags % NWIN
    hits = jnp.sum(mine.astype(jnp.int32), axis=1)
    first = jnp.min(jnp.where(mine, code, held * NWIN), axis=1)
    second = jnp.max(jnp.where(mine, code, -1), axis=1)
    window = jnp.stack(
        [
            jnp.where(hits >= 1, first % NWIN, -1),
            jnp.where(hits >= 2, second % NWIN, -1),
        ],
        axis=1,
    ).reshape(tiles * CAP)
    gridded, turned = gather_windows(got, window)
    wide = widen(turned)
    far = 1 << 20
    limits = jnp.stack(
        [
            jnp.where(ty == 0, 0, -far),
            jnp.where(ty == ny - 1, 128, far),
            jnp.where(tx == 0, 0, -far),
            jnp.where(tx == nx - 1, 64, far),
        ]
    ).astype(jnp.int32)
    down_two = level_one(wide, patch_weights(kernel_one), reduce_two.reshape(256, 128), limits)
    level_two = conv(down_two[:142, :78], kernel_two, 1).astype(jnp.bfloat16)
    down_three = on_map(conv(level_two, reduce_three, 2), 3, tx, ty, nx, ny).astype(jnp.bfloat16)
    level_three = conv(down_three, kernel_three, 1).astype(jnp.bfloat16)
    down_four = on_map(conv(level_three, reduce_four, 2), 1, tx, ty, nx, ny).astype(jnp.bfloat16)
    bottleneck = conv(down_four, kernel_four, 1).astype(jnp.bfloat16)
    return (gridded, jnp.transpose(bottleneck, (2, 0, 1)))


def solution(mesh):
    in_specs = (
        P(("tx", "ty"), None, None, None),
        P(("tx", "ty"), None, None),
        P(),
        P(("tx", "ty")),
        P(("tx", "ty")),
        P(("tx", "ty")),
        P(),
        P(),
        P(),
        P(),
        P(),
        P(),
        P(),
    )
    out_specs = (P(None, "ty", "tx"), P(None, "ty", "tx"))
    return jax.shard_map(body, mesh=mesh, in_specs=in_specs, out_specs=out_specs, check_vma=False)
```

time: 451 us -> 239 us (0.53)
  the two profiles are of different devices: /device:TPU:29 before, /device:TPU:1 now
where the time goes in v1:
time: 239 us; the launch traced here: 237 us
  blocking collectives  138 us (58%)
  Pallas kernels  49.4 us (21%)
  local copies, waits for them, and re-layouts  17.6 us (7%)
  matrix products  17.1 us (7%)
  starting transfers between devices  11.9 us (5%)
    unnamed x1, blocking collectives  138 us
    pallas_call x1, Pallas kernels, resample(): pl.pallas_call(resample_kernel, grid=(held // per,), in_specs=[pl.BlockSp...  21.1 us
    conv_general_dilated x5, matrix products, conv(): lax.conv_general_dilated(field[None], kernel, (stride, stride), 'VALID',...  16.3 us
    pallas_call x1, Pallas kernels, gather_windows(): pl.pallas_call(gather_kernel, grid=(slots // per,), in_specs=[pl.BlockSpe...  14.2 us
    all_to_all x1, starting transfers between devices, body(): lax.all_to_all(sent.reshape(tiles, CAP * BR, 128), ('tx', 'ty'), split_ax...  11.9 us
    unnamed x44, local copies, waits for them, and re-layouts  10.7 us
    pallas_call x1, Pallas kernels, level_one(): pl.pallas_call(level_one_kernel, grid=(steps,), in_specs=[pl.BlockSpec(me...  7.72 us
    pallas_call x1, Pallas kernels, widen(): pl.pallas_call(widen_kernel, in_specs=[pl.BlockSpec(memory_space=pltpu.VM...  6.51 us
  transfers between devices with their start and end apart: 1, of which 0 were waited for; matrix products, arithmetic and copies ran while one was open for 1% of the time, Pallas kernels for 0%

profile of v1, /device:TPU:1, one launch (start us, length us, event | category | flops | bytes accessed | tf_op | source)
XLA Modules:
  0.0 237.1 jit_solution(11320581605536141269)
XLA Ops:
  0.6 1.0 copy.21
  1.6 2.0 copy-done.2
  3.6 0.9 copy-done.3
  4.6 0.7 copy-done.5
  5.2 0.7 copy-done.7
  5.9 21.1 %resample.1 = bf16[256,104,128]{2,1,0:T(8,128)(2,1)S(1)} custom-call(s32[64]{0:T(128)S(1)} %copy-done.5, s32[64]{0:T(128)S(1)} %copy-done.7, bf16[64,13,16,128]{3,2,1,0:T(8,128)(2,1)S(1)} %copy-done.2, bf16[512,16]{1,0:T(8,128)(2,1)S(1)} %bitcast.83, bf16[8,128,128]{2,1,0:T(8,128)(2,1)S(1)} %copy-done.3), custom_call_target="tpu_custom_call" | custom-call | tf_op jit(solution)/shard_map/resample/pallas_call | solution.py:65
  26.9 2.9 %copy-done.1 = bf16[256,104,128]{2,1,0:T(8,128)(2,1)} copy-done((bf16[256,104,128]{2,1,0:T(8,128)(2,1)}, bf16[256,104,128]{2,1,0:T(8,128)(2,1)S(1)}, u32[]{:S(2)}) %copy-start.1) | copy-done | bytes 6815768
  29.8 11.9 %all-to-all-start = ((bf16[128,208,128]{2,1,0:T(8,128)(2,1)}), bf16[128,208,128]{2,1,0:T(8,128)(2,1)}, u32[]{:S(2)}, u32[]{:S(2)}) async-start(bf16[128,208,128]{2,1,0:T(8,128)(2,1)} %bitcast.81), calls=%async_computation | async-start | bytes 13631488 | tf_op jit(solution)/shard_map/all_to_all | solution.py:395
  41.9 138.2 %all-reduce.1 = s32[8192]{0:T(1024)S(1)} all-reduce(s32[8192]{0:T(1024)S(1)} %add_dynamic-update-slice_fusion), channel_id=2, replica_groups=mesh['tx'=8,'ty'=16] {'tx','ty'}, use_global_device_ids=true, to_apply=%add.1 | all-reduce | flops 8192 | bytes 65536
  180.9 0.6 convolution_bitcast_fusion
  181.5 0.9 copy.22
  182.5 0.5 reshape.221
  183.3 14.2 %gather_windows.1 = (bf16[13,256,128]{2,1,0:T(8,128)(2,1)}, bf16[32,128,128]{2,1,0:T(8,128)(2,1)S(1)}) custom-call(s32[256]{0:T(256)S(1)} %reshape.217.window, bf16[256,104,128]{2,1,0:T(8,128)(2,1)} %bitcast.6.got), custom_call_target="tpu_custom_call" | custom-call | tf_op jit(solution)/shard_map/gather_windows/pallas_call | solution.py:132
  197.7 6.5 %widen.1.wide = bf16[36,160,128]{2,1,0:T(8,128)(2,1)S(1)} custom-call(bf16[32,128,128]{2,1,0:T(8,128)(2,1)S(1)} %broadcast_in_dim.51.zeros, bf16[32,128,128]{2,1,0:T(8,128)(2,1)S(1)} %get-tuple-element.5.tile), custom_call_target="tpu_custom_call" | custom-call | tf_op jit(solution)/shard_map/widen/pallas_call | solution.py:249
  204.3 7.7 %level_one.1 = bf16[144,80,128]{2,1,0:T(8,128)(2,1)S(1)} custom-call(s32[4]{0:T(128)S(1)} %pad_add_fusion.1.limits, bf16[36,160,128]{2,1,0:T(8,128)(2,1)S(1)} %widen.1.wide, bf16[512,512]{1,0:T(8,128)(2,1)S(1)} %bitcast.82, bf16[256,128]{1,0:T(8,128)(2,1)S(1)} %bitcast.84), custom_call_target="tpu_custom_call" | custom-call | tf_op jit(solution)/shard_map/level_one/pallas_call | solution.py:311
  212.0 0.5 slice_bitcast_fusion
  212.5 0.7 copy.42
  213.5 1.1 copy.25
  214.8 7.1 %fusion.19 = bf16[140,1,8,10,128]{4,2,3,0,1:T(8,128)(2,1)S(1)} fusion(pred[8,10]{0,1:T(8,128)(4,1)S(1)} %copy-done.15, bf16[3,3,128,128]{3,2,1,0:T(8,128)(2,1)S(1)} %copy-done.13, bf16[142,1,7,2,128]{4,2,3,0,1:T(8,128)(2,1)S(1)} %slice.13, bf16[142,1,8,10,128]{4,2,3,0,1:T(8,128)(2,1)S(1)} %copy.25), kind=kOutput, calls=%fused_computation.23 | convolution fusion | flops 3319218176 | bytes 6579280 | tf_op jit(solution)/shard_map/conv_general_dilated | solution.py:351
  222.0 0.9 fusion.36
  222.9 0.3 copy.26
  223.2 0.8 fusion.20
  224.2 0.3 copy.28
  224.7 3.4 %fusion.49 = bf16[68,8,5,256]{3,1,2,0:T(8,128)(2,1)S(1)} fusion(bf16[3,3,256,256]{3,2,1,0:T(8,128)(2,1)S(1)} %copy-done, bf16[70,1,7,2,256]{4,2,3,0,1:T(8,128)(2,1)S(1)} %slice.16, bf16[70,1,8,5,256]{4,2,3,0,1:T(8,128)(2,1)S(1)} %copy.28, pred[8,5]{0,1:T(8,128)(4,1)S(1)} %copy-done.16), kind=kOutput, calls=%fused_computation.48 | convolution fusion | flops 3217448960 | bytes 4507688 | tf_op jit(solution)/shard_map/conv_general_dilated | solution.py:351
  228.2 0.3 copy.29
  228.6 0.6 copy.31
  229.2 0.6 copy-done.12
  229.8 1.0 fusion.41
  230.8 0.3 copy.32
  231.1 0.2 fusion.44
  231.9 3.8 %maximum_convert_fusion.2 = bf16[32,8,3,512]{3,1,2,0:T(8,128)(2,1)S(1)} fusion(bf16[3,3,512,512]{3,2,1,0:T(8,128)(2,1)S(1)} %bitcast.95, bf16[34,1,7,2,512]{4,2,3,0,1:T(8,128)(2,1)S(1)} %slice.19, bf16[34,1,8,3,512]{4,2,3,0,1:T(8,128)(2,1)S(1)} %copy.34, pred[8,3]{0,1:T(4,128)(4,1)S(1)} %copy-done.17), kind=kOutput, calls=%fused_computation.44 | convolution fusion | flops 3629236224 | bytes 6828056 | tf_op jit(solution)/shard_map/conv_general_dilated | solution.py:351
  236.0 1.1 copy.36
  (67 shorter events, 3.2 us)
Async XLA Ops:
  0.6 224.0 %copy-start = (bf16[3,3,256,256]{3,2,1,0:T(8,128)(2,1)S(1)}, bf16[3,3,256,256]{3,2,1,0:T(8,128)(2,1)}, u32[]{:S(2)}) copy-start(bf16[3,3,256,256]{3,2,1,0:T(8,128)(2,1)} %param.25) | copy-start | bytes 3538948
  1.6 2.0 copy-start.2
  3.6 0.9 copy-start.3
  4.5 0.7 copy-start.5
  5.2 0.7 copy-start.7
  26.9 2.9 %copy-start.1 = (bf16[256,104,128]{2,1,0:T(8,128)(2,1)}, bf16[256,104,128]{2,1,0:T(8,128)(2,1)S(1)}, u32[]{:S(2)}) copy-start(bf16[256,104,128]{2,1,0:T(8,128)(2,1)S(1)} %resample.1) | copy-start | bytes 20447236
  29.8 12.0 %copy-start.6 = (s32[64]{0:T(128)S(1)}, s32[64]{0:T(128)}, u32[]{:S(2)}) copy-start(s32[64]{0:T(128)} %dest.1) | copy-start | bytes 772
  29.8 12.0 %copy-start.11 = (s32[64]{0:T(128)S(1)}, s32[64]{0:T(128)}, u32[]{:S(2)}) copy-start(s32[64]{0:T(128)} %param.19) | copy-start | bytes 772
  29.8 150.9 %copy-start.8 = (bf16[3,3,13,64]{3,2,1,0:T(8,128)(2,1)S(1)}, bf16[3,3,13,64]{3,2,1,0:T(8,128)(2,1)}, u32[]{:S(2)}) copy-start(bf16[3,3,13,64]{3,2,1,0:T(8,128)(2,1)} %param.21) | copy-start | bytes 44932
  29.8 150.9 %copy-start.9 = (bf16[8,4,3,1,1]{2,1,4,3,0:T(4,128)(2,1)S(1)}, bf16[8,4,3,1,1]{2,1,4,3,0:T(4,128)(2,1)}, u32[]{:S(2)}) copy-start(bf16[8,4,3,1,1]{2,1,4,3,0:T(4,128)(2,1)} %constant.148) | copy-start | bytes 580
  29.8 151.1 %copy-start.10 = (bf16[4,2,3,1,1,1]{2,0,1,5,4,3:T(4,128)(2,1)S(1)}, bf16[4,2,3,1,1,1]{2,0,1,5,4,3:T(4,128)(2,1)}, u32[]{:S(2)}) copy-start(bf16[4,2,3,1,1,1]{2,0,1,5,4,3:T(4,128)(2,1)} %constant.149) | copy-start | bytes 148
  29.8 153.5 %all-to-all-start = ((bf16[128,208,128]{2,1,0:T(8,128)(2,1)}), bf16[128,208,128]{2,1,0:T(8,128)(2,1)}, u32[]{:S(2)}, u32[]{:S(2)}) async-start(bf16[128,208,128]{2,1,0:T(8,128)(2,1)} %bitcast.81), calls=%async_computation | async-start | bytes 13631488 | tf_op jit(solution)/shard_map/all_to_all | solution.py:395
  197.5 6.8 %copy-start.4 = (bf16[2,2,64,128]{3,2,1,0:T(8,128)(2,1)S(1)}, bf16[2,2,64,128]{3,2,1,0:T(8,128)(2,1)}, u32[]{:S(2)}) copy-start(bf16[2,2,64,128]{3,2,1,0:T(8,128)(2,1)} %param.22) | copy-start | bytes 196612
  213.5 1.3 copy-start.13
  213.5 1.3 copy-start.15
  214.8 7.2 %copy-start.14 = (bf16[2,2,128,256]{3,2,1,0:T(8,128)(2,1)S(1)}, bf16[2,2,128,256]{3,2,1,0:T(8,128)(2,1)}, u32[]{:S(2)}) copy-start(bf16[2,2,128,256]{3,2,1,0:T(8,128)(2,1)} %param.24) | copy-start | bytes 786436
  224.0 0.7 copy-start.16
  228.6 1.2 copy-start.12
  228.6 3.3 %slice-start = ((s8[4718592]{0:T(1024)(128)(4,1)}), s8[4194304]{0:T(1024)(128)(4,1)S(1)}, s32[]{:S(2)}) async-start(s8[4718592]{0:T(1024)(128)(4,1)} %bitcast.94), calls=%async_computation.1 | async-start | bytes 8388608
  229.8 2.1 slice-start.1
  231.1 0.8 copy-start.17

commit v2 on v1

--- a/solution.py
+++ b/solution.py
@@ -15,6 +15,7 @@
 NWIN = 32
 BR = BANDS * WIN
 HALO = 16
+BIG_VMEM = 56 << 20
 
 
 def resample_kernel(dest, bank_index, raw, weights, bank, out, tiled, res, count, sem):
@@ -39,16 +40,23 @@
         lax.broadcasted_iota(jnp.int32, (BANDS, WIN, lanes), 2) // 16
         == lax.broadcasted_iota(jnp.int32, (BANDS, WIN, lanes), 0)
     )
+    rowed = []
     for k in range(per):
         n = step * per + k
         row = tiled[pl.ds(pl.multiple_of(n * WIN, WIN), WIN), :]
         block = jnp.where(own_band, row[None], 0.0).reshape(BR, lanes).astype(jnp.bfloat16)
-        rowed = jnp.dot(
-            block, raw[k].reshape(lanes, 128), preferred_element_type=jnp.float32
+        rowed.append(
+            jnp.dot(
+                block, raw[k].reshape(lanes, 128), preferred_element_type=jnp.float32
+            ).astype(jnp.bfloat16)
+        )
+    for k in range(per):
+        n = step * per + k
+        res[n] = jnp.dot(
+            rowed[k], bank[bank_index[n]], preferred_element_type=jnp.float32
         ).astype(jnp.bfloat16)
-        res[n] = jnp.dot(
-            rowed, bank[bank_index[n]], preferred_element_type=jnp.float32
-        ).astype(jnp.bfloat16)
+    for k in range(per):
+        n = step * per + k
         tile = dest[n]
         rank = count[tile]
         count[tile] = rank + 1
@@ -61,7 +69,7 @@
 
 def resample(raw, weights, bank, dest, bank_index, tiles):
     held = raw.shape[0]
-    per = 8
+    per = 16
     return pl.pallas_call(
         resample_kernel,
         grid=(held // per,),
@@ -72,7 +80,7 @@
             pl.BlockSpec((held * WIN, 16), lambda i: (0, 0)),
             pl.BlockSpec(bank.shape, lambda i: (0, 0, 0)),
         ],
-        out_specs=pl.BlockSpec(memory_space=pl.ANY),
+        out_specs=pl.BlockSpec(memory_space=pltpu.HBM),
         out_shape=jax.ShapeDtypeStruct((tiles * CAP, BR, 128), jnp.bfloat16),
         scratch_shapes=[
             pltpu.VMEM((held * WIN, BANDS * 16), jnp.float32),
@@ -80,60 +88,52 @@
             pltpu.SMEM((tiles,), jnp.int32),
             pltpu.SemaphoreType.DMA,
         ],
-        compiler_params=pltpu.CompilerParams(vmem_limit_bytes=24 << 20),
+        compiler_params=pltpu.CompilerParams(vmem_limit_bytes=BIG_VMEM),
         name="resample",
     )(dest, bank_index, raw, weights.reshape(held * WIN, 16), bank)
 
 
-def gather_kernel(window, got, gridded, turned, acc, count):
+def gather_kernel(window, inverse, got, gridded, turned, even, odd):
     step = pl.program_id(0)
     per = got.shape[0]
 
     @pl.when(step == 0)
     def _():
-        acc[...] = jnp.zeros_like(acc)
-
-        @pl.loop(0, NWIN)
-        def _(t):
-            count[t] = 0
-
-    @pl.loop(0, per)
-    def _(k):
-        w = window[step * per + k]
-
-        @pl.when(w >= 0)
-        def _():
-            acc[w] += got[k].astype(jnp.float32)
-            count[w] = count[w] + 1
+        even[...] = jnp.zeros_like(even)
+        odd[...] = jnp.zeros_like(odd)
+
+    @pl.loop(0, per // 8)
+    def _(group):
+        for u in range(8):
+            k = group * 8 + u
+            total = odd if u % 2 else even
+            total[window[step * per + k]] += got[k].astype(jnp.float32)
 
     @pl.when(step == pl.num_programs(0) - 1)
     def _():
         pad = jnp.zeros((128 - BR, 128), jnp.float32)
-
-        @pl.loop(0, NWIN // 2)
-        def _(p):
+        for p in range(NWIN // 2):
             pair = []
-            for e in range(2):
-                w = p * 2 + e
-                divisor = jnp.maximum(count[w], 1).astype(jnp.float32)
-                mean = acc[w] / jnp.full((BR, 128), divisor, jnp.float32)
+            for w in (2 * p, 2 * p + 1):
+                mean = (even[w] + odd[w]) * inverse[w : w + 1, :]
                 pair.append(mean)
-                turned[w] = jnp.concatenate([mean, pad], axis=0).T.astype(jnp.bfloat16)
+                turned[w] = jnp.concatenate([mean, pad], axis=0).astype(jnp.bfloat16).T
             for b in range(BANDS):
                 rows = slice(b * WIN, (b + 1) * WIN)
-                gridded[b, pl.ds(pl.multiple_of(p * 16, 16), 16), :] = jnp.concatenate(
+                gridded[b, p * 16 : (p + 1) * 16, :] = jnp.concatenate(
                     [pair[0][rows], pair[1][rows]], axis=0
                 ).astype(jnp.bfloat16)
 
 
-def gather_windows(got, window):
+def gather_windows(got, window, inverse):
     slots = got.shape[0]
-    per = 16
+    per = 64
     return pl.pallas_call(
         gather_kernel,
         grid=(slots // per,),
         in_specs=[
             pl.BlockSpec(memory_space=pltpu.SMEM),
+            pl.BlockSpec((NWIN, 128), lambda i: (0, 0)),
             pl.BlockSpec((per, BR, 128), lambda i: (i, 0, 0)),
         ],
         out_specs=[
@@ -144,13 +144,10 @@
             jax.ShapeDtypeStruct((BANDS, NWIN * WIN, 128), jnp.bfloat16),
             jax.ShapeDtypeStruct((NWIN, 128, 128), jnp.bfloat16),
         ],
-        scratch_shapes=[
-            pltpu.VMEM((NWIN, BR, 128), jnp.float32),
-            pltpu.SMEM((NWIN,), jnp.int32),
-        ],
-        compiler_params=pltpu.CompilerParams(vmem_limit_bytes=24 << 20),
+        scratch_shapes=[pltpu.VMEM((NWIN + 1, BR, 128), jnp.float32)] * 2,
+        compiler_params=pltpu.CompilerParams(vmem_limit_bytes=32 << 20),
         name="gather_windows",
-    )(window, got)
+    )(window, inverse, got)
 
 
 HALO_WIN = HALO // WIN
@@ -390,12 +387,13 @@
     tx, ty = lax.axis_index("tx"), lax.axis_index("ty")
     tiles = nx * ny
     held = destination.shape[0]
-    tags = lax.all_gather(destination * NWIN + window_index, ("tx", "ty"), tiled=False)
+    tags = jnp.pad((destination * NWIN + window_index)[None, :], ((0, 15), (0, 128 - held)))
+    tags = lax.all_gather(tags, ("tx", "ty"), tiled=True)
     sent = resample(granule_blocks, row_weights, column_bank, destination, bank_index, tiles)
     got = lax.all_to_all(
         sent.reshape(tiles, CAP * BR, 128), ("tx", "ty"), split_axis=0, concat_axis=0, tiled=True
     ).reshape(tiles * CAP, BR, 128)
-    tags = tags.reshape(tiles, held)
+    tags = tags.reshape(tiles, 16, 128)[:, 0, :held]
     mine = tags // NWIN == tx * ny + ty
     code = jnp.arange(held, dtype=jnp.int32)[None, :] * NWIN + tags % NWIN
     hits = jnp.sum(mine.astype(jnp.int32), axis=1)
@@ -403,12 +401,18 @@
     second = jnp.max(jnp.where(mine, code, -1), axis=1)
     window = jnp.stack(
         [
-            jnp.where(hits >= 1, first % NWIN, -1),
-            jnp.where(hits >= 2, second % NWIN, -1),
+            jnp.where(hits >= 1, first % NWIN, NWIN),
+            jnp.where(hits >= 2, second % NWIN, NWIN),
         ],
         axis=1,
     ).reshape(tiles * CAP)
-    gridded, turned = gather_windows(got, window)
+    counts = jnp.sum(
+        (window[None, :] == jnp.arange(NWIN, dtype=jnp.int32)[:, None]).astype(jnp.int32), axis=1
+    )
+    inverse = jnp.broadcast_to(
+        (1.0 / jnp.maximum(counts, 1).astype(jnp.float32))[:, None], (NWIN, 128)
+    )
+    gridded, turned = gather_windows(got, window, inverse)
     wide = widen(turned)
     far = 1 << 20
     limits = jnp.stack(

time: 239 us -> 198 us (0.83)
  blocking collectives: 138 us -> 0 us
  waiting for transfers between devices: 0.01 us -> 114 us
  Pallas kernels: 49.4 us -> 25.6 us
  between operations: 1.22 us -> 14.6 us
  local copies, waits for them, and re-layouts: 17.6 us -> 12.8 us
    unnamed x1 -> x0, blocking collectives: 138 us -> none
    all_gather x0 -> x1, waiting for transfers between devices: none -> 114 us  [body(): tags = lax.all_gather(tags, ('tx', 'ty'), tiled=True)]
    pallas_call x1, Pallas kernels: 21.1 us -> 6.35 us  [resample(): pl.pallas_call(resample_kernel, grid=(held // per,), in_specs=[pl.BlockSp...]
    pallas_call x1, Pallas kernels: 14.2 us -> 5.74 us  [gather_windows(): pl.pallas_call(gather_kernel, grid=(slots // per,), in_specs=[pl.BlockSpe...]
    unnamed x44 -> x33, local copies, waits for them, and re-layouts: 10.7 us -> 4.22 us
  transfers between devices with their start and end apart: 1 -> 2, of which waited for: 0 -> 1; matrix products, arithmetic and copies ran while one was open for 1% -> 2% of each run, Pallas kernels for 0% -> 0%
where the time goes in v2:
time: 198 us
  waiting for transfers between devices  114 us (58%)
  Pallas kernels  25.6 us (13%)
  matrix products  17.1 us (9%)
  between operations  14.6 us (7%)
  local copies, waits for them, and re-layouts  12.8 us (6%)
  starting transfers between devices  11.9 us (6%)
    all_gather x1, waiting for transfers between devices, body(): tags = lax.all_gather(tags, ('tx', 'ty'), tiled=True)  114 us
    conv_general_dilated x5, matrix products, conv(): lax.conv_general_dilated(field[None], kernel, (stride, stride), 'VALID',...  16.3 us
    all_to_all x1, starting transfers between devices, body(): lax.all_to_all(sent.reshape(tiles, CAP * BR, 128), ('tx', 'ty'), split_ax...  11.9 us
    pallas_call x1, Pallas kernels, level_one(): pl.pallas_call(level_one_kernel, grid=(steps,), in_specs=[pl.BlockSpec(me...  7.72 us
    pallas_call x1, Pallas kernels, resample(): pl.pallas_call(resample_kernel, grid=(held // per,), in_specs=[pl.BlockSp...  6.35 us
    pallas_call x1, Pallas kernels, widen(): pl.pallas_call(widen_kernel, in_specs=[pl.BlockSpec(memory_space=pltpu.VM...  5.81 us
    pallas_call x1, Pallas kernels, gather_windows(): pl.pallas_call(gather_kernel, grid=(slots // per,), in_specs=[pl.BlockSpe...  5.74 us
    unnamed x33, local copies, waits for them, and re-layouts  4.22 us
  transfers between devices with their start and end apart: 2, of which 1 were waited for; matrix products, arithmetic and copies ran while one was open for 2% of the time, Pallas kernels for 0%

profile of v2, /device:TPU:1, one launch (start us, length us, event | category | flops | bytes accessed | tf_op | source)
XLA Modules:
  0.0 197.8 jit_solution(2265165291091687449)
XLA Ops:
  7.2 1.6 copy.38
  8.8 6.4 %resample.1 = bf16[256,104,128]{2,1,0:T(8,128)(2,1)} custom-call(s32[64]{0:T(128)} %dest.1, s32[64]{0:T(128)} %bank_index.1, bf16[64,13,16,128]{3,2,1,0:T(8,128)(2,1)} %raw.1, bf16[512,16]{1,0:T(8,128)(2,1)} %bitcast.95, bf16[8,128,128]{2,1,0:T(8,128)(2,1)} %bank.1), custom_call_target="tpu_custom_call" | custom-call | tf_op jit(solution)/shard_map/resample/pallas_call | solution.py:73
  15.2 11.9 %all-to-all-start = ((bf16[128,208,128]{2,1,0:T(8,128)(2,1)}), bf16[128,208,128]{2,1,0:T(8,128)(2,1)}, u32[]{:S(2)}, u32[]{:S(2)}) async-start(bf16[128,208,128]{2,1,0:T(8,128)(2,1)} %bitcast.86), calls=%async_computation | async-start | bytes 13631488 | tf_op jit(solution)/shard_map/all_to_all | solution.py:393
  27.2 0.6 pad.8
  28.1 0.6 convolution_bitcast_fusion
  28.7 0.9 copy.41
  29.7 0.5 reshape.231
  30.6 114.0 %all-gather.2.cloned.1.call-done = s32[2048,128]{1,0:T(8,128)} async-done(((s32[16,128]{1,0:T(8,128)}), s32[2048,128]{1,0:T(8,128)}) %all-gather.2.cloned.1.call-update) | async-done | bytes 1048592 | tf_op jit(solution)/shard_map/all_gather | solution.py:391
  144.6 1.1 slice.16
  146.3 5.7 %gather_windows.1 = (bf16[13,256,128]{2,1,0:T(8,128)(2,1)}, bf16[32,128,128]{2,1,0:T(8,128)(2,1)S(1)}) custom-call(s32[256]{0:T(256)S(1)} %reshape.227.window, f32[32,128]{1,0:T(8,128)S(1)} %broadcast_in_dim.38.inverse, bf16[256,104,128]{2,1,0:T(8,128)(2,1)} %bitcast.9.got), custom_call_target="tpu_custom_call" | custom-call | tf_op jit(solution)/shard_map/gather_windows/pallas_call | solution.py:131
  152.3 5.8 %widen.1.wide = bf16[36,160,128]{2,1,0:T(8,128)(2,1)S(1)} custom-call(bf16[32,128,128]{2,1,0:T(8,128)(2,1)S(1)} %broadcast_in_dim.60.zeros, bf16[32,128,128]{2,1,0:T(8,128)(2,1)S(1)} %get-tuple-element.5.tile), custom_call_target="tpu_custom_call" | custom-call | tf_op jit(solution)/shard_map/widen/pallas_call | solution.py:246
  158.1 7.7 %level_one.1 = bf16[144,80,128]{2,1,0:T(8,128)(2,1)S(1)} custom-call(s32[4]{0:T(128)S(1)} %pad_add_fusion.1.limits, bf16[36,160,128]{2,1,0:T(8,128)(2,1)S(1)} %widen.1.wide, bf16[512,512]{1,0:T(8,128)(2,1)S(1)} %bitcast.84, bf16[256,128]{1,0:T(8,128)(2,1)S(1)} %bitcast.85), custom_call_target="tpu_custom_call" | custom-call | tf_op jit(solution)/shard_map/level_one/pallas_call | solution.py:308
  165.9 0.5 slice_bitcast_fusion
  166.4 0.7 copy.61
  167.1 0.2 pad.10.clone
  167.4 1.1 copy.44
  168.7 7.1 %fusion.19 = bf16[140,1,8,10,128]{4,2,3,0,1:T(8,128)(2,1)S(1)} fusion(pred[8,10]{0,1:T(8,128)(4,1)S(1)} %copy-done.10, bf16[3,3,128,128]{3,2,1,0:T(8,128)(2,1)S(1)} %copy-done.7, bf16[142,1,7,2,128]{4,2,3,0,1:T(8,128)(2,1)S(1)} %slice.18, bf16[142,1,8,10,128]{4,2,3,0,1:T(8,128)(2,1)S(1)} %copy.44), kind=kOutput, calls=%fused_computation.23 | convolution fusion | flops 3319218176 | bytes 6579280 | tf_op jit(solution)/shard_map/conv_general_dilated | solution.py:348
  175.9 0.9 fusion.36
  176.8 0.3 copy.45
  177.1 0.8 fusion.20
  178.0 0.3 copy.47
  178.6 3.4 %fusion.49 = bf16[68,8,5,256]{3,1,2,0:T(8,128)(2,1)S(1)} fusion(bf16[3,3,256,256]{3,2,1,0:T(8,128)(2,1)S(1)} %copy-done, bf16[70,1,7,2,256]{4,2,3,0,1:T(8,128)(2,1)S(1)} %slice.21, bf16[70,1,8,5,256]{4,2,3,0,1:T(8,128)(2,1)S(1)} %copy.47, pred[8,5]{0,1:T(8,128)(4,1)S(1)} %copy-done.11), kind=kOutput, calls=%fused_computation.48 | convolution fusion | flops 3217448960 | bytes 4507688 | tf_op jit(solution)/shard_map/conv_general_dilated | solution.py:348
  182.0 0.3 copy.48
  182.5 0.6 copy.50
  183.1 0.6 copy-done.6
  183.7 1.0 fusion.41
  184.7 0.3 copy.51
  185.0 0.2 fusion.44
  185.3 0.2 copy.53
  185.8 3.8 %maximum_convert_fusion.2 = bf16[32,8,3,512]{3,1,2,0:T(8,128)(2,1)S(1)} fusion(bf16[3,3,512,512]{3,2,1,0:T(8,128)(2,1)S(1)} %bitcast.99, bf16[34,1,7,2,512]{4,2,3,0,1:T(8,128)(2,1)S(1)} %slice.24, bf16[34,1,8,3,512]{4,2,3,0,1:T(8,128)(2,1)S(1)} %copy.53, pred[8,3]{0,1:T(4,128)(4,1)S(1)} %copy-done.12), kind=kOutput, calls=%fused_computation.44 | convolution fusion | flops 3629236224 | bytes 6828056 | tf_op jit(solution)/shard_map/conv_general_dilated | solution.py:348
  189.6 0.2 copy.54
  189.9 1.1 copy.55
  (62 shorter events, 2.6 us)
Async XLA Ops:
  7.2 171.3 %copy-start = (bf16[3,3,256,256]{3,2,1,0:T(8,128)(2,1)S(1)}, bf16[3,3,256,256]{3,2,1,0:T(8,128)(2,1)}, u32[]{:S(2)}) copy-start(bf16[3,3,256,256]{3,2,1,0:T(8,128)(2,1)} %param.25) | copy-start | bytes 3538948
  15.2 12.0 %copy-start.5 = (s32[64]{0:T(128)S(1)}, s32[64]{0:T(128)}, u32[]{:S(2)}) copy-start(s32[64]{0:T(128)} %dest.1) | copy-start | bytes 772
  15.2 12.0 %copy-start.9 = (s32[64]{0:T(128)S(1)}, s32[64]{0:T(128)}, u32[]{:S(2)}) copy-start(s32[64]{0:T(128)} %param.19) | copy-start | bytes 772
  15.2 12.7 %copy-start.2 = (bf16[3,3,13,64]{3,2,1,0:T(8,128)(2,1)S(1)}, bf16[3,3,13,64]{3,2,1,0:T(8,128)(2,1)}, u32[]{:S(2)}) copy-start(bf16[3,3,13,64]{3,2,1,0:T(8,128)(2,1)} %param.21) | copy-start | bytes 44932
  15.2 12.7 %copy-start.3 = (bf16[8,4,3,1,1]{2,1,4,3,0:T(4,128)(2,1)S(1)}, bf16[8,4,3,1,1]{2,1,4,3,0:T(4,128)(2,1)}, u32[]{:S(2)}) copy-start(bf16[8,4,3,1,1]{2,1,4,3,0:T(4,128)(2,1)} %constant.149) | copy-start | bytes 580
  15.2 12.9 %copy-start.4 = (bf16[4,2,3,1,1,1]{2,0,1,5,4,3:T(4,128)(2,1)S(1)}, bf16[4,2,3,1,1,1]{2,0,1,5,4,3:T(4,128)(2,1)}, u32[]{:S(2)}) copy-start(bf16[4,2,3,1,1,1]{2,0,1,5,4,3:T(4,128)(2,1)} %constant.150) | copy-start | bytes 148
  15.2 131.0 %all-to-all-start = ((bf16[128,208,128]{2,1,0:T(8,128)(2,1)}), bf16[128,208,128]{2,1,0:T(8,128)(2,1)}, u32[]{:S(2)}, u32[]{:S(2)}) async-start(bf16[128,208,128]{2,1,0:T(8,128)(2,1)} %bitcast.86), calls=%async_computation | async-start | bytes 13631488 | tf_op jit(solution)/shard_map/all_to_all | solution.py:393
  27.1 117.4 %all-gather.2.cloned.1.call-start = ((), (), s32[]{:S(2)}) async-start(), calls=%async_computation.1 | async-start | bytes 1056768 | tf_op jit(solution)/shard_map/all_gather | solution.py:391
  152.1 6.1 %copy-start.1 = (bf16[2,2,64,128]{3,2,1,0:T(8,128)(2,1)S(1)}, bf16[2,2,64,128]{3,2,1,0:T(8,128)(2,1)}, u32[]{:S(2)}) copy-start(bf16[2,2,64,128]{3,2,1,0:T(8,128)(2,1)} %param.22) | copy-start | bytes 196612
  167.4 1.3 copy-start.7
  167.4 1.3 copy-start.10
  168.7 7.2 %copy-start.8 = (bf16[2,2,128,256]{3,2,1,0:T(8,128)(2,1)S(1)}, bf16[2,2,128,256]{3,2,1,0:T(8,128)(2,1)}, u32[]{:S(2)}) copy-start(bf16[2,2,128,256]{3,2,1,0:T(8,128)(2,1)} %param.24) | copy-start | bytes 786436
  177.9 0.7 copy-start.11
  182.5 1.2 copy-start.6
  182.5 3.3 %slice-start = ((s8[4718592]{0:T(1024)(128)(4,1)}), s8[4194304]{0:T(1024)(128)(4,1)S(1)}, s32[]{:S(2)}) async-start(s8[4718592]{0:T(1024)(128)(4,1)} %bitcast.98), calls=%async_computation.2 | async-start | bytes 8388608
  183.7 2.1 %slice-start.1 = ((s8[4718592]{0:T(1024)(128)(4,1)}), s8[524288]{0:T(1024)(128)(4,1)S(1)}, s32[]{:S(2)}) async-start(s8[4718592]{0:T(1024)(128)(4,1)} %bitcast.98), calls=%async_computation.3 | async-start | bytes 1048576
  185.0 0.8 copy-start.12
Sparse Core Ops, SparseCore 0:
  31.3 113.2 all-gather.1

commit v3 on v2

--- a/solution.py
+++ b/solution.py
@@ -18,10 +18,13 @@
 BIG_VMEM = 56 << 20
 
 
-def resample_kernel(dest, bank_index, raw, weights, bank, out, tiled, res, count, sem):
+def resample_kernel(
+    dest, window, bank_index, raw, weights, bank, out, tiled, res, tags, tags_out, count, sem, tag_sem
+):
     step = pl.program_id(0)
     per = raw.shape[0]
     held = res.shape[0]
+    tiles = out.shape[0]
     lanes = BANDS * 16
 
     @pl.when(step == 0)
@@ -31,8 +34,24 @@
             == lax.broadcasted_iota(jnp.int32, (16, lanes), 0)
         ).astype(jnp.bfloat16)
         tiled[...] = jnp.dot(weights[...], spread, preferred_element_type=jnp.float32)
-
-        @pl.loop(0, count.shape[0])
+        tags[...] = jnp.full_like(tags, float(NWIN))
+
+        @pl.loop(0, tiles)
+        def _(t):
+            count[t] = 0
+
+        @pl.loop(0, held)
+        def _(n):
+            tile = dest[n]
+            tags[tile, pl.ds(count[tile], 1), :] = jnp.full((1, 128), window[n], jnp.int32).astype(
+                jnp.float32
+            )
+            count[tile] = count[tile] + 1
+
+        tags_out[...] = tags[...].astype(jnp.bfloat16)
+        pltpu.make_async_copy(tags_out, out.at[:, pl.ds(CAP * BR, 8)], tag_sem).start()
+
+        @pl.loop(0, tiles)
         def _(t):
             count[t] = 0
 
@@ -60,14 +79,17 @@
         tile = dest[n]
         rank = count[tile]
         count[tile] = rank + 1
-        pltpu.make_async_copy(res.at[n], out.at[tile * CAP + rank], sem).start()
+        pltpu.make_async_copy(
+            res.at[n], out.at[tile, pl.ds(pl.multiple_of(rank * BR, 8), BR)], sem
+        ).start()
 
     @pl.when(step == pl.num_programs(0) - 1)
     def _():
-        pltpu.make_async_copy(res, out.at[pl.ds(0, held)], sem).wait()
-
-
-def resample(raw, weights, bank, dest, bank_index, tiles):
+        pltpu.make_async_copy(res, res, sem).wait()
+        pltpu.make_async_copy(tags_out, out.at[:, pl.ds(CAP * BR, 8)], tag_sem).wait()
+
+
+def resample(raw, weights, bank, dest, window, bank_index, tiles):
     held = raw.shape[0]
     per = 16
     return pl.pallas_call(
@@ -76,38 +98,64 @@
         in_specs=[
             pl.BlockSpec(memory_space=pltpu.SMEM),
             pl.BlockSpec(memory_space=pltpu.SMEM),
+            pl.BlockSpec(memory_space=pltpu.SMEM),
             pl.BlockSpec((per, BANDS, 16, 128), lambda i: (i, 0, 0, 0)),
             pl.BlockSpec((held * WIN, 16), lambda i: (0, 0)),
             pl.BlockSpec(bank.shape, lambda i: (0, 0, 0)),
         ],
         out_specs=pl.BlockSpec(memory_space=pltpu.HBM),
-        out_shape=jax.ShapeDtypeStruct((tiles * CAP, BR, 128), jnp.bfloat16),
+        out_shape=jax.ShapeDtypeStruct((tiles, CAP * BR + 8, 128), jnp.bfloat16),
         scratch_shapes=[
             pltpu.VMEM((held * WIN, BANDS * 16), jnp.float32),
             pltpu.VMEM((held, BR, 128), jnp.bfloat16),
+            pltpu.VMEM((tiles, 8, 128), jnp.float32),
+            pltpu.VMEM((tiles, 8, 128), jnp.bfloat16),
             pltpu.SMEM((tiles,), jnp.int32),
             pltpu.SemaphoreType.DMA,
+            pltpu.SemaphoreType.DMA,
         ],
         compiler_params=pltpu.CompilerParams(vmem_limit_bytes=BIG_VMEM),
         name="resample",
-    )(dest, bank_index, raw, weights.reshape(held * WIN, 16), bank)
-
-
-def gather_kernel(window, inverse, got, gridded, turned, even, odd):
+    )(dest, window, bank_index, raw, weights.reshape(held * WIN, 16), bank)
+
+
+def gather_kernel(
+    got, all_got, gridded, turned, even, odd, tags, dense, window, inverse, sem, tag_sem
+):
     step = pl.program_id(0)
     per = got.shape[0]
+    tiles = all_got.shape[0]
 
     @pl.when(step == 0)
     def _():
+        fetch = pltpu.make_async_copy(all_got.at[:, pl.ds(CAP * BR, 8)], tags, tag_sem)
+        fetch.start()
         even[...] = jnp.zeros_like(even)
         odd[...] = jnp.zeros_like(odd)
-
-    @pl.loop(0, per // 8)
+        fetch.wait()
+        lane = lax.broadcasted_iota(jnp.int32, (8, 128), 1)
+        total = jnp.zeros((8, 128), jnp.float32)
+        for t in range(tiles):
+            total = total + jnp.where(lane == t, tags[t].astype(jnp.float32), 0.0)
+        dense[...] = total.astype(jnp.int32)
+        scalars = pltpu.make_async_copy(dense, window, sem)
+        scalars.start()
+        which = lax.broadcasted_iota(jnp.int32, (NWIN, 128), 0).astype(jnp.float32)
+        hits = jnp.zeros((NWIN, 128), jnp.float32)
+        for k in range(CAP):
+            hits = hits + jnp.where(which == total[k : k + 1, :], 1.0, 0.0)
+        counts = jnp.sum(hits, axis=1, keepdims=True)
+        inverse[...] = jnp.broadcast_to(1.0 / jnp.maximum(counts, 1.0), (NWIN, 128))
+        scalars.wait()
+
+    @pl.loop(0, per // 4)
     def _(group):
-        for u in range(8):
-            k = group * 8 + u
-            total = odd if u % 2 else even
-            total[window[step * per + k]] += got[k].astype(jnp.float32)
+        for u in range(4):
+            t = group * 4 + u
+            for k, total in ((0, even), (1, odd)):
+                total[window[k, step * per + t]] += got[t, k * BR : (k + 1) * BR, :].astype(
+                    jnp.float32
+                )
 
     @pl.when(step == pl.num_programs(0) - 1)
     def _():
@@ -125,16 +173,15 @@
                 ).astype(jnp.bfloat16)
 
 
-def gather_windows(got, window, inverse):
-    slots = got.shape[0]
-    per = 64
+def gather_windows(got):
+    tiles, rows, _ = got.shape
+    per = 32
     return pl.pallas_call(
         gather_kernel,
-        grid=(slots // per,),
+        grid=(tiles // per,),
         in_specs=[
-            pl.BlockSpec(memory_space=pltpu.SMEM),
-            pl.BlockSpec((NWIN, 128), lambda i: (0, 0)),
-            pl.BlockSpec((per, BR, 128), lambda i: (i, 0, 0)),
+            pl.BlockSpec((per, rows, 128), lambda i: (i, 0, 0)),
+            pl.BlockSpec(memory_space=pl.ANY),
         ],
         out_specs=[
             pl.BlockSpec((BANDS, NWIN * WIN, 128), lambda i: (0, 0, 0)),
@@ -144,10 +191,19 @@
             jax.ShapeDtypeStruct((BANDS, NWIN * WIN, 128), jnp.bfloat16),
             jax.ShapeDtypeStruct((NWIN, 128, 128), jnp.bfloat16),
         ],
-        scratch_shapes=[pltpu.VMEM((NWIN + 1, BR, 128), jnp.float32)] * 2,
+        scratch_shapes=[
+            pltpu.VMEM((NWIN + 1, BR, 128), jnp.float32),
+            pltpu.VMEM((NWIN + 1, BR, 128), jnp.float32),
+            pltpu.VMEM((tiles, 8, 128), jnp.bfloat16),
+            pltpu.VMEM((8, 128), jnp.int32),
+            pltpu.SMEM((8, 128), jnp.int32),
+            pltpu.VMEM((NWIN, 128), jnp.float32),
+            pltpu.SemaphoreType.DMA,
+            pltpu.SemaphoreType.DMA,
+        ],
         compiler_params=pltpu.CompilerParams(vmem_limit_bytes=32 << 20),
         name="gather_windows",
-    )(window, inverse, got)
+    )(got, got)
 
 
 HALO_WIN = HALO // WIN
@@ -386,33 +442,11 @@
     nx, ny = lax.axis_size("tx"), lax.axis_size("ty")
     tx, ty = lax.axis_index("tx"), lax.axis_index("ty")
     tiles = nx * ny
-    held = destination.shape[0]
-    tags = jnp.pad((destination * NWIN + window_index)[None, :], ((0, 15), (0, 128 - held)))
-    tags = lax.all_gather(tags, ("tx", "ty"), tiled=True)
-    sent = resample(granule_blocks, row_weights, column_bank, destination, bank_index, tiles)
-    got = lax.all_to_all(
-        sent.reshape(tiles, CAP * BR, 128), ("tx", "ty"), split_axis=0, concat_axis=0, tiled=True
-    ).reshape(tiles * CAP, BR, 128)
-    tags = tags.reshape(tiles, 16, 128)[:, 0, :held]
-    mine = tags // NWIN == tx * ny + ty
-    code = jnp.arange(held, dtype=jnp.int32)[None, :] * NWIN + tags % NWIN
-    hits = jnp.sum(mine.astype(jnp.int32), axis=1)
-    first = jnp.min(jnp.where(mine, code, held * NWIN), axis=1)
-    second = jnp.max(jnp.where(mine, code, -1), axis=1)
-    window = jnp.stack(
-        [
-            jnp.where(hits >= 1, first % NWIN, NWIN),
-            jnp.where(hits >= 2, second % NWIN, NWIN),
-        ],
-        axis=1,
-    ).reshape(tiles * CAP)
-    counts = jnp.sum(
-        (window[None, :] == jnp.arange(NWIN, dtype=jnp.int32)[:, None]).astype(jnp.int32), axis=1
-    )
-    inverse = jnp.broadcast_to(
-        (1.0 / jnp.maximum(counts, 1).astype(jnp.float32))[:, None], (NWIN, 128)
-    )
-    gridded, turned = gather_windows(got, window, inverse)
+    sent = resample(
+        granule_blocks, row_weights, column_bank, destination, window_index, bank_index, tiles
+    )
+    got = lax.all_to_all(sent, ("tx", "ty"), split_axis=0, concat_axis=0, tiled=True)
+    gridded, turned = gather_windows(got)
     wide = widen(turned)
     far = 1 << 20
     limits = jnp.stack(

time: 198 us -> 158 us (0.80)
  waiting for transfers between devices: 114 us -> 84 us
  between operations: 14.6 us -> 1.17 us
  Pallas kernels: 25.6 us -> 31.2 us
  local copies, waits for them, and re-layouts: 12.8 us -> 10.8 us
    all_gather x1 -> x0, waiting for transfers between devices: 114 us -> none  [body(): tags = lax.all_gather(tags, ('tx', 'ty'), tiled=True)]
    all_to_all x1, waiting for transfers between devices: 0.01 us -> 84 us  [body(): lax.all_to_all(sent, ('tx', 'ty'), split_axis=0, concat_axis=0, tiled=True)]
    pallas_call x1, Pallas kernels: 5.81 us -> 8.34 us  [widen(): pl.pallas_call(widen_kernel, in_specs=[pl.BlockSpec(memory_space=pltpu.VM...]
    unnamed x33 -> x29, local copies, waits for them, and re-layouts: 4.22 us -> 4.21 us
  transfers between devices with their start and end apart: 2 -> 1, of which waited for: 1 -> 1; matrix products, arithmetic and copies ran while one was open for 2% -> 2% of each run, Pallas kernels for 0% -> 0%
where the time goes in v3:
time: 158 us; the launch traced here: 157 us
  waiting for transfers between devices  84 us (53%)
  Pallas kernels  31.2 us (20%)
  matrix products  17.1 us (11%)
  starting transfers between devices  11.9 us (8%)
  local copies, waits for them, and re-layouts  10.8 us (7%)
    all_to_all x1, waiting for transfers between devices, body(): lax.all_to_all(sent, ('tx', 'ty'), split_axis=0, concat_axis=0, tiled=True)  84 us
    conv_general_dilated x5, matrix products, conv(): lax.conv_general_dilated(field[None], kernel, (stride, stride), 'VALID',...  16.3 us
    all_to_all x1, starting transfers between devices, body(): lax.all_to_all(sent, ('tx', 'ty'), split_axis=0, concat_axis=0, tiled=True)  11.9 us
    pallas_call x1, Pallas kernels, widen(): pl.pallas_call(widen_kernel, in_specs=[pl.BlockSpec(memory_space=pltpu.VM...  8.34 us
    pallas_call x1, Pallas kernels, resample(): pl.pallas_call(resample_kernel, grid=(held // per,), in_specs=[pl.BlockSp...  7.74 us
    pallas_call x1, Pallas kernels, level_one(): pl.pallas_call(level_one_kernel, grid=(steps,), in_specs=[pl.BlockSpec(me...  7.72 us
    pallas_call x1, Pallas kernels, gather_windows(): pl.pallas_call(gather_kernel, grid=(tiles // per,), in_specs=[pl.BlockSpe...  7.38 us
    unnamed x29, local copies, waits for them, and re-layouts  4.21 us
  transfers between devices with their start and end apart: 1, of which 1 were waited for; matrix products, arithmetic and copies ran while one was open for 2% of the time, Pallas kernels for 0%

profile of v3, /device:TPU:1, one launch (start us, length us, event | category | flops | bytes accessed | tf_op | source)
XLA Modules:
  0.0 157.5 jit_solution(1581469560095325128)
XLA Ops:
  0.6 1.6 %copy.20 = bf16[64,8,16]{2,1,0:T(8,128)(2,1)} copy(bf16[64,8,16]{0,2,1:T(8,128)(2,1)} %param.16) | data formatting | bytes 32768 | tf_op args[1]
  2.3 7.7 %resample.1 = bf16[128,216,128]{2,1,0:T(8,128)(2,1)} custom-call(s32[64]{0:T(128)} %dest.1, s32[64]{0:T(128)} %window.1, s32[64]{0:T(128)} %bank_index.1, bf16[64,13,16,128]{3,2,1,0:T(8,128)(2,1)} %raw.1, bf16[512,16]{1,0:T(8,128)(2,1)} %bitcast.81, bf16[8,128,128]{2,1,0:T(8,128)(2,1)} %bank.1), custom_call_target="tpu_custom_call" | custom-call | tf_op jit(solution)/shard_map/resample/pallas_call | solution.py:95
  10.1 11.9 %all-to-all-start = ((bf16[128,216,128]{2,1,0:T(8,128)(2,1)}), bf16[128,216,128]{2,1,0:T(8,128)(2,1)}, u32[]{:S(2)}, u32[]{:S(2)}) async-start(bf16[128,216,128]{2,1,0:T(8,128)(2,1)} %resample.1), calls=%async_computation | async-start | bytes 14155776 | tf_op jit(solution)/shard_map/all_to_all | solution.py:448
  22.0 0.2 fusion.63
  22.3 0.6 convolution_bitcast_fusion
  22.8 0.9 copy.21
  23.8 0.5 reshape.106
  24.6 84.0 %all-to-all-done.got.all_got = bf16[128,216,128]{2,1,0:T(8,128)(2,1)} async-done(((bf16[128,216,128]{2,1,0:T(8,128)(2,1)}), bf16[128,216,128]{2,1,0:T(8,128)(2,1)}, u32[]{:S(2)}, u32[]{:S(2)}) %all-to-all-start) | async-done | bytes 7077920 | tf_op jit(solution)/shard_map/all_to_all | solution.py:448
  108.6 7.4 %gather_windows.1 = (bf16[13,256,128]{2,1,0:T(8,128)(2,1)}, bf16[32,128,128]{2,1,0:T(8,128)(2,1)S(1)}) custom-call(bf16[128,216,128]{2,1,0:T(8,128)(2,1)} %all-to-all-done.got.all_got, bf16[128,216,128]{2,1,0:T(8,128)(2,1)} %all-to-all-done.got.all_got), custom_call_target="tpu_custom_call" | custom-call | tf_op jit(solution)/shard_map/gather_windows/pallas_call | solution.py:179
  116.0 0.2 broadcast_in_dim.22.zeros
  116.3 8.3 %widen.1.wide = bf16[36,160,128]{2,1,0:T(8,128)(2,1)S(1)} custom-call(bf16[32,128,128]{2,1,0:T(8,128)(2,1)S(1)} %broadcast_in_dim.22.zeros, bf16[32,128,128]{2,1,0:T(8,128)(2,1)S(1)} %get-tuple-element.5.tile), custom_call_target="tpu_custom_call" | custom-call | tf_op jit(solution)/shard_map/widen/pallas_call | solution.py:302
  124.6 7.7 %level_one.1 = bf16[144,80,128]{2,1,0:T(8,128)(2,1)S(1)} custom-call(s32[4]{0:T(128)S(1)} %pad_add_fusion.limits, bf16[36,160,128]{2,1,0:T(8,128)(2,1)S(1)} %widen.1.wide, bf16[512,512]{1,0:T(8,128)(2,1)S(1)} %bitcast.71, bf16[256,128]{1,0:T(8,128)(2,1)S(1)} %bitcast.72), custom_call_target="tpu_custom_call" | custom-call | tf_op jit(solution)/shard_map/level_one/pallas_call | solution.py:364
  132.4 0.5 slice_bitcast_fusion
  132.9 0.7 copy.41
  133.6 0.2 pad.5.clone
  133.9 1.1 copy.24
  135.2 7.1 %fusion.19 = bf16[140,1,8,10,128]{4,2,3,0,1:T(8,128)(2,1)S(1)} fusion(pred[8,10]{0,1:T(8,128)(4,1)S(1)} %copy-done.8, bf16[3,3,128,128]{3,2,1,0:T(8,128)(2,1)S(1)} %copy-done.6, bf16[142,1,7,2,128]{4,2,3,0,1:T(8,128)(2,1)S(1)} %slice.13, bf16[142,1,8,10,128]{4,2,3,0,1:T(8,128)(2,1)S(1)} %copy.24), kind=kOutput, calls=%fused_computation.23 | convolution fusion | flops 3319218176 | bytes 6579280 | tf_op jit(solution)/shard_map/conv_general_dilated | solution.py:404
  142.4 0.9 fusion.36
  143.3 0.3 copy.25
  143.6 0.8 fusion.20
  144.5 0.3 copy.27
  145.1 3.4 %fusion.49 = bf16[68,8,5,256]{3,1,2,0:T(8,128)(2,1)S(1)} fusion(bf16[3,3,256,256]{3,2,1,0:T(8,128)(2,1)S(1)} %copy-done, bf16[70,1,7,2,256]{4,2,3,0,1:T(8,128)(2,1)S(1)} %slice.16, bf16[70,1,8,5,256]{4,2,3,0,1:T(8,128)(2,1)S(1)} %copy.27, pred[8,5]{0,1:T(8,128)(4,1)S(1)} %copy-done.9), kind=kOutput, calls=%fused_computation.48 | convolution fusion | flops 3217448960 | bytes 4507688 | tf_op jit(solution)/shard_map/conv_general_dilated | solution.py:404
  148.5 0.3 copy.28
  149.0 0.6 copy.30
  149.6 0.6 copy-done.5
  150.2 1.0 fusion.41
  151.2 0.3 copy.31
  151.5 0.2 fusion.44
  151.8 0.2 copy.33
  152.3 3.8 %maximum_convert_fusion.2 = bf16[32,8,3,512]{3,1,2,0:T(8,128)(2,1)S(1)} fusion(bf16[3,3,512,512]{3,2,1,0:T(8,128)(2,1)S(1)} %bitcast.84, bf16[34,1,7,2,512]{4,2,3,0,1:T(8,128)(2,1)S(1)} %slice.19, bf16[34,1,8,3,512]{4,2,3,0,1:T(8,128)(2,1)S(1)} %copy.33, pred[8,3]{0,1:T(4,128)(4,1)S(1)} %copy-done.10), kind=kOutput, calls=%fused_computation.44 | convolution fusion | flops 3629236224 | bytes 6828056 | tf_op jit(solution)/shard_map/conv_general_dilated | solution.py:404
  156.1 0.2 copy.34
  156.4 1.1 copy.35
  (43 shorter events, 1.4 us)
Async XLA Ops:
  0.6 144.4 %copy-start = (bf16[3,3,256,256]{3,2,1,0:T(8,128)(2,1)S(1)}, bf16[3,3,256,256]{3,2,1,0:T(8,128)(2,1)}, u32[]{:S(2)}) copy-start(bf16[3,3,256,256]{3,2,1,0:T(8,128)(2,1)} %param.25) | copy-start | bytes 3538948
  10.0 12.0 %copy-start.2 = (bf16[3,3,13,64]{3,2,1,0:T(8,128)(2,1)S(1)}, bf16[3,3,13,64]{3,2,1,0:T(8,128)(2,1)}, u32[]{:S(2)}) copy-start(bf16[3,3,13,64]{3,2,1,0:T(8,128)(2,1)} %param.21) | copy-start | bytes 44932
  10.0 12.0 %copy-start.3 = (bf16[8,4,3,1,1]{2,1,4,3,0:T(4,128)(2,1)S(1)}, bf16[8,4,3,1,1]{2,1,4,3,0:T(4,128)(2,1)}, u32[]{:S(2)}) copy-start(bf16[8,4,3,1,1]{2,1,4,3,0:T(4,128)(2,1)} %constant.95) | copy-start | bytes 580
  10.1 12.2 %copy-start.4 = (bf16[4,2,3,1,1,1]{2,0,1,5,4,3:T(4,128)(2,1)S(1)}, bf16[4,2,3,1,1,1]{2,0,1,5,4,3:T(4,128)(2,1)}, u32[]{:S(2)}) copy-start(bf16[4,2,3,1,1,1]{2,0,1,5,4,3:T(4,128)(2,1)} %constant.96) | copy-start | bytes 148
  10.1 98.6 %all-to-all-start = ((bf16[128,216,128]{2,1,0:T(8,128)(2,1)}), bf16[128,216,128]{2,1,0:T(8,128)(2,1)}, u32[]{:S(2)}, u32[]{:S(2)}) async-start(bf16[128,216,128]{2,1,0:T(8,128)(2,1)} %resample.1), calls=%async_computation | async-start | bytes 14155776 | tf_op jit(solution)/shard_map/all_to_all | solution.py:448
  116.0 8.6 %copy-start.1 = (bf16[2,2,64,128]{3,2,1,0:T(8,128)(2,1)S(1)}, bf16[2,2,64,128]{3,2,1,0:T(8,128)(2,1)}, u32[]{:S(2)}) copy-start(bf16[2,2,64,128]{3,2,1,0:T(8,128)(2,1)} %param.22) | copy-start | bytes 196612
  133.9 1.3 copy-start.6
  133.9 1.3 copy-start.8
  135.2 7.2 %copy-start.7 = (bf16[2,2,128,256]{3,2,1,0:T(8,128)(2,1)S(1)}, bf16[2,2,128,256]{3,2,1,0:T(8,128)(2,1)}, u32[]{:S(2)}) copy-start(bf16[2,2,128,256]{3,2,1,0:T(8,128)(2,1)} %param.24) | copy-start | bytes 786436
  144.4 0.7 copy-start.9
  149.0 1.2 copy-start.5
  149.0 3.3 %slice-start = ((s8[4718592]{0:T(1024)(128)(4,1)}), s8[4194304]{0:T(1024)(128)(4,1)S(1)}, s32[]{:S(2)}) async-start(s8[4718592]{0:T(1024)(128)(4,1)} %bitcast.83), calls=%async_computation.1 | async-start | bytes 8388608
  150.2 2.1 %slice-start.1 = ((s8[4718592]{0:T(1024)(128)(4,1)}), s8[524288]{0:T(1024)(128)(4,1)S(1)}, s32[]{:S(2)}) async-start(s8[4718592]{0:T(1024)(128)(4,1)} %bitcast.83), calls=%async_computation.2 | async-start | bytes 1048576
  151.5 0.8 copy-start.10

commit v4 on v3

--- a/solution.py
+++ b/solution.py
@@ -319,66 +319,240 @@
     )(jnp.zeros((NWIN, 128, 128), jnp.bfloat16), turned)
 
 
+FAR = 1 << 20
 HALVES = 8
-PIX = 80
-
-
-def level_one_kernel(limits, wide, weight_one, weight_two, out, slab, patch):
-    step = pl.program_id(0)
+STEPS_ONE = 9
+PAIRS = 40
+PIX = 2 * PAIRS
+ROWS_TWO = STEPS_ONE * HALVES
+ROWS_THREE = 10
+STEPS_THREE = 7
+ROWS_FOUR = 6
+STEPS_FOUR = 6
+WIDE_FOUR = 24
+
+
+def encoder_kernel(
+    edges,
+    wide,
+    weight_one,
+    reduce_two,
+    hbm_two,
+    hbm_reduce_three,
+    hbm_three,
+    hbm_reduce_four,
+    hbm_four,
+    out,
+    slab,
+    patch,
+    even_two,
+    odd_two,
+    carry_two,
+    even_three,
+    odd_three,
+    carry_three,
+    spread_three,
+    taps_four,
+    weight_two,
+    reduce_three,
+    weight_three,
+    reduce_four,
+    weight_four,
+    sems,
+):
+    fetches = [
+        pltpu.make_async_copy(source, target, sems.at[i])
+        for i, (source, target) in enumerate(
+            (
+                (hbm_two, weight_two),
+                (hbm_reduce_three, reduce_three),
+                (hbm_three, weight_three),
+                (hbm_reduce_four, reduce_four),
+                (hbm_four, weight_four),
+            )
+        )
+    ]
+    for fetch in fetches:
+        fetch.start()
+
+    def dot(a, b):
+        return jnp.dot(a, b, preferred_element_type=jnp.float32)
+
+    def bounds(tile_rows, tile_cols):
+        return (
+            jnp.where(edges[0] == 1, 0, -FAR),
+            jnp.where(edges[1] == 1, tile_rows, FAR),
+            jnp.where(edges[2] == 1, 0, -FAR),
+            jnp.where(edges[3] == 1, tile_cols, FAR),
+        )
+
+    def on_map(value, row, col, limits):
+        top, bottom, left, right = limits
+        right = jnp.where(jnp.logical_and(row >= top, row < bottom), right, -FAR)
+        return jnp.where(jnp.logical_and(col >= left, col < right), value, 0.0)
+
+    def following(value, by):
+        return pltpu.roll(value, value.shape[0] - by, 0)
+
     last = wide.shape[0] - 1
     cols = wide.shape[1]
     low = lax.broadcasted_iota(jnp.int32, (cols, 128), 1) % 8 < 4
-    for k in range(HALVES):
-        w = step * (HALVES // 2) + k // 2
-        here = wide[jnp.minimum(w, last)].astype(jnp.float32)
-        if k % 2:
-            after = wide[jnp.minimum(w + 1, last)].astype(jnp.float32)
-            here = jnp.where(low, pltpu.roll(here, 124, 1), pltpu.roll(after, 4, 1))
-        slab[k, pl.ds(0, cols), :] = here
-        for q in range(4):
-            patch[k, :, q * 128 : (q + 1) * 128] = slab[
-                k, pl.ds(1 + q, PIX, stride=2), :
-            ].astype(jnp.bfloat16)
-    hidden = jnp.dot(
-        patch[...].reshape(HALVES * PIX, 512), weight_one[...], preferred_element_type=jnp.float32
-    )
-    hidden = jnp.maximum(hidden, 0.0).astype(jnp.bfloat16)
-    col = lax.broadcasted_iota(jnp.int32, (PIX, 128), 0) - 7
-    col_ok = jnp.logical_and(col >= limits[2], col < limits[3])
-    for e in range(2):
-        down = jnp.dot(
-            hidden[:, e * 256 : (e + 1) * 256],
-            weight_two[...],
-            preferred_element_type=jnp.float32,
-        )
-        down = jnp.maximum(down, 0.0).reshape(HALVES, PIX, 128)
+    at = lax.broadcasted_iota(jnp.int32, (PIX, 128), 0)
+    col_two = jnp.where(at < PAIRS, 2 * at, 2 * (at - PAIRS) + 1) - 7
+    limits_two = bounds(128, 64)
+    carry_two[...] = jnp.zeros_like(carry_two)
+
+    @pl.loop(0, STEPS_ONE)
+    def _(step):
         for k in range(HALVES):
-            row = (step * HALVES + k) * 2 + e - 7
-            row_ok = jnp.logical_and(row >= limits[0], row < limits[1])
-            keep = jnp.logical_and(col_ok, row_ok)
-            out[k * 2 + e] = jnp.where(keep, down[k], 0.0).astype(jnp.bfloat16)
-
-
-def level_one(wide, weight_one, weight_two, limits):
-    steps = 9
+            w = step * (HALVES // 2) + k // 2
+            here = wide[jnp.minimum(w, last)].astype(jnp.float32)
+            if k % 2:
+                after = wide[jnp.minimum(w + 1, last)].astype(jnp.float32)
+                here = jnp.where(low, pltpu.roll(here, 124, 1), pltpu.roll(after, 4, 1))
+            slab[k, pl.ds(0, cols), :] = here
+            for q in range(4):
+                both = [slab[k, pl.ds(first + q, PAIRS, stride=4), :] for first in (1, 3)]
+                patch[k, :, q * 128 : (q + 1) * 128] = jnp.concatenate(both, axis=0).astype(
+                    jnp.bfloat16
+                )
+        hidden = dot(patch[...].reshape(HALVES * PIX, 512), weight_one[...])
+        hidden = jnp.maximum(hidden, 0.0).astype(jnp.bfloat16)
+        down = [
+            jnp.maximum(dot(hidden[:, e * 256 : (e + 1) * 256], reduce_two[...]), 0.0).reshape(
+                HALVES, PIX, 128
+            )
+            for e in range(2)
+        ]
+        before = carry_two[...]
+        for k in range(HALVES):
+            h = step * HALVES + k
+            lines = []
+            for e in range(2):
+                value = on_map(down[e][k], 2 * h + e - 7, col_two, limits_two)
+                first, second = value[:PAIRS], value[PAIRS:]
+                lines.append(
+                    jnp.concatenate(
+                        [first, second, following(first, 1), following(second, 1)], axis=1
+                    )
+                )
+            even_two[h] = jnp.concatenate(lines, axis=0).astype(jnp.bfloat16)
+            odd_two[h] = jnp.concatenate([before, lines[0]], axis=0).astype(jnp.bfloat16)
+            before = lines[1]
+        carry_two[...] = before
+
+    fetches[0].wait()
+    fetches[1].wait()
+    col_three = lax.broadcasted_iota(jnp.int32, (PAIRS, 256), 0) - 3
+    limits_three = bounds(64, 32)
+    carry_three[...] = jnp.zeros_like(carry_three)
+    size = ROWS_THREE * PIX
+
+    @pl.loop(0, STEPS_THREE)
+    def _(step):
+        first = step * ROWS_THREE
+        hidden = (
+            dot(even_two[pl.ds(first, ROWS_THREE)].reshape(size, 512), weight_two[0])
+            + dot(odd_two[pl.ds(first + 1, ROWS_THREE)].reshape(size, 512), weight_two[1])
+            + dot(even_two[pl.ds(first + 1, ROWS_THREE)].reshape(size, 512), weight_two[2])
+        )
+        hidden = jnp.maximum(hidden, 0.0).reshape(ROWS_THREE, 2, PAIRS, 256)
+        hidden = jnp.concatenate([hidden[:, 0], hidden[:, 1]], axis=-1)
+        hidden = hidden.reshape(ROWS_THREE * PAIRS, 512).astype(jnp.bfloat16)
+        down = jnp.maximum(dot(hidden, reduce_three[...]), 0.0).reshape(ROWS_THREE, PAIRS, 256)
+        before = carry_three[...]
+        for k in range(0, ROWS_THREE, 2):
+            lines = []
+            for e in range(2):
+                value = on_map(down[k + e], first + k + e - 3, col_three, limits_three)
+                lines.append(
+                    jnp.concatenate([value, following(value, 1), following(value, 2)], axis=1)
+                )
+            i = step * (ROWS_THREE // 2) + k // 2
+            even_three[i] = jnp.concatenate(lines, axis=0).astype(jnp.bfloat16)
+            odd_three[i] = jnp.concatenate([before, lines[0]], axis=0).astype(jnp.bfloat16)
+            before = lines[1]
+        carry_three[...] = before
+
+    fetches[2].wait()
+    fetches[3].wait()
+    col_four = lax.broadcasted_iota(jnp.int32, (WIDE_FOUR, 512), 0) - 1
+    limits_four = bounds(32, 16)
+    size_four = ROWS_FOUR * PIX
+
+    @pl.loop(0, STEPS_FOUR)
+    def _(step):
+        first = step * ROWS_FOUR
+        hidden = (
+            dot(even_three[pl.ds(first, ROWS_FOUR)].reshape(size_four, 768), weight_three[0])
+            + dot(odd_three[pl.ds(first + 1, ROWS_FOUR)].reshape(size_four, 768), weight_three[1])
+            + dot(even_three[pl.ds(first + 1, ROWS_FOUR)].reshape(size_four, 768), weight_three[2])
+        )
+        hidden = jnp.maximum(hidden, 0.0)
+        for half in range(2):
+            spread_three[half, pl.ds(0, size_four), :] = hidden[:, half * 128 : (half + 1) * 128]
+        rows = []
+        for k in range(ROWS_FOUR):
+            rows.append(
+                jnp.concatenate(
+                    [
+                        spread_three[
+                            half,
+                            pl.ds(k * PIX + e * PAIRS + g, WIDE_FOUR, stride=2),
+                            :,
+                        ]
+                        for e in range(2)
+                        for g in range(2)
+                        for half in range(2)
+                    ],
+                    axis=1,
+                )
+            )
+        hidden = jnp.concatenate(rows, axis=0).astype(jnp.bfloat16)
+        down = jnp.maximum(dot(hidden, reduce_four[...]), 0.0)
+        for k in range(ROWS_FOUR):
+            value = down[k * WIDE_FOUR : (k + 1) * WIDE_FOUR]
+            value = on_map(value, first + k - 1, col_four, limits_four)
+            taps_four[first + k] = jnp.concatenate(
+                [value[:16], following(value, 1)[:16], following(value, 2)[:16]], axis=1
+            ).astype(jnp.bfloat16)
+
+    fetches[4].wait()
+    for half in range(2):
+        lanes = slice(half * 256, (half + 1) * 256)
+        hidden = sum(
+            dot(taps_four[u : u + 32].reshape(512, 1536), weight_four[u, :, lanes])
+            for u in range(3)
+        )
+        out[:, lanes] = jnp.maximum(hidden, 0.0).astype(jnp.bfloat16)
+
+
+def encode(wide, edges, one, two, reduce_three, three, reduce_four, four, reduce_two):
+    hbm = pl.BlockSpec(memory_space=pltpu.HBM)
+    vmem = pl.BlockSpec(memory_space=pltpu.VMEM)
+    big = (two, reduce_three, three, reduce_four, four)
     return pl.pallas_call(
-        level_one_kernel,
-        grid=(steps,),
-        in_specs=[
-            pl.BlockSpec(memory_space=pltpu.SMEM),
-            pl.BlockSpec(wide.shape, lambda i: (0, 0, 0)),
-            pl.BlockSpec(weight_one.shape, lambda i: (0, 0)),
-            pl.BlockSpec(weight_two.shape, lambda i: (0, 0)),
-        ],
-        out_specs=pl.BlockSpec((2 * HALVES, PIX, 128), lambda i: (i, 0, 0)),
-        out_shape=jax.ShapeDtypeStruct((steps * 2 * HALVES, PIX, 128), jnp.bfloat16),
+        encoder_kernel,
+        in_specs=[pl.BlockSpec(memory_space=pltpu.SMEM), vmem, vmem, vmem] + [hbm] * len(big),
+        out_specs=vmem,
+        out_shape=jax.ShapeDtypeStruct((512, 512), jnp.bfloat16),
         scratch_shapes=[
             pltpu.VMEM((HALVES, 168, 128), jnp.float32),
             pltpu.VMEM((HALVES, PIX, 512), jnp.bfloat16),
-        ],
-        compiler_params=pltpu.CompilerParams(vmem_limit_bytes=32 << 20),
-        name="level_one",
-    )(limits, wide, weight_one, weight_two)
+            pltpu.VMEM((ROWS_TWO, PIX, 512), jnp.bfloat16),
+            pltpu.VMEM((ROWS_TWO, PIX, 512), jnp.bfloat16),
+            pltpu.VMEM((PAIRS, 512), jnp.float32),
+            pltpu.VMEM((STEPS_FOUR * ROWS_FOUR + 1, PIX, 768), jnp.bfloat16),
+            pltpu.VMEM((STEPS_FOUR * ROWS_FOUR + 1, PIX, 768), jnp.bfloat16),
+            pltpu.VMEM((PAIRS, 768), jnp.float32),
+            pltpu.VMEM((2, ROWS_FOUR * PIX + 16, 128), jnp.float32),
+            pltpu.VMEM((STEPS_FOUR * ROWS_FOUR, 16, 1536), jnp.bfloat16),
+        ]
+        + [pltpu.VMEM(w.shape, jnp.bfloat16) for w in big]
+        + [pltpu.SemaphoreType.DMA((len(big),))],
+        compiler_params=pltpu.CompilerParams(vmem_limit_bytes=BIG_VMEM),
+        name="encoder",
+    )(edges, wide, one, reduce_two, *big)
 
 
 def patch_weights(kernel):
@@ -400,28 +574,11 @@
     return jnp.pad(spread, ((0, 0), (0, 128 - BR), (0, 0))).reshape(512, 512)
 
 
-def conv(field, kernel, stride):
-    out = lax.conv_general_dilated(
-        field[None],
-        kernel,
-        (stride, stride),
-        "VALID",
-        dimension_numbers=("NHWC", "HWIO", "NHWC"),
-        preferred_element_type=jnp.float32,
-    )[0]
-    return jnp.maximum(out, 0.0)
-
-
-def on_map(field, halo, tx, ty, nx, ny):
-    rows = jnp.arange(field.shape[0]) - halo
-    cols = jnp.arange(field.shape[1]) - halo
-    r = (rows + ty * (field.shape[0] - 2 * halo) >= 0) & (
-        rows + ty * (field.shape[0] - 2 * halo) < ny * (field.shape[0] - 2 * halo)
+def pair_weights(kernel):
+    taps = jnp.stack(
+        [jnp.pad(kernel, ((0, 0), (g, 1 - g), (0, 0), (0, 0))) for g in range(2)], axis=3
     )
-    c = (cols + tx * (field.shape[1] - 2 * halo) >= 0) & (
-        cols + tx * (field.shape[1] - 2 * halo) < nx * (field.shape[1] - 2 * halo)
-    )
-    return jnp.where((r[:, None] & c[None, :])[:, :, None], field, 0.0)
+    return taps.reshape(3, 512, 256)
 
 
 def body(
@@ -448,22 +605,19 @@
     got = lax.all_to_all(sent, ("tx", "ty"), split_axis=0, concat_axis=0, tiled=True)
     gridded, turned = gather_windows(got)
     wide = widen(turned)
-    far = 1 << 20
-    limits = jnp.stack(
-        [
-            jnp.where(ty == 0, 0, -far),
-            jnp.where(ty == ny - 1, 128, far),
-            jnp.where(tx == 0, 0, -far),
-            jnp.where(tx == nx - 1, 64, far),
-        ]
-    ).astype(jnp.int32)
-    down_two = level_one(wide, patch_weights(kernel_one), reduce_two.reshape(256, 128), limits)
-    level_two = conv(down_two[:142, :78], kernel_two, 1).astype(jnp.bfloat16)
-    down_three = on_map(conv(level_two, reduce_three, 2), 3, tx, ty, nx, ny).astype(jnp.bfloat16)
-    level_three = conv(down_three, kernel_three, 1).astype(jnp.bfloat16)
-    down_four = on_map(conv(level_three, reduce_four, 2), 1, tx, ty, nx, ny).astype(jnp.bfloat16)
-    bottleneck = conv(down_four, kernel_four, 1).astype(jnp.bfloat16)
-    return (gridded, jnp.transpose(bottleneck, (2, 0, 1)))
+    edges = jnp.stack([ty == 0, ty == ny - 1, tx == 0, tx == nx - 1]).astype(jnp.int32)
+    bottleneck = encode(
+        wide,
+        edges,
+        patch_weights(kernel_one),
+        pair_weights(kernel_two),
+        reduce_three.reshape(512, 256),
+        kernel_three.reshape(3, 768, 256),
+        reduce_four.reshape(1024, 512),
+        kernel_four.reshape(3, 1536, 512),
+        reduce_two.reshape(256, 128),
+    )
+    return (gridded, jnp.transpose(bottleneck.reshape(32, 16, 512), (2, 0, 1)))
 
 
 def solution(mesh):

time: 158 us -> 155 us (0.981)
  Pallas kernels: 31.2 us -> 51.6 us
  matrix products: 17.1 us -> 0.81 us
  waiting for transfers between devices: 84 us -> 80.5 us
  local copies, waits for them, and re-layouts: 10.8 us -> 7.56 us
    pallas_call x1, Pallas kernels: 7.72 us -> 28.2 us  [encode(): pl.pallas_call(encoder_kernel, in_specs=[pl.BlockSpec(memory_space=pltpu....]
    conv_general_dilated x5 -> x0, matrix products: 16.3 us -> none  [conv(): lax.conv_general_dilated(field[None], kernel, (stride, stride), 'VALID',...]
    all_to_all x1, waiting for transfers between devices: 84 us -> 80.5 us  [body(): lax.all_to_all(sent, ('tx', 'ty'), split_axis=0, concat_axis=0, tiled=True)]
    conv_general_dilated x6 -> x0, local copies, waits for them, and re-layouts: 2.08 us -> none  [conv(): lax.conv_general_dilated(field[None], kernel, (stride, stride), 'VALID',...]
    unnamed x29 -> x11, local copies, waits for them, and re-layouts: 4.21 us -> 2.7 us
  transfers between devices with their start and end apart: 1 -> 1, of which waited for: 1 -> 1; matrix products, arithmetic and copies ran while one was open for 2% -> 4% of each run, Pallas kernels for 0% -> 0%
where the time goes in v4:
time: 155 us; the launch traced here: 154 us
  waiting for transfers between devices  80.5 us (52%)
  Pallas kernels  51.6 us (33%)
  starting transfers between devices  11.9 us (8%)
  local copies, waits for them, and re-layouts  7.56 us (5%)
    all_to_all x1, waiting for transfers between devices, body(): lax.all_to_all(sent, ('tx', 'ty'), split_axis=0, concat_axis=0, tiled=True)  80.5 us
    pallas_call x1, Pallas kernels, encode(): pl.pallas_call(encoder_kernel, in_specs=[pl.BlockSpec(memory_space=pltpu....  28.2 us
    all_to_all x1, starting transfers between devices, body(): lax.all_to_all(sent, ('tx', 'ty'), split_axis=0, concat_axis=0, tiled=True)  11.9 us
    pallas_call x1, Pallas kernels, widen(): pl.pallas_call(widen_kernel, in_specs=[pl.BlockSpec(memory_space=pltpu.VM...  8.34 us
    pallas_call x1, Pallas kernels, resample(): pl.pallas_call(resample_kernel, grid=(held // per,), in_specs=[pl.BlockSp...  7.74 us
    pallas_call x1, Pallas kernels, gather_windows(): pl.pallas_call(gather_kernel, grid=(tiles // per,), in_specs=[pl.BlockSpe...  7.38 us
  transfers between devices with their start and end apart: 1, of which 1 were waited for; matrix products, arithmetic and copies ran while one was open for 4% of the time, Pallas kernels for 0%

profile of v4, /device:TPU:1, one launch (start us, length us, event | category | flops | bytes accessed | tf_op | source)
XLA Modules:
  0.0 153.8 jit_solution(9920665859487210334)
XLA Ops:
  0.6 0.0 copy-start
  0.6 1.5 %copy.19 = bf16[64,8,16]{2,1,0:T(8,128)(2,1)} copy(bf16[64,8,16]{0,2,1:T(8,128)(2,1)} %param.16) | data formatting | bytes 32768 | tf_op args[1]
  2.2 7.7 %resample.1 = bf16[128,216,128]{2,1,0:T(8,128)(2,1)} custom-call(s32[64]{0:T(128)} %dest.1, s32[64]{0:T(128)} %window.1, s32[64]{0:T(128)} %bank_index.1, bf16[64,13,16,128]{3,2,1,0:T(8,128)(2,1)} %raw.1, bf16[512,16]{1,0:T(8,128)(2,1)} %bitcast.41, bf16[8,128,128]{2,1,0:T(8,128)(2,1)} %bank.1), custom_call_target="tpu_custom_call" | custom-call | tf_op jit(solution)/shard_map/resample/pallas_call | solution.py:95
  9.9 0.0 copy-start.3
  9.9 0.0 copy-start.4
  10.0 11.9 %all-to-all-start = ((bf16[128,216,128]{2,1,0:T(8,128)(2,1)}), bf16[128,216,128]{2,1,0:T(8,128)(2,1)}, u32[]{:S(2)}, u32[]{:S(2)}) async-start(bf16[128,216,128]{2,1,0:T(8,128)(2,1)} %resample.1), calls=%async_computation | async-start | bytes 14155776 | tf_op jit(solution)/shard_map/all_to_all | solution.py:605
  21.9 0.0 copy-start.2
  21.9 0.0 copy-done
  21.9 0.0 copy-done.3
  21.9 0.2 fusion.2
  22.1 0.0 copy-done.4
  22.1 0.6 convolution_bitcast_fusion
  22.7 0.9 copy.20
  23.7 0.5 reshape.35
  24.2 0.0 copy-done.2
  24.2 0.1 pad_bitcast_fusion.1
  24.3 0.1 pad_maximum_fusion
  24.4 0.8 copy.21
  25.2 1.4 reshape.38.hbm_two
  26.7 0.8 pad.12
  27.5 0.6 add_convert_fusion.edges
  28.1 80.5 %all-to-all-done.got.all_got = bf16[128,216,128]{2,1,0:T(8,128)(2,1)} async-done(((bf16[128,216,128]{2,1,0:T(8,128)(2,1)}), bf16[128,216,128]{2,1,0:T(8,128)(2,1)}, u32[]{:S(2)}, u32[]{:S(2)}) %all-to-all-start) | async-done | bytes 7077920 | tf_op jit(solution)/shard_map/all_to_all | solution.py:605
  108.5 7.4 %gather_windows.1 = (bf16[13,256,128]{2,1,0:T(8,128)(2,1)}, bf16[32,128,128]{2,1,0:T(8,128)(2,1)S(1)}) custom-call(bf16[128,216,128]{2,1,0:T(8,128)(2,1)} %all-to-all-done.got.all_got, bf16[128,216,128]{2,1,0:T(8,128)(2,1)} %all-to-all-done.got.all_got), custom_call_target="tpu_custom_call" | custom-call | tf_op jit(solution)/shard_map/gather_windows/pallas_call | solution.py:179
  115.9 0.2 broadcast_in_dim.3.zeros
  116.2 8.3 %widen.1.wide = bf16[36,160,128]{2,1,0:T(8,128)(2,1)S(1)} custom-call(bf16[32,128,128]{2,1,0:T(8,128)(2,1)S(1)} %broadcast_in_dim.3.zeros, bf16[32,128,128]{2,1,0:T(8,128)(2,1)S(1)} %get-tuple-element.5.tile), custom_call_target="tpu_custom_call" | custom-call | tf_op jit(solution)/shard_map/widen/pallas_call | solution.py:302
  124.5 0.0 copy-start.1
  124.5 1.1 copy-done.1
  125.7 28.2 %encoder.1 = bf16[512,512]{1,0:T(8,128)(2,1)} custom-call(s32[4]{0:T(128)} %add_convert_fusion.edges, bf16[36,160,128]{2,1,0:T(8,128)(2,1)} %copy-done.1, bf16[512,512]{1,0:T(8,128)(2,1)} %bitcast.38, bf16[256,128]{1,0:T(8,128)(2,1)} %bitcast.44, bf16[3,512,256]{2,1,0:T(8,128)(2,1)} %reshape.38.hbm_two, bf16[512,256]{1,0:T(8,128)(2,1)} %bitcast.43, ...), custom_call_target="tpu_custom_call" | custom-call | tf_op jit(solution)/shard_map/encoder/pallas_call | solution.py:534
Async XLA Ops:
  0.6 21.3 %copy-start = (bf16[3,3,13,64]{3,2,1,0:T(8,128)(2,1)S(1)}, bf16[3,3,13,64]{3,2,1,0:T(8,128)(2,1)}, u32[]{:S(2)}) copy-start(bf16[3,3,13,64]{3,2,1,0:T(8,128)(2,1)} %param.21) | copy-start | bytes 44932
  9.9 12.0 %copy-start.3 = (bf16[8,4,3,1,1]{2,1,4,3,0:T(4,128)(2,1)S(1)}, bf16[8,4,3,1,1]{2,1,4,3,0:T(4,128)(2,1)}, u32[]{:S(2)}) copy-start(bf16[8,4,3,1,1]{2,1,4,3,0:T(4,128)(2,1)} %constant.35) | copy-start | bytes 580
  9.9 12.2 %copy-start.4 = (bf16[4,2,3,1,1,1]{2,0,1,5,4,3:T(4,128)(2,1)S(1)}, bf16[4,2,3,1,1,1]{2,0,1,5,4,3:T(4,128)(2,1)}, u32[]{:S(2)}) copy-start(bf16[4,2,3,1,1,1]{2,0,1,5,4,3:T(4,128)(2,1)} %constant.36) | copy-start | bytes 148
  10.0 98.6 %all-to-all-start = ((bf16[128,216,128]{2,1,0:T(8,128)(2,1)}), bf16[128,216,128]{2,1,0:T(8,128)(2,1)}, u32[]{:S(2)}, u32[]{:S(2)}) async-start(bf16[128,216,128]{2,1,0:T(8,128)(2,1)} %resample.1), calls=%async_computation | async-start | bytes 14155776 | tf_op jit(solution)/shard_map/all_to_all | solution.py:605
  21.9 2.3 %copy-start.2 = (bf16[3,3,128,128]{3,2,1,0:T(8,128)(2,1)S(1)}, bf16[3,3,128,128]{3,2,1,0:T(8,128)(2,1)}, u32[]{:S(2)}) copy-start(bf16[3,3,128,128]{3,2,1,0:T(8,128)(2,1)} %param.23) | copy-start | bytes 884740
  124.5 1.1 copy-start.1

commit v5 on v4

--- a/solution.py
+++ b/solution.py
@@ -15,11 +15,26 @@
 NWIN = 32
 BR = BANDS * WIN
 HALO = 16
-BIG_VMEM = 56 << 20
+BIG_VMEM = 58 << 20
 
 
 def resample_kernel(
-    dest, window, bank_index, raw, weights, bank, out, tiled, res, tags, tags_out, count, sem, tag_sem
+    dest,
+    window,
+    bank_index,
+    raw,
+    weights,
+    bank,
+    out,
+    tiled_low,
+    tiled_high,
+    res,
+    tags,
+    tags_out,
+    count,
+    rank,
+    sem,
+    tag_sem,
 ):
     step = pl.program_id(0)
     per = raw.shape[0]
@@ -30,30 +45,39 @@
     @pl.when(step == 0)
     def _():
         spread = (
-            lax.broadcasted_iota(jnp.int32, (16, lanes), 1) % 16
-            == lax.broadcasted_iota(jnp.int32, (16, lanes), 0)
+            lax.broadcasted_iota(jnp.int32, (16, 256), 1) % 16
+            == lax.broadcasted_iota(jnp.int32, (16, 256), 0)
         ).astype(jnp.bfloat16)
-        tiled[...] = jnp.dot(weights[...], spread, preferred_element_type=jnp.float32)
+        for r in range(WIN):
+            both = lax.dot_general(
+                weights[r],
+                spread,
+                (((0,), (0,)), ((), ())),
+                preferred_element_type=jnp.float32,
+            )
+            tiled_low[pl.ds(r, held, stride=WIN), :] = both[:, :128]
+            tiled_high[pl.ds(r, held, stride=WIN), :] = both[:, 128:]
         tags[...] = jnp.full_like(tags, float(NWIN))
 
-        @pl.loop(0, tiles)
+        @pl.loop(0, tiles // 8)
         def _(t):
-            count[t] = 0
-
-        @pl.loop(0, held)
-        def _(n):
-            tile = dest[n]
-            tags[tile, pl.ds(count[tile], 1), :] = jnp.full((1, 128), window[n], jnp.int32).astype(
-                jnp.float32
-            )
-            count[tile] = count[tile] + 1
+            for u in range(8):
+                count[t * 8 + u] = 0
+
+        @pl.loop(0, held // 4)
+        def _(group):
+            for u in range(4):
+                n = group * 4 + u
+                tile = dest[n]
+                place = count[tile]
+                rank[n] = place
+                count[tile] = place + 1
+                tags[tile, pl.ds(place, 1), :] = jnp.full((1, 128), window[n], jnp.int32).astype(
+                    jnp.float32
+                )
 
         tags_out[...] = tags[...].astype(jnp.bfloat16)
         pltpu.make_async_copy(tags_out, out.at[:, pl.ds(CAP * BR, 8)], tag_sem).start()
-
-        @pl.loop(0, tiles)
-        def _(t):
-            count[t] = 0
 
     own_band = (
         lax.broadcasted_iota(jnp.int32, (BANDS, WIN, lanes), 2) // 16
@@ -62,7 +86,8 @@
     rowed = []
     for k in range(per):
         n = step * per + k
-        row = tiled[pl.ds(pl.multiple_of(n * WIN, WIN), WIN), :]
+        rows = pl.ds(pl.multiple_of(n * WIN, WIN), WIN)
+        row = jnp.concatenate([tiled_low[rows, :], tiled_high[rows, : lanes - 128]], axis=1)
         block = jnp.where(own_band, row[None], 0.0).reshape(BR, lanes).astype(jnp.bfloat16)
         rowed.append(
             jnp.dot(
@@ -76,11 +101,8 @@
         ).astype(jnp.bfloat16)
     for k in range(per):
         n = step * per + k
-        tile = dest[n]
-        rank = count[tile]
-        count[tile] = rank + 1
         pltpu.make_async_copy(
-            res.at[n], out.at[tile, pl.ds(pl.multiple_of(rank * BR, 8), BR)], sem
+            res.at[n], out.at[dest[n], pl.ds(pl.multiple_of(rank[n] * BR, 8), BR)], sem
         ).start()
 
     @pl.when(step == pl.num_programs(0) - 1)
@@ -100,23 +122,25 @@
             pl.BlockSpec(memory_space=pltpu.SMEM),
             pl.BlockSpec(memory_space=pltpu.SMEM),
             pl.BlockSpec((per, BANDS, 16, 128), lambda i: (i, 0, 0, 0)),
-            pl.BlockSpec((held * WIN, 16), lambda i: (0, 0)),
+            pl.BlockSpec((WIN, 16, held), lambda i: (0, 0, 0)),
             pl.BlockSpec(bank.shape, lambda i: (0, 0, 0)),
         ],
         out_specs=pl.BlockSpec(memory_space=pltpu.HBM),
         out_shape=jax.ShapeDtypeStruct((tiles, CAP * BR + 8, 128), jnp.bfloat16),
         scratch_shapes=[
-            pltpu.VMEM((held * WIN, BANDS * 16), jnp.float32),
+            pltpu.VMEM((held * WIN, 128), jnp.float32),
+            pltpu.VMEM((held * WIN, 128), jnp.float32),
             pltpu.VMEM((held, BR, 128), jnp.bfloat16),
             pltpu.VMEM((tiles, 8, 128), jnp.float32),
             pltpu.VMEM((tiles, 8, 128), jnp.bfloat16),
             pltpu.SMEM((tiles,), jnp.int32),
+            pltpu.SMEM((held,), jnp.int32),
             pltpu.SemaphoreType.DMA,
             pltpu.SemaphoreType.DMA,
         ],
         compiler_params=pltpu.CompilerParams(vmem_limit_bytes=BIG_VMEM),
         name="resample",
-    )(dest, window, bank_index, raw, weights.reshape(held * WIN, 16), bank)
+    )(dest, window, bank_index, raw, jnp.transpose(weights, (1, 2, 0)), bank)
 
 
 def gather_kernel(
@@ -201,7 +225,7 @@
             pltpu.SemaphoreType.DMA,
             pltpu.SemaphoreType.DMA,
         ],
-        compiler_params=pltpu.CompilerParams(vmem_limit_bytes=32 << 20),
+        compiler_params=pltpu.CompilerParams(vmem_limit_bytes=BIG_VMEM),
         name="gather_windows",
     )(got, got)
 
@@ -222,7 +246,7 @@
 MOVES = [(1, 0), (-1, 0), (0, 1), (0, -1), (1, 1), (1, -1), (-1, 1), (-1, -1)]
 
 
-def widen_kernel(zeros, tile, wide, own_sem, zero_sem, send_sem, recv_sem):
+def widen_kernel(tile, wide, zero_rows, zero_cols, own_sem, zero_sem, send_sem, recv_sem):
     tx, ty = lax.axis_index("tx"), lax.axis_index("ty")
     nx, ny = lax.axis_size("tx"), lax.axis_size("ty")
 
@@ -253,6 +277,8 @@
 
     own = pltpu.make_async_copy(tile, target(0, 0), own_sem)
     own.start()
+    zero_rows[...] = jnp.zeros_like(zero_rows)
+    zero_cols[...] = jnp.zeros_like(zero_cols)
     peers = sum(inside(dx, dy).astype(jnp.int32) for dx, dy in MOVES)
     pl.semaphore_wait(barrier, peers)
 
@@ -267,6 +293,7 @@
             device_id_type=MESH,
         )
         (w, wn), (c, cn) = SIDE[dy][1], EDGE[dx][1]
+        zeros = zero_rows if dy else zero_cols
         blank = pltpu.make_async_copy(
             zeros.at[pl.ds(0, wn), pl.ds(0, cn)], target(dx, dy), zero_sem.at[i]
         )
@@ -301,40 +328,42 @@
     moves = len(MOVES)
     return pl.pallas_call(
         widen_kernel,
-        in_specs=[pl.BlockSpec(memory_space=pltpu.VMEM), pl.BlockSpec(memory_space=pl.ANY)],
+        in_specs=[pl.BlockSpec(memory_space=pl.ANY)],
         out_specs=pl.BlockSpec(memory_space=pl.ANY),
         out_shape=jax.ShapeDtypeStruct(
             (NWIN + 2 * HALO_WIN, 128 + 2 * HALO, 128), jnp.bfloat16
         ),
         scratch_shapes=[
+            pltpu.VMEM((HALO_WIN, 128, 128), jnp.bfloat16),
+            pltpu.VMEM((NWIN, HALO, 128), jnp.bfloat16),
             pltpu.SemaphoreType.DMA,
             pltpu.SemaphoreType.DMA((moves,)),
             pltpu.SemaphoreType.DMA((moves,)),
             pltpu.SemaphoreType.DMA((moves,)),
         ],
         compiler_params=pltpu.CompilerParams(
-            collective_id=0, has_side_effects=True, vmem_limit_bytes=16 << 20
+            collective_id=0, has_side_effects=True, vmem_limit_bytes=BIG_VMEM
         ),
         name="widen",
-    )(jnp.zeros((NWIN, 128, 128), jnp.bfloat16), turned)
+    )(turned)
 
 
 FAR = 1 << 20
-HALVES = 8
-STEPS_ONE = 9
+HALVES = 18
+STEPS_ONE = 4
 PAIRS = 40
 PIX = 2 * PAIRS
 ROWS_TWO = STEPS_ONE * HALVES
-ROWS_THREE = 10
-STEPS_THREE = 7
-ROWS_FOUR = 6
-STEPS_FOUR = 6
+ROWS_THREE = 14
+STEPS_THREE = 5
+ROWS_FOUR = 17
+STEPS_FOUR = 2
 WIDE_FOUR = 24
 
 
 def encoder_kernel(
     edges,
-    wide,
+    hbm_wide,
     weight_one,
     reduce_two,
     hbm_two,
@@ -343,6 +372,7 @@
     hbm_reduce_four,
     hbm_four,
     out,
+    wide,
     slab,
     patch,
     even_two,
@@ -359,7 +389,14 @@
     reduce_four,
     weight_four,
     sems,
+    wide_sems,
 ):
+    def part(i):
+        here = pl.ds(i * (HALVES // 2), HALVES // 2)
+        return pltpu.make_async_copy(hbm_wide.at[here], wide.at[here], wide_sems.at[i])
+
+    for i in range(STEPS_ONE):
+        part(i).start()
     fetches = [
         pltpu.make_async_copy(source, target, sems.at[i])
         for i, (source, target) in enumerate(
@@ -401,9 +438,14 @@
     col_two = jnp.where(at < PAIRS, 2 * at, 2 * (at - PAIRS) + 1) - 7
     limits_two = bounds(128, 64)
     carry_two[...] = jnp.zeros_like(carry_two)
+    part(0).wait()
 
     @pl.loop(0, STEPS_ONE)
     def _(step):
+        @pl.when(step < STEPS_ONE - 1)
+        def _():
+            part(step + 1).wait()
+
         for k in range(HALVES):
             w = step * (HALVES // 2) + k // 2
             here = wide[jnp.minimum(w, last)].astype(jnp.float32)
@@ -533,10 +575,11 @@
     big = (two, reduce_three, three, reduce_four, four)
     return pl.pallas_call(
         encoder_kernel,
-        in_specs=[pl.BlockSpec(memory_space=pltpu.SMEM), vmem, vmem, vmem] + [hbm] * len(big),
+        in_specs=[pl.BlockSpec(memory_space=pltpu.SMEM), hbm, vmem, vmem] + [hbm] * len(big),
         out_specs=vmem,
         out_shape=jax.ShapeDtypeStruct((512, 512), jnp.bfloat16),
         scratch_shapes=[
+            pltpu.VMEM(wide.shape, jnp.bfloat16),
             pltpu.VMEM((HALVES, 168, 128), jnp.float32),
             pltpu.VMEM((HALVES, PIX, 512), jnp.bfloat16),
             pltpu.VMEM((ROWS_TWO, PIX, 512), jnp.bfloat16),
@@ -549,7 +592,7 @@
             pltpu.VMEM((STEPS_FOUR * ROWS_FOUR, 16, 1536), jnp.bfloat16),
         ]
         + [pltpu.VMEM(w.shape, jnp.bfloat16) for w in big]
-        + [pltpu.SemaphoreType.DMA((len(big),))],
+        + [pltpu.SemaphoreType.DMA((len(big),)), pltpu.SemaphoreType.DMA((STEPS_ONE,))],
         compiler_params=pltpu.CompilerParams(vmem_limit_bytes=BIG_VMEM),
         name="encoder",
     )(edges, wide, one, reduce_two, *big)

time: 155 us -> 176 us (1.14); the launches traced: 154 us -> 173 us
  Pallas kernels: 51.6 us -> 73.3 us
  local copies, waits for them, and re-layouts: 7.56 us -> 4.66 us
    pallas_call x1, Pallas kernels: 8.34 us -> 33.4 us  [widen(): pl.pallas_call(widen_kernel, in_specs=[pl.BlockSpec(memory_space=pl.ANY)]...]
    unnamed x11 -> x8, local copies, waits for them, and re-layouts: 2.7 us -> 0.03 us
    pallas_call x1, Pallas kernels: 28.2 us -> 25.9 us  [encode(): pl.pallas_call(encoder_kernel, in_specs=[pl.BlockSpec(memory_space=pltpu....]
where the time goes in v5:
time: 176 us; the launch traced here: 173 us
  waiting for transfers between devices  80.5 us (46%)
  Pallas kernels  73.3 us (42%)
  starting transfers between devices  11.9 us (7%)
  local copies, waits for them, and re-layouts  4.66 us (3%)
    all_to_all x1, waiting for transfers between devices, body(): lax.all_to_all(sent, ('tx', 'ty'), split_axis=0, concat_axis=0, tiled=True)  80.5 us
    pallas_call x1, Pallas kernels, widen(): pl.pallas_call(widen_kernel, in_specs=[pl.BlockSpec(memory_space=pl.ANY)]...  33.4 us
    pallas_call x1, Pallas kernels, encode(): pl.pallas_call(encoder_kernel, in_specs=[pl.BlockSpec(memory_space=pltpu....  25.9 us
    all_to_all x1, starting transfers between devices, body(): lax.all_to_all(sent, ('tx', 'ty'), split_axis=0, concat_axis=0, tiled=True)  11.9 us
    pallas_call x1, Pallas kernels, gather_windows(): pl.pallas_call(gather_kernel, grid=(tiles // per,), in_specs=[pl.BlockSpe...  7.73 us
    pallas_call x1, Pallas kernels, resample(): pl.pallas_call(resample_kernel, grid=(held // per,), in_specs=[pl.BlockSp...  6.24 us
  transfers between devices with their start and end apart: 1, of which 1 were waited for; matrix products, arithmetic and copies ran while one was open for 4% of the time, Pallas kernels for 0%

profile of v5, /device:TPU:1, one launch (start us, length us, event | category | flops | bytes accessed | tf_op | source)
XLA Modules:
  0.0 172.8 jit_solution(14007599881374210429)
XLA Ops:
  0.6 0.0 copy-start
  0.6 6.2 %resample.1 = bf16[128,216,128]{2,1,0:T(8,128)(2,1)} custom-call(s32[64]{0:T(128)} %dest.1, s32[64]{0:T(128)} %window.1, s32[64]{0:T(128)} %bank_index.1, bf16[64,13,16,128]{3,2,1,0:T(8,128)(2,1)} %raw.1, bf16[8,16,64]{2,1,0:T(8,128)(2,1)} %bitcast.44, bf16[8,128,128]{2,1,0:T(8,128)(2,1)} %bank.1), custom_call_target="tpu_custom_call" | custom-call | tf_op jit(solution)/shard_map/resample/pallas_call | solution.py:117
  6.9 0.0 copy-start.2
  6.9 0.0 copy-start.3
  6.9 11.9 %all-to-all-start = ((bf16[128,216,128]{2,1,0:T(8,128)(2,1)}), bf16[128,216,128]{2,1,0:T(8,128)(2,1)}, u32[]{:S(2)}, u32[]{:S(2)}) async-start(bf16[128,216,128]{2,1,0:T(8,128)(2,1)} %resample.1), calls=%async_computation | async-start | bytes 14155776 | tf_op jit(solution)/shard_map/all_to_all | solution.py:648
  18.8 0.0 copy-start.1
  18.9 0.0 copy-done
  18.9 0.0 copy-done.2
  18.9 0.2 fusion.2
  19.1 0.0 copy-done.3
  19.1 0.6 convolution_bitcast_fusion
  19.7 0.9 copy.18
  20.6 0.5 reshape.31
  21.2 0.0 copy-done.1
  21.2 0.1 pad_bitcast_fusion.1
  21.3 0.1 pad_maximum_fusion
  21.4 0.8 copy.19
  22.2 1.4 reshape.34.hbm_two
  23.6 0.8 pad.12
  24.5 0.6 add_convert_fusion.edges
  25.1 80.5 %all-to-all-done.got.all_got = bf16[128,216,128]{2,1,0:T(8,128)(2,1)} async-done(((bf16[128,216,128]{2,1,0:T(8,128)(2,1)}), bf16[128,216,128]{2,1,0:T(8,128)(2,1)}, u32[]{:S(2)}, u32[]{:S(2)}) %all-to-all-start) | async-done | bytes 7077920 | tf_op jit(solution)/shard_map/all_to_all | solution.py:648
  105.5 7.7 %gather_windows.1 = (bf16[13,256,128]{2,1,0:T(8,128)(2,1)}, bf16[32,128,128]{2,1,0:T(8,128)(2,1)}) custom-call(bf16[128,216,128]{2,1,0:T(8,128)(2,1)} %all-to-all-done.got.all_got, bf16[128,216,128]{2,1,0:T(8,128)(2,1)} %all-to-all-done.got.all_got), custom_call_target="tpu_custom_call" | custom-call | tf_op jit(solution)/shard_map/gather_windows/pallas_call | solution.py:203
  113.2 33.4 %widen.1.hbm_wide = bf16[36,160,128]{2,1,0:T(8,128)(2,1)} custom-call(bf16[32,128,128]{2,1,0:T(8,128)(2,1)} %get-tuple-element.5.tile), custom_call_target="tpu_custom_call" | custom-call | tf_op jit(solution)/shard_map/widen/pallas_call | solution.py:329
  146.7 25.9 %encoder.1 = bf16[512,512]{1,0:T(8,128)(2,1)} custom-call(s32[4]{0:T(128)} %add_convert_fusion.edges, bf16[36,160,128]{2,1,0:T(8,128)(2,1)} %widen.1.hbm_wide, bf16[512,512]{1,0:T(8,128)(2,1)} %bitcast.38, bf16[256,128]{1,0:T(8,128)(2,1)} %bitcast.43, bf16[3,512,256]{2,1,0:T(8,128)(2,1)} %reshape.34.hbm_two, bf16[512,256]{1,0:T(8,128)(2,1)} %bitcast.42, ...), custom_call_target="tpu_custom_call" | custom-call | tf_op jit(solution)/shard_map/encoder/pallas_call | solution.py:576
Async XLA Ops:
  0.6 18.2 %copy-start = (bf16[3,3,13,64]{3,2,1,0:T(8,128)(2,1)S(1)}, bf16[3,3,13,64]{3,2,1,0:T(8,128)(2,1)}, u32[]{:S(2)}) copy-start(bf16[3,3,13,64]{3,2,1,0:T(8,128)(2,1)} %param.21) | copy-start | bytes 44932
  6.9 12.0 %copy-start.2 = (bf16[8,4,3,1,1]{2,1,4,3,0:T(4,128)(2,1)S(1)}, bf16[8,4,3,1,1]{2,1,4,3,0:T(4,128)(2,1)}, u32[]{:S(2)}) copy-start(bf16[8,4,3,1,1]{2,1,4,3,0:T(4,128)(2,1)} %constant.34) | copy-start | bytes 580
  6.9 12.2 %copy-start.3 = (bf16[4,2,3,1,1,1]{2,0,1,5,4,3:T(4,128)(2,1)S(1)}, bf16[4,2,3,1,1,1]{2,0,1,5,4,3:T(4,128)(2,1)}, u32[]{:S(2)}) copy-start(bf16[4,2,3,1,1,1]{2,0,1,5,4,3:T(4,128)(2,1)} %constant.35) | copy-start | bytes 148
  6.9 98.6 %all-to-all-start = ((bf16[128,216,128]{2,1,0:T(8,128)(2,1)}), bf16[128,216,128]{2,1,0:T(8,128)(2,1)}, u32[]{:S(2)}, u32[]{:S(2)}) async-start(bf16[128,216,128]{2,1,0:T(8,128)(2,1)} %resample.1), calls=%async_computation | async-start | bytes 14155776 | tf_op jit(solution)/shard_map/all_to_all | solution.py:648
  18.8 2.3 %copy-start.1 = (bf16[3,3,128,128]{3,2,1,0:T(8,128)(2,1)S(1)}, bf16[3,3,128,128]{3,2,1,0:T(8,128)(2,1)}, u32[]{:S(2)}) copy-start(bf16[3,3,128,128]{3,2,1,0:T(8,128)(2,1)} %param.23) | copy-start | bytes 884740

commit v6 on v5

--- a/solution.py
+++ b/solution.py
@@ -231,22 +231,24 @@
 
 
 HALO_WIN = HALO // WIN
-LAST_WIN = NWIN + HALO_WIN
-LAST_COL = 128 + HALO
-SIDE = {
-    -1: ((0, HALO_WIN), (LAST_WIN, HALO_WIN)),
-    0: ((0, NWIN), (HALO_WIN, NWIN)),
-    1: ((NWIN - HALO_WIN, HALO_WIN), (0, HALO_WIN)),
-}
-EDGE = {
-    -1: ((0, HALO), (LAST_COL, HALO)),
-    0: ((0, 128), (HALO, 128)),
-    1: ((128 - HALO, HALO), (0, HALO)),
-}
+WIDE_WIN = NWIN + 2 * HALO_WIN
+WIDE_COL = 128 + 2 * HALO
 MOVES = [(1, 0), (-1, 0), (0, 1), (0, -1), (1, 1), (1, -1), (-1, 1), (-1, -1)]
 
 
-def widen_kernel(tile, wide, zero_rows, zero_cols, own_sem, zero_sem, send_sem, recv_sem):
+def rim_kernel(
+    tile,
+    rim_rows,
+    rim_cols,
+    edge_rows,
+    edge_cols,
+    zero_rows,
+    zero_cols,
+    edge_sem,
+    zero_sem,
+    send_sem,
+    recv_sem,
+):
     tx, ty = lax.axis_index("tx"), lax.axis_index("ty")
     nx, ny = lax.axis_size("tx"), lax.axis_size("ty")
 
@@ -259,12 +261,16 @@
         return ok
 
     def source(dx, dy):
-        (w, wn), (c, cn) = SIDE[dy][0], EDGE[dx][0]
-        return tile.at[pl.ds(w, wn), pl.ds(c, cn)]
+        if dy == 0:
+            return edge_cols.at[:, pl.ds(HALO if dx > 0 else 0, HALO)]
+        c, cn = {-1: (0, HALO), 0: (0, 128), 1: (128 - HALO, HALO)}[dx]
+        return edge_rows.at[pl.ds(HALO_WIN if dy > 0 else 0, HALO_WIN), pl.ds(c, cn)]
 
     def target(dx, dy):
-        (w, wn), (c, cn) = SIDE[dy][1], EDGE[dx][1]
-        return wide.at[pl.ds(w, wn), pl.ds(c, cn)]
+        if dy == 0:
+            return rim_cols.at[:, pl.ds(0 if dx > 0 else HALO, HALO)]
+        c, cn = {-1: (HALO + 128, HALO), 0: (HALO, 128), 1: (0, HALO)}[dx]
+        return rim_rows.at[pl.ds(0 if dy > 0 else HALO_WIN, HALO_WIN), pl.ds(c, cn)]
 
     barrier = pltpu.get_barrier_semaphore()
     for dx, dy in MOVES:
@@ -275,10 +281,26 @@
                 barrier, inc=1, device_id=(tx + dx, ty + dy), device_id_type=MESH
             )
 
-    own = pltpu.make_async_copy(tile, target(0, 0), own_sem)
-    own.start()
+    edges = [
+        pltpu.make_async_copy(src, dst, edge_sem.at[i])
+        for i, (src, dst) in enumerate(
+            (
+                (tile.at[pl.ds(0, HALO_WIN)], edge_rows.at[pl.ds(0, HALO_WIN)]),
+                (
+                    tile.at[pl.ds(NWIN - HALO_WIN, HALO_WIN)],
+                    edge_rows.at[pl.ds(HALO_WIN, HALO_WIN)],
+                ),
+                (tile.at[:, pl.ds(0, HALO)], edge_cols.at[:, pl.ds(0, HALO)]),
+                (tile.at[:, pl.ds(128 - HALO, HALO)], edge_cols.at[:, pl.ds(HALO, HALO)]),
+            )
+        )
+    ]
+    for edge in edges:
+        edge.start()
     zero_rows[...] = jnp.zeros_like(zero_rows)
     zero_cols[...] = jnp.zeros_like(zero_cols)
+    for edge in edges:
+        edge.wait()
     peers = sum(inside(dx, dy).astype(jnp.int32) for dx, dy in MOVES)
     pl.semaphore_wait(barrier, peers)
 
@@ -292,11 +314,8 @@
             device_id=(tx + dx, ty + dy),
             device_id_type=MESH,
         )
-        (w, wn), (c, cn) = SIDE[dy][1], EDGE[dx][1]
-        zeros = zero_rows if dy else zero_cols
-        blank = pltpu.make_async_copy(
-            zeros.at[pl.ds(0, wn), pl.ds(0, cn)], target(dx, dy), zero_sem.at[i]
-        )
+        zeros = zero_rows.at[:, pl.ds(0, HALO if dx else 128)] if dy else zero_cols
+        blank = pltpu.make_async_copy(zeros, target(dx, dy), zero_sem.at[i])
         copies.append((send, blank, inside(dx, dy), inside(-dx, -dy)))
     for send, blank, goes, comes in copies:
 
@@ -308,7 +327,6 @@
         def _():
             blank.start()
 
-    own.wait()
     for send, blank, goes, comes in copies:
 
         @pl.when(goes)
@@ -324,19 +342,23 @@
             blank.wait()
 
 
-def widen(turned):
+def rim(turned):
     moves = len(MOVES)
+    vmem = pl.BlockSpec(memory_space=pltpu.VMEM)
     return pl.pallas_call(
-        widen_kernel,
+        rim_kernel,
         in_specs=[pl.BlockSpec(memory_space=pl.ANY)],
-        out_specs=pl.BlockSpec(memory_space=pl.ANY),
-        out_shape=jax.ShapeDtypeStruct(
-            (NWIN + 2 * HALO_WIN, 128 + 2 * HALO, 128), jnp.bfloat16
-        ),
+        out_specs=[vmem, vmem],
+        out_shape=[
+            jax.ShapeDtypeStruct((2 * HALO_WIN, WIDE_COL, 128), jnp.bfloat16),
+            jax.ShapeDtypeStruct((NWIN, 2 * HALO, 128), jnp.bfloat16),
+        ],
         scratch_shapes=[
+            pltpu.VMEM((2 * HALO_WIN, 128, 128), jnp.bfloat16),
+            pltpu.VMEM((NWIN, 2 * HALO, 128), jnp.bfloat16),
             pltpu.VMEM((HALO_WIN, 128, 128), jnp.bfloat16),
             pltpu.VMEM((NWIN, HALO, 128), jnp.bfloat16),
-            pltpu.SemaphoreType.DMA,
+            pltpu.SemaphoreType.DMA((4,)),
             pltpu.SemaphoreType.DMA((moves,)),
             pltpu.SemaphoreType.DMA((moves,)),
             pltpu.SemaphoreType.DMA((moves,)),
@@ -344,7 +366,7 @@
         compiler_params=pltpu.CompilerParams(
             collective_id=0, has_side_effects=True, vmem_limit_bytes=BIG_VMEM
         ),
-        name="widen",
+        name="rim",
     )(turned)
 
 
@@ -363,7 +385,9 @@
 
 def encoder_kernel(
     edges,
-    hbm_wide,
+    tile,
+    rim_rows,
+    rim_cols,
     weight_one,
     reduce_two,
     hbm_two,
@@ -391,12 +415,32 @@
     sems,
     wide_sems,
 ):
-    def part(i):
-        here = pl.ds(i * (HALVES // 2), HALVES // 2)
-        return pltpu.make_async_copy(hbm_wide.at[here], wide.at[here], wide_sems.at[i])
-
+    per = HALVES // 2
+    parts = []
     for i in range(STEPS_ONE):
-        part(i).start()
+        low_win, high_win = max(i * per, HALO_WIN), min((i + 1) * per, HALO_WIN + NWIN)
+        inner = pl.ds(low_win - HALO_WIN, high_win - low_win)
+        outer = pl.ds(low_win, high_win - low_win)
+        moves = [
+            (tile.at[inner], wide.at[outer, pl.ds(HALO, 128)]),
+            (rim_cols.at[inner, pl.ds(0, HALO)], wide.at[outer, pl.ds(0, HALO)]),
+            (rim_cols.at[inner, pl.ds(HALO, HALO)], wide.at[outer, pl.ds(HALO + 128, HALO)]),
+        ]
+        if i == 0:
+            moves.append((rim_rows.at[pl.ds(0, HALO_WIN)], wide.at[pl.ds(0, HALO_WIN)]))
+        if i == STEPS_ONE - 1:
+            moves.append(
+                (rim_rows.at[pl.ds(HALO_WIN, HALO_WIN)], wide.at[pl.ds(WIDE_WIN - HALO_WIN, HALO_WIN)])
+            )
+        parts.append(
+            [
+                pltpu.make_async_copy(src, dst, wide_sems.at[i, j])
+                for j, (src, dst) in enumerate(moves)
+            ]
+        )
+    for copies in parts:
+        for copy in copies:
+            copy.start()
     fetches = [
         pltpu.make_async_copy(source, target, sems.at[i])
         for i, (source, target) in enumerate(
@@ -438,13 +482,17 @@
     col_two = jnp.where(at < PAIRS, 2 * at, 2 * (at - PAIRS) + 1) - 7
     limits_two = bounds(128, 64)
     carry_two[...] = jnp.zeros_like(carry_two)
-    part(0).wait()
+    for copy in parts[0]:
+        copy.wait()
 
     @pl.loop(0, STEPS_ONE)
     def _(step):
-        @pl.when(step < STEPS_ONE - 1)
-        def _():
-            part(step + 1).wait()
+        for i in range(1, STEPS_ONE):
+
+            @pl.when(step == i - 1)
+            def _():
+                for copy in parts[i]:
+                    copy.wait()
 
         for k in range(HALVES):
             w = step * (HALVES // 2) + k // 2
@@ -569,17 +617,20 @@
         out[:, lanes] = jnp.maximum(hidden, 0.0).astype(jnp.bfloat16)
 
 
-def encode(wide, edges, one, two, reduce_three, three, reduce_four, four, reduce_two):
+def encode(tile, rims, edges, one, two, reduce_three, three, reduce_four, four, reduce_two):
     hbm = pl.BlockSpec(memory_space=pltpu.HBM)
     vmem = pl.BlockSpec(memory_space=pltpu.VMEM)
     big = (two, reduce_three, three, reduce_four, four)
     return pl.pallas_call(
         encoder_kernel,
-        in_specs=[pl.BlockSpec(memory_space=pltpu.SMEM), hbm, vmem, vmem] + [hbm] * len(big),
+        in_specs=[pl.BlockSpec(memory_space=pltpu.SMEM)]
+        + [hbm] * 3
+        + [vmem] * 2
+        + [hbm] * len(big),
         out_specs=vmem,
         out_shape=jax.ShapeDtypeStruct((512, 512), jnp.bfloat16),
         scratch_shapes=[
-            pltpu.VMEM(wide.shape, jnp.bfloat16),
+            pltpu.VMEM((WIDE_WIN, WIDE_COL, 128), jnp.bfloat16),
             pltpu.VMEM((HALVES, 168, 128), jnp.float32),
             pltpu.VMEM((HALVES, PIX, 512), jnp.bfloat16),
             pltpu.VMEM((ROWS_TWO, PIX, 512), jnp.bfloat16),
@@ -592,10 +643,10 @@
             pltpu.VMEM((STEPS_FOUR * ROWS_FOUR, 16, 1536), jnp.bfloat16),
         ]
         + [pltpu.VMEM(w.shape, jnp.bfloat16) for w in big]
-        + [pltpu.SemaphoreType.DMA((len(big),)), pltpu.SemaphoreType.DMA((STEPS_ONE,))],
+        + [pltpu.SemaphoreType.DMA((len(big),)), pltpu.SemaphoreType.DMA((STEPS_ONE, 4))],
         compiler_params=pltpu.CompilerParams(vmem_limit_bytes=BIG_VMEM),
         name="encoder",
-    )(edges, wide, one, reduce_two, *big)
+    )(edges, tile, *rims, one, reduce_two, *big)
 
 
 def patch_weights(kernel):
@@ -647,10 +698,10 @@
     )
     got = lax.all_to_all(sent, ("tx", "ty"), split_axis=0, concat_axis=0, tiled=True)
     gridded, turned = gather_windows(got)
-    wide = widen(turned)
     edges = jnp.stack([ty == 0, ty == ny - 1, tx == 0, tx == nx - 1]).astype(jnp.int32)
     bottleneck = encode(
-        wide,
+        turned,
+        rim(turned),
         edges,
         patch_weights(kernel_one),
         pair_weights(kernel_two),

time: 176 us -> 149 us (0.85); the launches traced: 173 us -> 149 us
  Pallas kernels: 73.3 us -> 49.1 us
    pallas_call x1, Pallas kernels: 33.4 us -> 9.32 us  [rim(): pl.pallas_call(rim_kernel, in_specs=[pl.BlockSpec(memory_space=pl.ANY)],...]
where the time goes in v6:
time: 149 us
  waiting for transfers between devices  80.5 us (54%)
  Pallas kernels  49.1 us (33%)
  starting transfers between devices  11.9 us (8%)
  local copies, waits for them, and re-layouts  4.66 us (3%)
    all_to_all x1, waiting for transfers between devices, body(): lax.all_to_all(sent, ('tx', 'ty'), split_axis=0, concat_axis=0, tiled=True)  80.5 us
    pallas_call x1, Pallas kernels, encode(): pl.pallas_call(encoder_kernel, in_specs=[pl.BlockSpec(memory_space=pltpu....  25.8 us
    all_to_all x1, starting transfers between devices, body(): lax.all_to_all(sent, ('tx', 'ty'), split_axis=0, concat_axis=0, tiled=True)  11.9 us
    pallas_call x1, Pallas kernels, rim(): pl.pallas_call(rim_kernel, in_specs=[pl.BlockSpec(memory_space=pl.ANY)],...  9.32 us
    pallas_call x1, Pallas kernels, gather_windows(): pl.pallas_call(gather_kernel, grid=(tiles // per,), in_specs=[pl.BlockSpe...  7.74 us
    pallas_call x1, Pallas kernels, resample(): pl.pallas_call(resample_kernel, grid=(held // per,), in_specs=[pl.BlockSp...  6.22 us
  transfers between devices with their start and end apart: 1, of which 1 were waited for; matrix products, arithmetic and copies ran while one was open for 4% of the time, Pallas kernels for 0%

profile of v6, /device:TPU:1, one launch (start us, length us, event | category | flops | bytes accessed | tf_op | source)
XLA Modules:
  0.0 148.6 jit_solution(17616273319702341580)
XLA Ops:
  0.6 0.0 copy-start
  0.6 6.2 %resample.1 = bf16[128,216,128]{2,1,0:T(8,128)(2,1)} custom-call(s32[64]{0:T(128)} %dest.1, s32[64]{0:T(128)} %window.1, s32[64]{0:T(128)} %bank_index.1, bf16[64,13,16,128]{3,2,1,0:T(8,128)(2,1)} %raw.1, bf16[8,16,64]{2,1,0:T(8,128)(2,1)} %bitcast.44, bf16[8,128,128]{2,1,0:T(8,128)(2,1)} %bank.1), custom_call_target="tpu_custom_call" | custom-call | tf_op jit(solution)/shard_map/resample/pallas_call | solution.py:117
  6.9 0.0 copy-start.2
  6.9 0.0 copy-start.3
  6.9 11.9 %all-to-all-start = ((bf16[128,216,128]{2,1,0:T(8,128)(2,1)}), bf16[128,216,128]{2,1,0:T(8,128)(2,1)}, u32[]{:S(2)}, u32[]{:S(2)}) async-start(bf16[128,216,128]{2,1,0:T(8,128)(2,1)} %resample.1), calls=%async_computation | async-start | bytes 14155776 | tf_op jit(solution)/shard_map/all_to_all | solution.py:699
  18.8 0.0 copy-start.1
  18.9 0.0 copy-done
  18.9 0.0 copy-done.2
  18.9 0.2 fusion.2
  19.1 0.0 copy-done.3
  19.1 0.6 convolution_bitcast_fusion
  19.7 0.9 copy.18
  20.7 0.5 reshape.31
  21.2 0.0 copy-done.1
  21.2 0.1 pad_bitcast_fusion.1
  21.3 0.1 pad_maximum_fusion
  21.4 0.8 copy.19
  22.2 1.4 reshape.34.hbm_two
  23.6 0.8 pad.12
  24.5 0.6 add_convert_fusion.edges
  25.1 80.5 %all-to-all-done.got.all_got = bf16[128,216,128]{2,1,0:T(8,128)(2,1)} async-done(((bf16[128,216,128]{2,1,0:T(8,128)(2,1)}), bf16[128,216,128]{2,1,0:T(8,128)(2,1)}, u32[]{:S(2)}, u32[]{:S(2)}) %all-to-all-start) | async-done | bytes 7077920 | tf_op jit(solution)/shard_map/all_to_all | solution.py:699
  105.5 7.7 %gather_windows.1 = (bf16[13,256,128]{2,1,0:T(8,128)(2,1)}, bf16[32,128,128]{2,1,0:T(8,128)(2,1)}) custom-call(bf16[128,216,128]{2,1,0:T(8,128)(2,1)} %all-to-all-done.got.all_got, bf16[128,216,128]{2,1,0:T(8,128)(2,1)} %all-to-all-done.got.all_got), custom_call_target="tpu_custom_call" | custom-call | tf_op jit(solution)/shard_map/gather_windows/pallas_call | solution.py:203
  113.3 9.3 %rim.1 = (bf16[4,160,128]{2,1,0:T(8,128)(2,1)}, bf16[32,32,128]{2,1,0:T(8,128)(2,1)}) custom-call(bf16[32,128,128]{2,1,0:T(8,128)(2,1)} %get-tuple-element.7.tile), custom_call_target="tpu_custom_call" | custom-call | tf_op jit(solution)/shard_map/rim/pallas_call | solution.py:348
  122.6 25.8 %encoder.1 = bf16[512,512]{1,0:T(8,128)(2,1)} custom-call(s32[4]{0:T(128)} %add_convert_fusion.edges, bf16[32,128,128]{2,1,0:T(8,128)(2,1)} %get-tuple-element.7.tile, bf16[4,160,128]{2,1,0:T(8,128)(2,1)} %get-tuple-element.8.rim_rows, bf16[32,32,128]{2,1,0:T(8,128)(2,1)} %get-tuple-element.9.rim_cols, bf16[512,512]{1,0:T(8,128)(2,1)} %bitcast.38, ...), custom_call_target="tpu_custom_call" | custom-call | tf_op jit(solution)/shard_map/encoder/pallas_call | solution.py:624
Async XLA Ops:
  0.6 18.2 %copy-start = (bf16[3,3,13,64]{3,2,1,0:T(8,128)(2,1)S(1)}, bf16[3,3,13,64]{3,2,1,0:T(8,128)(2,1)}, u32[]{:S(2)}) copy-start(bf16[3,3,13,64]{3,2,1,0:T(8,128)(2,1)} %param.21) | copy-start | bytes 44932
  6.9 12.0 %copy-start.2 = (bf16[8,4,3,1,1]{2,1,4,3,0:T(4,128)(2,1)S(1)}, bf16[8,4,3,1,1]{2,1,4,3,0:T(4,128)(2,1)}, u32[]{:S(2)}) copy-start(bf16[8,4,3,1,1]{2,1,4,3,0:T(4,128)(2,1)} %constant.34) | copy-start | bytes 580
  6.9 12.2 %copy-start.3 = (bf16[4,2,3,1,1,1]{2,0,1,5,4,3:T(4,128)(2,1)S(1)}, bf16[4,2,3,1,1,1]{2,0,1,5,4,3:T(4,128)(2,1)}, u32[]{:S(2)}) copy-start(bf16[4,2,3,1,1,1]{2,0,1,5,4,3:T(4,128)(2,1)} %constant.35) | copy-start | bytes 148
  6.9 98.6 %all-to-all-start = ((bf16[128,216,128]{2,1,0:T(8,128)(2,1)}), bf16[128,216,128]{2,1,0:T(8,128)(2,1)}, u32[]{:S(2)}, u32[]{:S(2)}) async-start(bf16[128,216,128]{2,1,0:T(8,128)(2,1)} %resample.1), calls=%async_computation | async-start | bytes 14155776 | tf_op jit(solution)/shard_map/all_to_all | solution.py:699
  18.8 2.3 %copy-start.1 = (bf16[3,3,128,128]{3,2,1,0:T(8,128)(2,1)S(1)}, bf16[3,3,128,128]{3,2,1,0:T(8,128)(2,1)}, u32[]{:S(2)}) copy-start(bf16[3,3,128,128]{3,2,1,0:T(8,128)(2,1)} %param.23) | copy-start | bytes 884740

commit v7 on v6

--- a/solution.py
+++ b/solution.py
@@ -113,7 +113,7 @@
 
 def resample(raw, weights, bank, dest, window, bank_index, tiles):
     held = raw.shape[0]
-    per = 16
+    per = 32
     return pl.pallas_call(
         resample_kernel,
         grid=(held // per,),
@@ -143,48 +143,75 @@
     )(dest, window, bank_index, raw, jnp.transpose(weights, (1, 2, 0)), bank)
 
 
+CHUNKS = 4
+QUARTERS = 4
+
+
 def gather_kernel(
-    got, all_got, gridded, turned, even, odd, tags, dense, window, inverse, sem, tag_sem
+    got,
+    gridded_out,
+    turned_out,
+    held,
+    gridded,
+    turned,
+    even,
+    odd,
+    tags,
+    dense,
+    window,
+    inverse,
+    tag_sem,
+    dense_sem,
+    chunk_sem,
+    out_sem,
 ):
-    step = pl.program_id(0)
-    per = got.shape[0]
-    tiles = all_got.shape[0]
-
-    @pl.when(step == 0)
-    def _():
-        fetch = pltpu.make_async_copy(all_got.at[:, pl.ds(CAP * BR, 8)], tags, tag_sem)
-        fetch.start()
-        even[...] = jnp.zeros_like(even)
-        odd[...] = jnp.zeros_like(odd)
-        fetch.wait()
-        lane = lax.broadcasted_iota(jnp.int32, (8, 128), 1)
-        total = jnp.zeros((8, 128), jnp.float32)
-        for t in range(tiles):
-            total = total + jnp.where(lane == t, tags[t].astype(jnp.float32), 0.0)
-        dense[...] = total.astype(jnp.int32)
-        scalars = pltpu.make_async_copy(dense, window, sem)
-        scalars.start()
-        which = lax.broadcasted_iota(jnp.int32, (NWIN, 128), 0).astype(jnp.float32)
-        hits = jnp.zeros((NWIN, 128), jnp.float32)
-        for k in range(CAP):
-            hits = hits + jnp.where(which == total[k : k + 1, :], 1.0, 0.0)
-        counts = jnp.sum(hits, axis=1, keepdims=True)
-        inverse[...] = jnp.broadcast_to(1.0 / jnp.maximum(counts, 1.0), (NWIN, 128))
-        scalars.wait()
-
-    @pl.loop(0, per // 4)
-    def _(group):
-        for u in range(4):
-            t = group * 4 + u
-            for k, total in ((0, even), (1, odd)):
-                total[window[k, step * per + t]] += got[t, k * BR : (k + 1) * BR, :].astype(
-                    jnp.float32
-                )
-
-    @pl.when(step == pl.num_programs(0) - 1)
-    def _():
-        pad = jnp.zeros((128 - BR, 128), jnp.float32)
-        for p in range(NWIN // 2):
+    tiles = got.shape[0]
+    per = tiles // CHUNKS
+    fetch = pltpu.make_async_copy(got.at[:, pl.ds(CAP * BR, 8)], tags, tag_sem)
+    fetch.start()
+    chunks = [
+        pltpu.make_async_copy(
+            got.at[pl.ds(i * per, per), pl.ds(0, CAP * BR)],
+            held.at[pl.ds(i * per, per)],
+            chunk_sem.at[i],
+        )
+        for i in range(CHUNKS)
+    ]
+    for chunk in chunks:
+        chunk.start()
+    even[...] = jnp.zeros_like(even)
+    odd[...] = jnp.zeros_like(odd)
+    fetch.wait()
+    lane = lax.broadcasted_iota(jnp.int32, (8, 128), 1)
+    total = jnp.zeros((8, 128), jnp.float32)
+    for t in range(tiles):
+        total = total + jnp.where(lane == t, tags[t].astype(jnp.float32), 0.0)
+    dense[...] = total.astype(jnp.int32)
+    scalars = pltpu.make_async_copy(dense, window, dense_sem)
+    scalars.start()
+    which = lax.broadcasted_iota(jnp.int32, (NWIN, 128), 0).astype(jnp.float32)
+    hits = jnp.zeros((NWIN, 128), jnp.float32)
+    for k in range(CAP):
+        hits = hits + jnp.where(which == total[k : k + 1, :], 1.0, 0.0)
+    counts = jnp.sum(hits, axis=1, keepdims=True)
+    inverse[...] = jnp.broadcast_to(1.0 / jnp.maximum(counts, 1.0), (NWIN, 128))
+    scalars.wait()
+
+    for i in range(CHUNKS):
+        chunks[i].wait()
+
+        @pl.loop(0, per // 4)
+        def _(group):
+            for u in range(4):
+                t = i * per + group * 4 + u
+                for k, sums in ((0, even), (1, odd)):
+                    sums[window[k, t]] += held[t, k * BR : (k + 1) * BR, :].astype(jnp.float32)
+
+    pad = jnp.zeros((128 - BR, 128), jnp.float32)
+    outs = []
+    pairs = NWIN // 2 // QUARTERS
+    for q in range(QUARTERS):
+        for p in range(q * pairs, (q + 1) * pairs):
             pair = []
             for w in (2 * p, 2 * p + 1):
                 mean = (even[w] + odd[w]) * inverse[w : w + 1, :]
@@ -195,27 +222,35 @@
                 gridded[b, p * 16 : (p + 1) * 16, :] = jnp.concatenate(
                     [pair[0][rows], pair[1][rows]], axis=0
                 ).astype(jnp.bfloat16)
+        wins = pl.ds(q * 2 * pairs, 2 * pairs)
+        rows = pl.ds(q * 16 * pairs, 16 * pairs)
+        outs.append(pltpu.make_async_copy(turned.at[wins], turned_out.at[wins], out_sem.at[q, 0]))
+        outs.append(
+            pltpu.make_async_copy(gridded.at[:, rows], gridded_out.at[:, rows], out_sem.at[q, 1])
+        )
+        outs[-2].start()
+        outs[-1].start()
+    for copy in outs:
+        copy.wait()
 
 
 def gather_windows(got):
-    tiles, rows, _ = got.shape
-    per = 32
+    tiles = got.shape[0]
+    hbm = pl.BlockSpec(memory_space=pltpu.HBM)
+    grid_shape = (BANDS, NWIN * WIN, 128)
+    turned_shape = (NWIN, 128, 128)
     return pl.pallas_call(
         gather_kernel,
-        grid=(tiles // per,),
-        in_specs=[
-            pl.BlockSpec((per, rows, 128), lambda i: (i, 0, 0)),
-            pl.BlockSpec(memory_space=pl.ANY),
-        ],
-        out_specs=[
-            pl.BlockSpec((BANDS, NWIN * WIN, 128), lambda i: (0, 0, 0)),
-            pl.BlockSpec((NWIN, 128, 128), lambda i: (0, 0, 0)),
-        ],
+        in_specs=[hbm],
+        out_specs=[hbm, hbm],
         out_shape=[
-            jax.ShapeDtypeStruct((BANDS, NWIN * WIN, 128), jnp.bfloat16),
-            jax.ShapeDtypeStruct((NWIN, 128, 128), jnp.bfloat16),
+            jax.ShapeDtypeStruct(grid_shape, jnp.bfloat16),
+            jax.ShapeDtypeStruct(turned_shape, jnp.bfloat16),
         ],
         scratch_shapes=[
+            pltpu.VMEM((tiles, CAP * BR, 128), jnp.bfloat16),
+            pltpu.VMEM(grid_shape, jnp.bfloat16),
+            pltpu.VMEM(turned_shape, jnp.bfloat16),
             pltpu.VMEM((NWIN + 1, BR, 128), jnp.float32),
             pltpu.VMEM((NWIN + 1, BR, 128), jnp.float32),
             pltpu.VMEM((tiles, 8, 128), jnp.bfloat16),
@@ -224,10 +259,12 @@
             pltpu.VMEM((NWIN, 128), jnp.float32),
             pltpu.SemaphoreType.DMA,
             pltpu.SemaphoreType.DMA,
+            pltpu.SemaphoreType.DMA((CHUNKS,)),
+            pltpu.SemaphoreType.DMA((QUARTERS, 2)),
         ],
         compiler_params=pltpu.CompilerParams(vmem_limit_bytes=BIG_VMEM),
         name="gather_windows",
-    )(got, got)
+    )(got)
 
 
 HALO_WIN = HALO // WIN

time: 149 us -> 147 us (0.987)
  Pallas kernels: 49.1 us -> 46.8 us
    pallas_call x1, Pallas kernels: 7.74 us -> 6.06 us  [gather_windows(): pl.pallas_call(gather_kernel, in_specs=[hbm], out_specs=[hbm, hbm], out_s...]
where the time goes in v7:
time: 147 us; the launch traced here: 146 us
  waiting for transfers between devices  80.5 us (55%)
  Pallas kernels  46.8 us (32%)
  starting transfers between devices  11.9 us (8%)
  local copies, waits for them, and re-layouts  4.66 us (3%)
    all_to_all x1, waiting for transfers between devices, body(): lax.all_to_all(sent, ('tx', 'ty'), split_axis=0, concat_axis=0, tiled=True)  80.5 us
    pallas_call x1, Pallas kernels, encode(): pl.pallas_call(encoder_kernel, in_specs=[pl.BlockSpec(memory_space=pltpu....  25.8 us
    all_to_all x1, starting transfers between devices, body(): lax.all_to_all(sent, ('tx', 'ty'), split_axis=0, concat_axis=0, tiled=True)  11.9 us
    pallas_call x1, Pallas kernels, rim(): pl.pallas_call(rim_kernel, in_specs=[pl.BlockSpec(memory_space=pl.ANY)],...  9.34 us
    pallas_call x1, Pallas kernels, gather_windows(): pl.pallas_call(gather_kernel, in_specs=[hbm], out_specs=[hbm, hbm], out_s...  6.06 us
    pallas_call x1, Pallas kernels, resample(): pl.pallas_call(resample_kernel, grid=(held // per,), in_specs=[pl.BlockSp...  5.6 us
  transfers between devices with their start and end apart: 1, of which 1 were waited for; matrix products, arithmetic and copies ran while one was open for 4% of the time, Pallas kernels for 0%

profile of v7, /device:TPU:1, one launch (start us, length us, event | category | flops | bytes accessed | tf_op | source)
XLA Modules:
  0.0 146.2 jit_solution(11943772072230705136)
XLA Ops:
  0.6 0.0 copy-start
  0.6 5.6 %resample.1 = bf16[128,216,128]{2,1,0:T(8,128)(2,1)} custom-call(s32[64]{0:T(128)} %dest.1, s32[64]{0:T(128)} %window.1, s32[64]{0:T(128)} %bank_index.1, bf16[64,13,16,128]{3,2,1,0:T(8,128)(2,1)} %raw.1, bf16[8,16,64]{2,1,0:T(8,128)(2,1)} %bitcast.44, bf16[8,128,128]{2,1,0:T(8,128)(2,1)} %bank.1), custom_call_target="tpu_custom_call" | custom-call | tf_op jit(solution)/shard_map/resample/pallas_call | solution.py:117
  6.3 0.0 copy-start.2
  6.3 0.0 copy-start.3
  6.3 11.9 %all-to-all-start = ((bf16[128,216,128]{2,1,0:T(8,128)(2,1)}), bf16[128,216,128]{2,1,0:T(8,128)(2,1)}, u32[]{:S(2)}, u32[]{:S(2)}) async-start(bf16[128,216,128]{2,1,0:T(8,128)(2,1)} %resample.1), calls=%async_computation | async-start | bytes 14155776 | tf_op jit(solution)/shard_map/all_to_all | solution.py:736
  18.2 0.0 copy-start.1
  18.2 0.0 copy-done
  18.2 0.0 copy-done.2
  18.2 0.2 fusion.2
  18.5 0.0 copy-done.3
  18.5 0.6 convolution_bitcast_fusion
  19.1 0.9 copy.18
  20.0 0.5 reshape.31
  20.5 0.0 copy-done.1
  20.5 0.1 pad_bitcast_fusion.1
  20.7 0.1 pad_maximum_fusion
  20.7 0.8 copy.19
  21.6 1.4 reshape.34.hbm_two
  23.0 0.8 pad.12
  23.8 0.6 add_convert_fusion.edges
  24.4 80.5 %all-to-all-done.got = bf16[128,216,128]{2,1,0:T(8,128)(2,1)} async-done(((bf16[128,216,128]{2,1,0:T(8,128)(2,1)}), bf16[128,216,128]{2,1,0:T(8,128)(2,1)}, u32[]{:S(2)}, u32[]{:S(2)}) %all-to-all-start) | async-done | bytes 7077920 | tf_op jit(solution)/shard_map/all_to_all | solution.py:736
  104.9 6.1 %gather_windows.1 = (bf16[13,256,128]{2,1,0:T(8,128)(2,1)}, bf16[32,128,128]{2,1,0:T(8,128)(2,1)}) custom-call(bf16[128,216,128]{2,1,0:T(8,128)(2,1)} %all-to-all-done.got), custom_call_target="tpu_custom_call" | custom-call | tf_op jit(solution)/shard_map/gather_windows/pallas_call | solution.py:242
  110.9 9.3 %rim.1 = (bf16[4,160,128]{2,1,0:T(8,128)(2,1)}, bf16[32,32,128]{2,1,0:T(8,128)(2,1)}) custom-call(bf16[32,128,128]{2,1,0:T(8,128)(2,1)} %get-tuple-element.7.tile), custom_call_target="tpu_custom_call" | custom-call | tf_op jit(solution)/shard_map/rim/pallas_call | solution.py:385
  120.3 25.8 %encoder.1 = bf16[512,512]{1,0:T(8,128)(2,1)} custom-call(s32[4]{0:T(128)} %add_convert_fusion.edges, bf16[32,128,128]{2,1,0:T(8,128)(2,1)} %get-tuple-element.7.tile, bf16[4,160,128]{2,1,0:T(8,128)(2,1)} %get-tuple-element.8.rim_rows, bf16[32,32,128]{2,1,0:T(8,128)(2,1)} %get-tuple-element.9.rim_cols, bf16[512,512]{1,0:T(8,128)(2,1)} %bitcast.38, ...), custom_call_target="tpu_custom_call" | custom-call | tf_op jit(solution)/shard_map/encoder/pallas_call | solution.py:661
Async XLA Ops:
  0.6 17.6 %copy-start = (bf16[3,3,13,64]{3,2,1,0:T(8,128)(2,1)S(1)}, bf16[3,3,13,64]{3,2,1,0:T(8,128)(2,1)}, u32[]{:S(2)}) copy-start(bf16[3,3,13,64]{3,2,1,0:T(8,128)(2,1)} %param.21) | copy-start | bytes 44932
  6.3 12.0 %copy-start.2 = (bf16[8,4,3,1,1]{2,1,4,3,0:T(4,128)(2,1)S(1)}, bf16[8,4,3,1,1]{2,1,4,3,0:T(4,128)(2,1)}, u32[]{:S(2)}) copy-start(bf16[8,4,3,1,1]{2,1,4,3,0:T(4,128)(2,1)} %constant.34) | copy-start | bytes 580
  6.3 12.2 %copy-start.3 = (bf16[4,2,3,1,1,1]{2,0,1,5,4,3:T(4,128)(2,1)S(1)}, bf16[4,2,3,1,1,1]{2,0,1,5,4,3:T(4,128)(2,1)}, u32[]{:S(2)}) copy-start(bf16[4,2,3,1,1,1]{2,0,1,5,4,3:T(4,128)(2,1)} %constant.35) | copy-start | bytes 148
  6.3 98.6 %all-to-all-start = ((bf16[128,216,128]{2,1,0:T(8,128)(2,1)}), bf16[128,216,128]{2,1,0:T(8,128)(2,1)}, u32[]{:S(2)}, u32[]{:S(2)}) async-start(bf16[128,216,128]{2,1,0:T(8,128)(2,1)} %resample.1), calls=%async_computation | async-start | bytes 14155776 | tf_op jit(solution)/shard_map/all_to_all | solution.py:736
  18.2 2.3 %copy-start.1 = (bf16[3,3,128,128]{3,2,1,0:T(8,128)(2,1)S(1)}, bf16[3,3,128,128]{3,2,1,0:T(8,128)(2,1)}, u32[]{:S(2)}) copy-start(bf16[3,3,128,128]{3,2,1,0:T(8,128)(2,1)} %param.23) | copy-start | bytes 884740

commit v8 on v7

--- a/solution.py
+++ b/solution.py
@@ -128,8 +128,8 @@
         out_specs=pl.BlockSpec(memory_space=pltpu.HBM),
         out_shape=jax.ShapeDtypeStruct((tiles, CAP * BR + 8, 128), jnp.bfloat16),
         scratch_shapes=[
-            pltpu.VMEM((held * WIN, 128), jnp.float32),
-            pltpu.VMEM((held * WIN, 128), jnp.float32),
+            pltpu.VMEM(((held + 1) * WIN, 128), jnp.float32),
+            pltpu.VMEM(((held + 1) * WIN, 128), jnp.float32),
             pltpu.VMEM((held, BR, 128), jnp.bfloat16),
             pltpu.VMEM((tiles, 8, 128), jnp.float32),
             pltpu.VMEM((tiles, 8, 128), jnp.bfloat16),
@@ -381,11 +381,10 @@
 
 def rim(turned):
     moves = len(MOVES)
-    vmem = pl.BlockSpec(memory_space=pltpu.VMEM)
     return pl.pallas_call(
         rim_kernel,
         in_specs=[pl.BlockSpec(memory_space=pl.ANY)],
-        out_specs=[vmem, vmem],
+        out_specs=[pl.BlockSpec(memory_space=pl.ANY)] * 2,
         out_shape=[
             jax.ShapeDtypeStruct((2 * HALO_WIN, WIDE_COL, 128), jnp.bfloat16),
             jax.ShapeDtypeStruct((NWIN, 2 * HALO, 128), jnp.bfloat16),
@@ -425,8 +424,8 @@
     tile,
     rim_rows,
     rim_cols,
-    weight_one,
-    reduce_two,
+    hbm_one,
+    hbm_reduce_two,
     hbm_two,
     hbm_reduce_three,
     hbm_three,
@@ -444,6 +443,8 @@
     carry_three,
     spread_three,
     taps_four,
+    weight_one,
+    reduce_two,
     weight_two,
     reduce_three,
     weight_three,
@@ -475,13 +476,12 @@
                 for j, (src, dst) in enumerate(moves)
             ]
         )
-    for copies in parts:
-        for copy in copies:
-            copy.start()
     fetches = [
         pltpu.make_async_copy(source, target, sems.at[i])
         for i, (source, target) in enumerate(
             (
+                (hbm_one, weight_one),
+                (hbm_reduce_two, reduce_two),
                 (hbm_two, weight_two),
                 (hbm_reduce_three, reduce_three),
                 (hbm_three, weight_three),
@@ -490,8 +490,8 @@
             )
         )
     ]
-    for fetch in fetches:
-        fetch.start()
+    for copy in parts[0] + fetches[:2] + sum(parts[1:], []) + fetches[2:]:
+        copy.start()
 
     def dot(a, b):
         return jnp.dot(a, b, preferred_element_type=jnp.float32)
@@ -519,7 +519,7 @@
     col_two = jnp.where(at < PAIRS, 2 * at, 2 * (at - PAIRS) + 1) - 7
     limits_two = bounds(128, 64)
     carry_two[...] = jnp.zeros_like(carry_two)
-    for copy in parts[0]:
+    for copy in parts[0] + fetches[:2]:
         copy.wait()
 
     @pl.loop(0, STEPS_ONE)
@@ -568,8 +568,8 @@
             before = lines[1]
         carry_two[...] = before
 
-    fetches[0].wait()
-    fetches[1].wait()
+    fetches[2].wait()
+    fetches[3].wait()
     col_three = lax.broadcasted_iota(jnp.int32, (PAIRS, 256), 0) - 3
     limits_three = bounds(64, 32)
     carry_three[...] = jnp.zeros_like(carry_three)
@@ -601,8 +601,8 @@
             before = lines[1]
         carry_three[...] = before
 
-    fetches[2].wait()
-    fetches[3].wait()
+    fetches[4].wait()
+    fetches[5].wait()
     col_four = lax.broadcasted_iota(jnp.int32, (WIDE_FOUR, 512), 0) - 1
     limits_four = bounds(32, 16)
     size_four = ROWS_FOUR * PIX
@@ -644,7 +644,7 @@
                 [value[:16], following(value, 1)[:16], following(value, 2)[:16]], axis=1
             ).astype(jnp.bfloat16)
 
-    fetches[4].wait()
+    fetches[6].wait()
     for half in range(2):
         lanes = slice(half * 256, (half + 1) * 256)
         hidden = sum(
@@ -656,15 +656,11 @@
 
 def encode(tile, rims, edges, one, two, reduce_three, three, reduce_four, four, reduce_two):
     hbm = pl.BlockSpec(memory_space=pltpu.HBM)
-    vmem = pl.BlockSpec(memory_space=pltpu.VMEM)
-    big = (two, reduce_three, three, reduce_four, four)
+    big = (one, reduce_two, two, reduce_three, three, reduce_four, four)
     return pl.pallas_call(
         encoder_kernel,
-        in_specs=[pl.BlockSpec(memory_space=pltpu.SMEM)]
-        + [hbm] * 3
-        + [vmem] * 2
-        + [hbm] * len(big),
-        out_specs=vmem,
+        in_specs=[pl.BlockSpec(memory_space=pltpu.SMEM)] + [hbm] * (3 + len(big)),
+        out_specs=pl.BlockSpec(memory_space=pltpu.VMEM),
         out_shape=jax.ShapeDtypeStruct((512, 512), jnp.bfloat16),
         scratch_shapes=[
             pltpu.VMEM((WIDE_WIN, WIDE_COL, 128), jnp.bfloat16),
@@ -683,7 +679,7 @@
         + [pltpu.SemaphoreType.DMA((len(big),)), pltpu.SemaphoreType.DMA((STEPS_ONE, 4))],
         compiler_params=pltpu.CompilerParams(vmem_limit_bytes=BIG_VMEM),
         name="encoder",
-    )(edges, tile, *rims, one, reduce_two, *big)
+    )(edges, tile, *rims, *big)
 
 
 def patch_weights(kernel):

time: 147 us -> 146 us (level)
  no operation moved by 1% of the time
where the time goes in v8:
time: 146 us
  waiting for transfers between devices  80.5 us (55%)
  Pallas kernels  46.1 us (32%)
  starting transfers between devices  11.9 us (8%)
  local copies, waits for them, and re-layouts  4.66 us (3%)
    all_to_all x1, waiting for transfers between devices, body(): lax.all_to_all(sent, ('tx', 'ty'), split_axis=0, concat_axis=0, tiled=True)  80.5 us
    pallas_call x1, Pallas kernels, encode(): pl.pallas_call(encoder_kernel, in_specs=[pl.BlockSpec(memory_space=pltpu....  25.7 us
    all_to_all x1, starting transfers between devices, body(): lax.all_to_all(sent, ('tx', 'ty'), split_axis=0, concat_axis=0, tiled=True)  11.9 us
    pallas_call x1, Pallas kernels, rim(): pl.pallas_call(rim_kernel, in_specs=[pl.BlockSpec(memory_space=pl.ANY)],...  8.76 us
    pallas_call x1, Pallas kernels, gather_windows(): pl.pallas_call(gather_kernel, in_specs=[hbm], out_specs=[hbm, hbm], out_s...  6.06 us
    pallas_call x1, Pallas kernels, resample(): pl.pallas_call(resample_kernel, grid=(held // per,), in_specs=[pl.BlockSp...  5.63 us
  transfers between devices with their start and end apart: 1, of which 1 were waited for; matrix products, arithmetic and copies ran while one was open for 4% of the time, Pallas kernels for 0%

profile of v8, /device:TPU:1, one launch (start us, length us, event | category | flops | bytes accessed | tf_op | source)
XLA Modules:
  0.0 145.5 jit_solution(17742289575250076602)
XLA Ops:
  0.6 0.0 copy-start
  0.6 5.6 %resample.1 = bf16[128,216,128]{2,1,0:T(8,128)(2,1)} custom-call(s32[64]{0:T(128)} %dest.1, s32[64]{0:T(128)} %window.1, s32[64]{0:T(128)} %bank_index.1, bf16[64,13,16,128]{3,2,1,0:T(8,128)(2,1)} %raw.1, bf16[8,16,64]{2,1,0:T(8,128)(2,1)} %bitcast.44, bf16[8,128,128]{2,1,0:T(8,128)(2,1)} %bank.1), custom_call_target="tpu_custom_call" | custom-call | tf_op jit(solution)/shard_map/resample/pallas_call | solution.py:117
  6.3 0.0 copy-start.2
  6.3 0.0 copy-start.3
  6.3 11.9 %all-to-all-start = ((bf16[128,216,128]{2,1,0:T(8,128)(2,1)}), bf16[128,216,128]{2,1,0:T(8,128)(2,1)}, u32[]{:S(2)}, u32[]{:S(2)}) async-start(bf16[128,216,128]{2,1,0:T(8,128)(2,1)} %resample.1), calls=%async_computation | async-start | bytes 14155776 | tf_op jit(solution)/shard_map/all_to_all | solution.py:732
  18.2 0.0 copy-start.1
  18.2 0.0 copy-done
  18.2 0.0 copy-done.2
  18.2 0.2 fusion.2
  18.5 0.0 copy-done.3
  18.5 0.6 convolution_bitcast_fusion
  19.1 0.9 copy.18
  20.0 0.5 reshape.31
  20.5 0.0 copy-done.1
  20.5 0.1 pad_bitcast_fusion.1
  20.7 0.1 pad_maximum_fusion
  20.7 0.8 copy.19
  21.6 1.4 reshape.34.hbm_two
  23.0 0.8 pad.12
  23.8 0.6 add_convert_fusion.edges
  24.4 80.5 %all-to-all-done.got = bf16[128,216,128]{2,1,0:T(8,128)(2,1)} async-done(((bf16[128,216,128]{2,1,0:T(8,128)(2,1)}), bf16[128,216,128]{2,1,0:T(8,128)(2,1)}, u32[]{:S(2)}, u32[]{:S(2)}) %all-to-all-start) | async-done | bytes 7077920 | tf_op jit(solution)/shard_map/all_to_all | solution.py:732
  104.9 6.1 %gather_windows.1 = (bf16[13,256,128]{2,1,0:T(8,128)(2,1)}, bf16[32,128,128]{2,1,0:T(8,128)(2,1)}) custom-call(bf16[128,216,128]{2,1,0:T(8,128)(2,1)} %all-to-all-done.got), custom_call_target="tpu_custom_call" | custom-call | tf_op jit(solution)/shard_map/gather_windows/pallas_call | solution.py:242
  110.9 8.8 %rim.1 = (bf16[4,160,128]{2,1,0:T(8,128)(2,1)}, bf16[32,32,128]{2,1,0:T(8,128)(2,1)}) custom-call(bf16[32,128,128]{2,1,0:T(8,128)(2,1)} %get-tuple-element.7.tile), custom_call_target="tpu_custom_call" | custom-call | tf_op jit(solution)/shard_map/rim/pallas_call | solution.py:384
  119.7 25.7 %encoder.1 = bf16[512,512]{1,0:T(8,128)(2,1)} custom-call(s32[4]{0:T(128)} %add_convert_fusion.edges, bf16[32,128,128]{2,1,0:T(8,128)(2,1)} %get-tuple-element.7.tile, bf16[4,160,128]{2,1,0:T(8,128)(2,1)} %get-tuple-element.8.rim_rows, bf16[32,32,128]{2,1,0:T(8,128)(2,1)} %get-tuple-element.9.rim_cols, bf16[512,512]{1,0:T(8,128)(2,1)} %bitcast.38, ...), custom_call_target="tpu_custom_call" | custom-call | tf_op jit(solution)/shard_map/encoder/pallas_call | solution.py:660
Async XLA Ops:
  0.6 17.6 %copy-start = (bf16[3,3,13,64]{3,2,1,0:T(8,128)(2,1)S(1)}, bf16[3,3,13,64]{3,2,1,0:T(8,128)(2,1)}, u32[]{:S(2)}) copy-start(bf16[3,3,13,64]{3,2,1,0:T(8,128)(2,1)} %param.21) | copy-start | bytes 44932
  6.3 11.9 %copy-start.2 = (bf16[8,4,3,1,1]{2,1,4,3,0:T(4,128)(2,1)S(1)}, bf16[8,4,3,1,1]{2,1,4,3,0:T(4,128)(2,1)}, u32[]{:S(2)}) copy-start(bf16[8,4,3,1,1]{2,1,4,3,0:T(4,128)(2,1)} %constant.34) | copy-start | bytes 580
  6.3 12.2 %copy-start.3 = (bf16[4,2,3,1,1,1]{2,0,1,5,4,3:T(4,128)(2,1)S(1)}, bf16[4,2,3,1,1,1]{2,0,1,5,4,3:T(4,128)(2,1)}, u32[]{:S(2)}) copy-start(bf16[4,2,3,1,1,1]{2,0,1,5,4,3:T(4,128)(2,1)} %constant.35) | copy-start | bytes 148
  6.3 98.5 %all-to-all-start = ((bf16[128,216,128]{2,1,0:T(8,128)(2,1)}), bf16[128,216,128]{2,1,0:T(8,128)(2,1)}, u32[]{:S(2)}, u32[]{:S(2)}) async-start(bf16[128,216,128]{2,1,0:T(8,128)(2,1)} %resample.1), calls=%async_computation | async-start | bytes 14155776 | tf_op jit(solution)/shard_map/all_to_all | solution.py:732
  18.2 2.3 %copy-start.1 = (bf16[3,3,128,128]{3,2,1,0:T(8,128)(2,1)S(1)}, bf16[3,3,128,128]{3,2,1,0:T(8,128)(2,1)}, u32[]{:S(2)}) copy-start(bf16[3,3,128,128]{3,2,1,0:T(8,128)(2,1)} %param.23) | copy-start | bytes 884740

commit v9 on v8

--- a/solution.py
+++ b/solution.py
@@ -84,21 +84,24 @@
         == lax.broadcasted_iota(jnp.int32, (BANDS, WIN, lanes), 0)
     )
     rowed = []
-    for k in range(per):
+    for k in range(0, per, 2):
+        pair = []
+        for m in (k, k + 1):
+            rows = pl.ds(pl.multiple_of((step * per + m) * WIN, WIN), WIN)
+            row = jnp.concatenate([tiled_low[rows, :], tiled_high[rows, : lanes - 128]], axis=1)
+            pair.append(jnp.where(own_band, row[None], 0.0))
+        left = jnp.concatenate(pair, axis=0).reshape(2 * BR, lanes).astype(jnp.bfloat16)
+        right = jnp.concatenate([raw[m].reshape(lanes, 128) for m in (k, k + 1)], axis=1)
+        both = jnp.dot(left, right, preferred_element_type=jnp.float32)
+        rowed.append(
+            jnp.concatenate([both[:BR, :128], both[BR:, 128:]], axis=0).astype(jnp.bfloat16)
+        )
+    for k in range(0, per, 2):
         n = step * per + k
-        rows = pl.ds(pl.multiple_of(n * WIN, WIN), WIN)
-        row = jnp.concatenate([tiled_low[rows, :], tiled_high[rows, : lanes - 128]], axis=1)
-        block = jnp.where(own_band, row[None], 0.0).reshape(BR, lanes).astype(jnp.bfloat16)
-        rowed.append(
-            jnp.dot(
-                block, raw[k].reshape(lanes, 128), preferred_element_type=jnp.float32
-            ).astype(jnp.bfloat16)
-        )
-    for k in range(per):
-        n = step * per + k
-        res[n] = jnp.dot(
-            rowed[k], bank[bank_index[n]], preferred_element_type=jnp.float32
-        ).astype(jnp.bfloat16)
+        right = jnp.concatenate([bank[bank_index[n]], bank[bank_index[n + 1]]], axis=1)
+        both = jnp.dot(rowed[k // 2], right, preferred_element_type=jnp.float32)
+        res[n] = both[:BR, :128].astype(jnp.bfloat16)
+        res[n + 1] = both[BR:, 128:].astype(jnp.bfloat16)
     for k in range(per):
         n = step * per + k
         pltpu.make_async_copy(
@@ -407,8 +410,8 @@
 
 
 FAR = 1 << 20
-HALVES = 18
-STEPS_ONE = 4
+HALVES = 24
+STEPS_ONE = 3
 PAIRS = 40
 PIX = 2 * PAIRS
 ROWS_TWO = STEPS_ONE * HALVES

time: 146 us -> 146 us (level)
  no operation moved by 1% of the time
where the time goes in v9:
time: 146 us; the launch traced here: 145 us
  waiting for transfers between devices  80.5 us (55%)
  Pallas kernels  45.7 us (31%)
  starting transfers between devices  11.9 us (8%)
  local copies, waits for them, and re-layouts  4.66 us (3%)
    all_to_all x1, waiting for transfers between devices, body(): lax.all_to_all(sent, ('tx', 'ty'), split_axis=0, concat_axis=0, tiled=True)  80.5 us
    pallas_call x1, Pallas kernels, encode(): pl.pallas_call(encoder_kernel, in_specs=[pl.BlockSpec(memory_space=pltpu....  25.3 us
    all_to_all x1, starting transfers between devices, body(): lax.all_to_all(sent, ('tx', 'ty'), split_axis=0, concat_axis=0, tiled=True)  11.9 us
    pallas_call x1, Pallas kernels, rim(): pl.pallas_call(rim_kernel, in_specs=[pl.BlockSpec(memory_space=pl.ANY)],...  8.75 us
    pallas_call x1, Pallas kernels, gather_windows(): pl.pallas_call(gather_kernel, in_specs=[hbm], out_specs=[hbm, hbm], out_s...  6.06 us
    pallas_call x1, Pallas kernels, resample(): pl.pallas_call(resample_kernel, grid=(held // per,), in_specs=[pl.BlockSp...  5.51 us
  transfers between devices with their start and end apart: 1, of which 1 were waited for; matrix products, arithmetic and copies ran while one was open for 4% of the time, Pallas kernels for 0%

profile of v9, /device:TPU:1, one launch (start us, length us, event | category | flops | bytes accessed | tf_op | source)
XLA Modules:
  0.0 145.1 jit_solution(1123092056243452625)
XLA Ops:
  0.6 0.0 copy-start
  0.6 5.5 %resample.1 = bf16[128,216,128]{2,1,0:T(8,128)(2,1)} custom-call(s32[64]{0:T(128)} %dest.1, s32[64]{0:T(128)} %window.1, s32[64]{0:T(128)} %bank_index.1, bf16[64,13,16,128]{3,2,1,0:T(8,128)(2,1)} %raw.1, bf16[8,16,64]{2,1,0:T(8,128)(2,1)} %bitcast.44, bf16[8,128,128]{2,1,0:T(8,128)(2,1)} %bank.1), custom_call_target="tpu_custom_call" | custom-call | tf_op jit(solution)/shard_map/resample/pallas_call | solution.py:120
  6.2 0.0 copy-start.2
  6.2 0.0 copy-start.3
  6.2 11.9 %all-to-all-start = ((bf16[128,216,128]{2,1,0:T(8,128)(2,1)}), bf16[128,216,128]{2,1,0:T(8,128)(2,1)}, u32[]{:S(2)}, u32[]{:S(2)}) async-start(bf16[128,216,128]{2,1,0:T(8,128)(2,1)} %resample.1), calls=%async_computation | async-start | bytes 14155776 | tf_op jit(solution)/shard_map/all_to_all | solution.py:735
  18.1 0.0 copy-start.1
  18.1 0.0 copy-done
  18.1 0.0 copy-done.2
  18.1 0.2 fusion.2
  18.3 0.0 copy-done.3
  18.3 0.6 convolution_bitcast_fusion
  18.9 0.9 copy.18
  19.9 0.5 reshape.31
  20.4 0.0 copy-done.1
  20.4 0.1 pad_bitcast_fusion.1
  20.5 0.1 pad_maximum_fusion
  20.6 0.8 copy.19
  21.4 1.4 reshape.34.hbm_two
  22.9 0.8 pad.12
  23.7 0.6 add_convert_fusion.edges
  24.3 80.5 %all-to-all-done.got = bf16[128,216,128]{2,1,0:T(8,128)(2,1)} async-done(((bf16[128,216,128]{2,1,0:T(8,128)(2,1)}), bf16[128,216,128]{2,1,0:T(8,128)(2,1)}, u32[]{:S(2)}, u32[]{:S(2)}) %all-to-all-start) | async-done | bytes 7077920 | tf_op jit(solution)/shard_map/all_to_all | solution.py:735
  104.7 6.1 %gather_windows.1 = (bf16[13,256,128]{2,1,0:T(8,128)(2,1)}, bf16[32,128,128]{2,1,0:T(8,128)(2,1)}) custom-call(bf16[128,216,128]{2,1,0:T(8,128)(2,1)} %all-to-all-done.got), custom_call_target="tpu_custom_call" | custom-call | tf_op jit(solution)/shard_map/gather_windows/pallas_call | solution.py:245
  110.8 8.8 %rim.1 = (bf16[4,160,128]{2,1,0:T(8,128)(2,1)}, bf16[32,32,128]{2,1,0:T(8,128)(2,1)}) custom-call(bf16[32,128,128]{2,1,0:T(8,128)(2,1)} %get-tuple-element.7.tile), custom_call_target="tpu_custom_call" | custom-call | tf_op jit(solution)/shard_map/rim/pallas_call | solution.py:387
  119.6 25.3 %encoder.1 = bf16[512,512]{1,0:T(8,128)(2,1)} custom-call(s32[4]{0:T(128)} %add_convert_fusion.edges, bf16[32,128,128]{2,1,0:T(8,128)(2,1)} %get-tuple-element.7.tile, bf16[4,160,128]{2,1,0:T(8,128)(2,1)} %get-tuple-element.8.rim_rows, bf16[32,32,128]{2,1,0:T(8,128)(2,1)} %get-tuple-element.9.rim_cols, bf16[512,512]{1,0:T(8,128)(2,1)} %bitcast.38, ...), custom_call_target="tpu_custom_call" | custom-call | tf_op jit(solution)/shard_map/encoder/pallas_call | solution.py:663
Async XLA Ops:
  0.6 17.5 %copy-start = (bf16[3,3,13,64]{3,2,1,0:T(8,128)(2,1)S(1)}, bf16[3,3,13,64]{3,2,1,0:T(8,128)(2,1)}, u32[]{:S(2)}) copy-start(bf16[3,3,13,64]{3,2,1,0:T(8,128)(2,1)} %param.21) | copy-start | bytes 44932
  6.2 11.9 %copy-start.2 = (bf16[8,4,3,1,1]{2,1,4,3,0:T(4,128)(2,1)S(1)}, bf16[8,4,3,1,1]{2,1,4,3,0:T(4,128)(2,1)}, u32[]{:S(2)}) copy-start(bf16[8,4,3,1,1]{2,1,4,3,0:T(4,128)(2,1)} %constant.34) | copy-start | bytes 580
  6.2 12.2 %copy-start.3 = (bf16[4,2,3,1,1,1]{2,0,1,5,4,3:T(4,128)(2,1)S(1)}, bf16[4,2,3,1,1,1]{2,0,1,5,4,3:T(4,128)(2,1)}, u32[]{:S(2)}) copy-start(bf16[4,2,3,1,1,1]{2,0,1,5,4,3:T(4,128)(2,1)} %constant.35) | copy-start | bytes 148
  6.2 98.5 %all-to-all-start = ((bf16[128,216,128]{2,1,0:T(8,128)(2,1)}), bf16[128,216,128]{2,1,0:T(8,128)(2,1)}, u32[]{:S(2)}, u32[]{:S(2)}) async-start(bf16[128,216,128]{2,1,0:T(8,128)(2,1)} %resample.1), calls=%async_computation | async-start | bytes 14155776 | tf_op jit(solution)/shard_map/all_to_all | solution.py:735
  18.1 2.3 %copy-start.1 = (bf16[3,3,128,128]{3,2,1,0:T(8,128)(2,1)S(1)}, bf16[3,3,128,128]{3,2,1,0:T(8,128)(2,1)}, u32[]{:S(2)}) copy-start(bf16[3,3,128,128]{3,2,1,0:T(8,128)(2,1)} %param.23) | copy-start | bytes 884740

commit v10 on v9

--- a/solution.py
+++ b/solution.py
@@ -147,7 +147,7 @@
 
 
 CHUNKS = 4
-QUARTERS = 4
+QUARTERS = 2
 
 
 def gather_kernel(

time: 146 us -> 146 us (level)
  no operation moved by 1% of the time
where the time goes in v10:
time: 146 us; the launch traced here: 145 us
  waiting for transfers between devices  80.5 us (55%)
  Pallas kernels  45.7 us (31%)
  starting transfers between devices  11.9 us (8%)
  local copies, waits for them, and re-layouts  4.66 us (3%)
    all_to_all x1, waiting for transfers between devices, body(): lax.all_to_all(sent, ('tx', 'ty'), split_axis=0, concat_axis=0, tiled=True)  80.5 us
    pallas_call x1, Pallas kernels, encode(): pl.pallas_call(encoder_kernel, in_specs=[pl.BlockSpec(memory_space=pltpu....  25.3 us
    all_to_all x1, starting transfers between devices, body(): lax.all_to_all(sent, ('tx', 'ty'), split_axis=0, concat_axis=0, tiled=True)  11.9 us
    pallas_call x1, Pallas kernels, rim(): pl.pallas_call(rim_kernel, in_specs=[pl.BlockSpec(memory_space=pl.ANY)],...  8.76 us
    pallas_call x1, Pallas kernels, gather_windows(): pl.pallas_call(gather_kernel, in_specs=[hbm], out_specs=[hbm, hbm], out_s...  6.12 us
    pallas_call x1, Pallas kernels, resample(): pl.pallas_call(resample_kernel, grid=(held // per,), in_specs=[pl.BlockSp...  5.48 us
  transfers between devices with their start and end apart: 1, of which 1 were waited for; matrix products, arithmetic and copies ran while one was open for 4% of the time, Pallas kernels for 0%

profile of v10, /device:TPU:1, one launch (start us, length us, event | category | flops | bytes accessed | tf_op | source)
XLA Modules:
  0.0 145.1 jit_solution(9447013432012814870)
XLA Ops:
  0.6 0.0 copy-start
  0.6 5.5 %resample.1 = bf16[128,216,128]{2,1,0:T(8,128)(2,1)} custom-call(s32[64]{0:T(128)} %dest.1, s32[64]{0:T(128)} %window.1, s32[64]{0:T(128)} %bank_index.1, bf16[64,13,16,128]{3,2,1,0:T(8,128)(2,1)} %raw.1, bf16[8,16,64]{2,1,0:T(8,128)(2,1)} %bitcast.44, bf16[8,128,128]{2,1,0:T(8,128)(2,1)} %bank.1), custom_call_target="tpu_custom_call" | custom-call | tf_op jit(solution)/shard_map/resample/pallas_call | solution.py:120
  6.1 0.0 copy-start.2
  6.1 0.0 copy-start.3
  6.2 11.9 %all-to-all-start = ((bf16[128,216,128]{2,1,0:T(8,128)(2,1)}), bf16[128,216,128]{2,1,0:T(8,128)(2,1)}, u32[]{:S(2)}, u32[]{:S(2)}) async-start(bf16[128,216,128]{2,1,0:T(8,128)(2,1)} %resample.1), calls=%async_computation | async-start | bytes 14155776 | tf_op jit(solution)/shard_map/all_to_all | solution.py:735
  18.1 0.0 copy-start.1
  18.1 0.0 copy-done
  18.1 0.0 copy-done.2
  18.1 0.2 fusion.2
  18.3 0.0 copy-done.3
  18.4 0.6 convolution_bitcast_fusion
  18.9 0.9 copy.18
  19.9 0.5 reshape.31
  20.4 0.0 copy-done.1
  20.4 0.1 pad_bitcast_fusion.1
  20.6 0.1 pad_maximum_fusion
  20.6 0.8 copy.19
  21.5 1.4 reshape.34.hbm_two
  22.9 0.8 pad.12
  23.7 0.6 add_convert_fusion.edges
  24.3 80.5 %all-to-all-done.got = bf16[128,216,128]{2,1,0:T(8,128)(2,1)} async-done(((bf16[128,216,128]{2,1,0:T(8,128)(2,1)}), bf16[128,216,128]{2,1,0:T(8,128)(2,1)}, u32[]{:S(2)}, u32[]{:S(2)}) %all-to-all-start) | async-done | bytes 7077920 | tf_op jit(solution)/shard_map/all_to_all | solution.py:735
  104.8 6.1 %gather_windows.1 = (bf16[13,256,128]{2,1,0:T(8,128)(2,1)}, bf16[32,128,128]{2,1,0:T(8,128)(2,1)}) custom-call(bf16[128,216,128]{2,1,0:T(8,128)(2,1)} %all-to-all-done.got), custom_call_target="tpu_custom_call" | custom-call | tf_op jit(solution)/shard_map/gather_windows/pallas_call | solution.py:245
  110.9 8.8 %rim.1 = (bf16[4,160,128]{2,1,0:T(8,128)(2,1)}, bf16[32,32,128]{2,1,0:T(8,128)(2,1)}) custom-call(bf16[32,128,128]{2,1,0:T(8,128)(2,1)} %get-tuple-element.7.tile), custom_call_target="tpu_custom_call" | custom-call | tf_op jit(solution)/shard_map/rim/pallas_call | solution.py:387
  119.6 25.3 %encoder.1 = bf16[512,512]{1,0:T(8,128)(2,1)} custom-call(s32[4]{0:T(128)} %add_convert_fusion.edges, bf16[32,128,128]{2,1,0:T(8,128)(2,1)} %get-tuple-element.7.tile, bf16[4,160,128]{2,1,0:T(8,128)(2,1)} %get-tuple-element.8.rim_rows, bf16[32,32,128]{2,1,0:T(8,128)(2,1)} %get-tuple-element.9.rim_cols, bf16[512,512]{1,0:T(8,128)(2,1)} %bitcast.38, ...), custom_call_target="tpu_custom_call" | custom-call | tf_op jit(solution)/shard_map/encoder/pallas_call | solution.py:663
Async XLA Ops:
  0.6 17.5 %copy-start = (bf16[3,3,13,64]{3,2,1,0:T(8,128)(2,1)S(1)}, bf16[3,3,13,64]{3,2,1,0:T(8,128)(2,1)}, u32[]{:S(2)}) copy-start(bf16[3,3,13,64]{3,2,1,0:T(8,128)(2,1)} %param.21) | copy-start | bytes 44932
  6.1 12.0 %copy-start.2 = (bf16[8,4,3,1,1]{2,1,4,3,0:T(4,128)(2,1)S(1)}, bf16[8,4,3,1,1]{2,1,4,3,0:T(4,128)(2,1)}, u32[]{:S(2)}) copy-start(bf16[8,4,3,1,1]{2,1,4,3,0:T(4,128)(2,1)} %constant.34) | copy-start | bytes 580
  6.1 12.2 %copy-start.3 = (bf16[4,2,3,1,1,1]{2,0,1,5,4,3:T(4,128)(2,1)S(1)}, bf16[4,2,3,1,1,1]{2,0,1,5,4,3:T(4,128)(2,1)}, u32[]{:S(2)}) copy-start(bf16[4,2,3,1,1,1]{2,0,1,5,4,3:T(4,128)(2,1)} %constant.35) | copy-start | bytes 148
  6.2 98.6 %all-to-all-start = ((bf16[128,216,128]{2,1,0:T(8,128)(2,1)}), bf16[128,216,128]{2,1,0:T(8,128)(2,1)}, u32[]{:S(2)}, u32[]{:S(2)}) async-start(bf16[128,216,128]{2,1,0:T(8,128)(2,1)} %resample.1), calls=%async_computation | async-start | bytes 14155776 | tf_op jit(solution)/shard_map/all_to_all | solution.py:735
  18.1 2.3 %copy-start.1 = (bf16[3,3,128,128]{3,2,1,0:T(8,128)(2,1)S(1)}, bf16[3,3,128,128]{3,2,1,0:T(8,128)(2,1)}, u32[]{:S(2)}) copy-start(bf16[3,3,128,128]{3,2,1,0:T(8,128)(2,1)} %param.23) | copy-start | bytes 884740
